TPU v7x, 256 devices: a whole 4x4x8 slice. The times are simulated.
256 devices in a mesh: dp: 32 (over x, z_hi, core), tensor: 8 (over y, z_lo).
Axes of the slice: x: 4, y: 4, z: 8 (z_hi: 4, z_lo: 2; z = z_hi * 2 + z_lo), core: 2. Of those that a mesh axis runs over, the one named last changes fastest.
Arguments:
- tokens: bfloat16 [32, 256, 8192], P('dp', None, 'tensor'), may hold values from -6 to 6
- segment_ids: int32 [32, 256], P('dp'), may hold values from 0 to 3, never falling along the last dimension, each value on 1 to 128 neighbouring positions
- queries: bfloat16 [32, 256, 8192], P('dp', None, 'tensor'), may hold values from -7 to 7
- teacher_keys: bfloat16 [32, 256, 1024], P('dp', None, 'tensor'), may hold values from -7 to 7
- teacher_values: bfloat16 [32, 256, 1024], P('dp', None, 'tensor'), may hold values from -6 to 6
- down_weight: bfloat16 [8192, 512], P('tensor'), may hold values from -0.0625 to 0.0625
- rope_weight: bfloat16 [64, 8192], P(None, 'tensor'), may hold values from -1 to 1
- key_up: bfloat16 [512, 4096], P(None, 'tensor'), may hold values from -0.25 to 0.25
- value_up: bfloat16 [512, 8192], P(None, 'tensor'), may hold values from -0.25 to 0.25
Outputs:
- grad_down: float32 [8192, 512], P('tensor')
- grad_rope: float32 [64, 8192], P(None, 'tensor')
- grad_key_up: float32 [512, 4096], P(None, 'tensor')
- grad_value_up: float32 [512, 8192], P(None, 'tensor')
Inputs may be any that keep to these rules, and one draw needn't show every extreme that they name: `segment_ids`: along a sequence the document number never falls; each of the 4 documents holds 1 to 128 tokens, and one holds exactly 128.
All inputs are finite; a program needn't handle non-finite values.
Results may differ from a plain program's by a relative error of at most 0.011.
Values sent between devices are 32-bit elements; how exact they have to be, the bound alone decides.
No kernel may reach another device: no remote copies, remote signals or barrier semaphores. Data moves between devices by JAX's collectives and lax.ppermute only.
A program may use at most 64 MiB of HBM per device.

v0:
```python
import math

import jax
import jax.numpy as jnp
from jax import lax
from jax.sharding import PartitionSpec as P

HEAD = 128
ROPE = 64


theta_base = 500000.0
norm_eps = 1e-06


def angle_tables(positions, width):
    half_width = width // 2
    exponent = jnp.arange(half_width, dtype=jnp.float32) * (2.0 / width)
    frequency = jnp.exp(-exponent * jnp.log(jnp.float32(theta_base)))
    angles = positions.astype(jnp.float32)[:, None] * frequency[None, :]
    return (jnp.cos(angles), jnp.sin(angles))


def rotate_last(tensor, cosine, sine_tab):
    half_width = tensor.shape[-1] // 2
    first_half = tensor[..., :half_width]
    second_half = tensor[..., half_width:]
    return jnp.concatenate(
        [
            first_half * cosine - second_half * sine_tab,
            second_half * cosine + first_half * sine_tab,
        ],
        axis=-1,
    )


def rotate_rows(matrix, cosine, sine_tab):
    half_width = matrix.shape[0] // 2
    first_half = matrix[:half_width]
    second_half = matrix[half_width:]
    return jnp.concatenate(
        [
            first_half * cosine - second_half * sine_tab,
            second_half * cosine + first_half * sine_tab,
        ],
        axis=0,
    )


def unrotate_rows(matrix, cosine, sine_tab):
    half_width = matrix.shape[0] // 2
    first_half = matrix[:half_width]
    second_half = matrix[half_width:]
    return jnp.concatenate(
        [
            first_half * cosine + second_half * sine_tab,
            second_half * cosine - first_half * sine_tab,
        ],
        axis=0,
    )


def doc_positions(segments_row):
    position_index = jnp.arange(segments_row.shape[0], dtype=jnp.int32)
    is_start = jnp.concatenate(
        [jnp.ones((1,), dtype=jnp.bool_), segments_row[1:] != segments_row[:-1]]
    )
    doc_start = lax.cummax(jnp.where(is_start, position_index, 0), axis=0)
    return position_index - doc_start


def block_mask(seg_block, segments_row, row_start):
    rows_index = row_start + jnp.arange(seg_block.shape[0], dtype=jnp.int32)
    cols_index = jnp.arange(segments_row.shape[0], dtype=jnp.int32)
    return (
        (seg_block[:, None] == segments_row[None, :]) & (cols_index[None, :] <= rows_index[:, None])
    ).astype(jnp.int32)


def masked_softmax(scores, doc_mask):
    masked = jnp.where(doc_mask > 0, scores, -jnp.inf)
    peak = jnp.max(masked, axis=-1, keepdims=True)
    weights = jnp.exp(masked - peak)
    return weights / jnp.sum(weights, axis=-1, keepdims=True)


def local(
    tokens,
    segment_ids,
    queries,
    teacher_keys,
    teacher_values,
    down_weight,
    rope_weight,
    key_up,
    value_up,
):
    f32 = jnp.float32
    bf16 = jnp.bfloat16
    token_rows = tokens[0]
    segments_row = segment_ids[0]
    seq_len = token_rows.shape[0]
    heads_local = queries.shape[2] // HEAD
    kv_local = teacher_keys.shape[2] // HEAD
    group_size = heads_local // kv_local
    nope_width = HEAD - ROPE
    score_scale = 1.0 / math.sqrt(HEAD)
    contract_cols = (((1,), (1,)), ((), ()))
    contract_rows = (((0,), (0,)), ((), ()))
    positions = doc_positions(segments_row)
    cos_full, sin_full = angle_tables(positions, HEAD)
    cos_rope, sin_rope = angle_tables(positions, ROPE)
    latent_part = jnp.dot(token_rows, down_weight, preferred_element_type=f32)
    rope_part = lax.dot_general(rope_weight, token_rows, contract_cols, preferred_element_type=f32)
    latent_raw, rope_sum = lax.psum((latent_part, rope_part), "tensor")
    inv_rms = lax.rsqrt(jnp.mean(latent_raw * latent_raw, axis=-1, keepdims=True) + norm_eps)
    normed = latent_raw * inv_rms
    latent = normed.astype(bf16)
    rope_key = rotate_rows(rope_sum, cos_rope.T, sin_rope.T).astype(bf16)
    head_queries = queries[0].reshape(seq_len, heads_local, HEAD).transpose(1, 0, 2)
    teacher_q = (
        rotate_last(head_queries.astype(f32), cos_full, sin_full)
        .astype(bf16)
        .reshape(kv_local, group_size, seq_len, HEAD)
    )
    teacher_k = rotate_last(
        teacher_keys[0].reshape(seq_len, kv_local, HEAD).transpose(1, 0, 2).astype(f32),
        cos_full,
        sin_full,
    ).astype(bf16)
    teacher_v = teacher_values[0].reshape(seq_len, kv_local, HEAD).transpose(1, 0, 2)
    key_nope = (
        jnp.dot(latent, key_up, preferred_element_type=f32)
        .astype(bf16)
        .reshape(seq_len, heads_local, nope_width)
        .transpose(1, 0, 2)
    )
    head_values = (
        jnp.dot(latent, value_up, preferred_element_type=f32)
        .astype(bf16)
        .reshape(seq_len, heads_local, HEAD)
        .transpose(1, 0, 2)
    )
    rotated_q = rotate_last(head_queries[..., :ROPE].astype(f32), cos_rope, sin_rope).astype(bf16)
    student_q = jnp.concatenate([head_queries[..., ROPE:], rotated_q], axis=-1)
    student_k = jnp.concatenate(
        [key_nope, jnp.broadcast_to(rope_key.T[None], (heads_local, seq_len, ROPE))], axis=-1
    )
    block_rows = min(seq_len, 512)
    block_count = seq_len // block_rows

    def attend_block(carry, block_index):
        value_acc, key_acc = carry
        row_start = block_index * block_rows
        doc_mask = block_mask(segments_row, segments_row, row_start)
        teacher_scores = (
            jnp.einsum("kgqd,kpd->kgqp", teacher_q, teacher_k, preferred_element_type=f32)
            * score_scale
        )
        teacher_weights = masked_softmax(teacher_scores, doc_mask).astype(bf16)
        teacher_out = jnp.einsum(
            "kgqp,kpd->kgqd", teacher_weights, teacher_v, preferred_element_type=f32
        ).reshape(heads_local, block_rows, HEAD)
        student_scores = (
            jnp.einsum("hqd,hpd->hqp", student_q, student_k, preferred_element_type=f32)
            * score_scale
        )
        student_weights = masked_softmax(student_scores, doc_mask)
        student_low = student_weights.astype(bf16)
        student_out = jnp.einsum(
            "hqp,hpd->hqd", student_low, head_values, preferred_element_type=f32
        )
        out_grad = (student_out - teacher_out).astype(bf16)
        weight_grad = jnp.einsum("hqd,hpd->hqp", out_grad, head_values, preferred_element_type=f32)
        row_dot = jnp.sum(student_weights * weight_grad, axis=-1, keepdims=True)
        score_grad = (student_weights * (weight_grad - row_dot) * score_scale).astype(bf16)
        value_acc = value_acc + jnp.einsum(
            "hqp,hqd->hpd", student_low, out_grad, preferred_element_type=f32
        )
        key_acc = key_acc + jnp.einsum(
            "hqp,hqd->hpd", score_grad, student_q, preferred_element_type=f32
        )
        return ((value_acc, key_acc), None)

    zeros_acc = jnp.zeros((heads_local, seq_len, HEAD), f32)
    accums, unused = lax.scan(
        attend_block, (zeros_acc, zeros_acc), jnp.arange(block_count, dtype=jnp.int32)
    )
    value_acc, key_acc = accums
    value_flat = value_acc.astype(bf16).transpose(1, 0, 2).reshape(seq_len, heads_local * HEAD)
    nope_grad = (
        key_acc[..., :nope_width]
        .astype(bf16)
        .transpose(1, 0, 2)
        .reshape(seq_len, heads_local * nope_width)
    )
    rope_grad_part = jnp.sum(key_acc[..., nope_width:], axis=0).T
    norm_grad_part = lax.dot_general(
        nope_grad, key_up, contract_cols, preferred_element_type=f32
    ) + lax.dot_general(value_flat, value_up, contract_cols, preferred_element_type=f32)
    grad_kup = lax.dot_general(latent, nope_grad, contract_rows, preferred_element_type=f32)
    grad_vup = lax.dot_general(latent, value_flat, contract_rows, preferred_element_type=f32)
    norm_grad, rope_grad_sum = lax.psum((norm_grad_part, rope_grad_part), "tensor")
    latent_grad = (
        (norm_grad - normed * jnp.mean(norm_grad * normed, axis=-1, keepdims=True)) * inv_rms
    ).astype(bf16)
    rope_grad = unrotate_rows(rope_grad_sum, cos_rope.T, sin_rope.T).astype(bf16)
    grad_down = lax.dot_general(token_rows, latent_grad, contract_rows, preferred_element_type=f32)
    grad_rope = jnp.dot(rope_grad, token_rows, preferred_element_type=f32)
    grad_down, grad_rope, grad_kup, grad_vup = lax.psum(
        (grad_down, grad_rope, grad_kup, grad_vup), "dp"
    )
    return (grad_down, grad_rope, grad_kup, grad_vup)


def solution(mesh):
    in_specs = (
        P("dp", None, "tensor"),
        P("dp", None),
        P("dp", None, "tensor"),
        P("dp", None, "tensor"),
        P("dp", None, "tensor"),
        P("tensor", None),
        P(None, "tensor"),
        P(None, "tensor"),
        P(None, "tensor"),
    )
    out_specs = (P("tensor", None), P(None, "tensor"), P(None, "tensor"), P(None, "tensor"))
    return jax.shard_map(local, mesh=mesh, in_specs=in_specs, out_specs=out_specs, check_vma=False)
```

profile of v0, /device:TPU:32, one launch (start us, length us, event | category | flops | bytes accessed | tf_op | source)
XLA Modules:
  0.0 527.6 jit_solution(17835268048351347968)
XLA Ops:
  7.3 2.1 fusion.33
  9.4 2.6 fusion.35
  12.9 1.2 multiply_cosine_fusion.1
  14.1 1.2 fusion.62
  17.3 1.3 subtract_convert_fusion
  18.6 3.4 fusion.105
  22.0 1.5 subtract_convert_fusion.1
  23.5 69.9 %all-reduce.11.cloned.1.call-done = (f32[256,512]{1,0:T(8,128)}, f32[64,256]{1,0:T(8,128)}) async-done(((f32[256,512]{1,0:T(8,128)}, f32[64,256]{1,0:T(8,128)}), (f32[256,512]{1,0:T(8,128)}, f32[64,256]{1,0:T(8,128)})) %all-reduce.11.cloned.1.call-update) | async-done | bytes 589840 | tf_op jit(solution)/shard_map/psum | solution.py:115
  94.4 1.2 multiply_reduce_fusion.2
  99.0 4.0 fusion.102
  103.0 2.2 fusion.21
  106.9 1.3 convolution_convert_fusion.1
  108.6 4.9 fusion.7
  113.5 1.8 slice_reduce_fusion
  116.4 1.4 fusion.108
  117.8 1.3 convolution_add_fusion
  119.1 1.3 fusion.109
  120.5 1.8 fusion.110
  122.3 76.9 %all-reduce.9.cloned.1.call-done = (f32[256,512]{1,0:T(8,128)}, f32[64,256]{1,0:T(8,128)}) async-done(((f32[256,512]{1,0:T(8,128)}, f32[64,256]{1,0:T(8,128)}), (f32[256,512]{1,0:T(8,128)}, f32[64,256]{1,0:T(8,128)})) %all-reduce.9.cloned.1.call-update) | async-done | bytes 589840 | tf_op jit(solution)/shard_map/psum | solution.py:203
  200.2 1.2 multiply_reduce_fusion.1
  201.4 3.0 convolution_bitcast_fusion
  205.3 309.7 %all-reduce.7.cloned.1.call-done = (f32[1024,512]{0,1:T(8,128)}, f32[64,1024]{1,0:T(8,128)}, f32[512,512]{1,0:T(8,128)}, f32[512,1024]{1,0:T(8,128)}) async-done(((f32[1024,512]{0,1:T(8,128)}, f32[64,1024]{1,0:T(8,128)}, f32[512,512]{1,0:T(8,128)}, f32[512,1024]{1,0:T(8,128)}), (f32[1024,512]{0,1:T(8,128)}, f32[64,1024]{1,0:T(8,128)}, f32[512,512]{1,0:T(8,128)}, ...) | async-done | bytes 5505040 | tf_op jit(solution)/shard_map/psum | solution.py:210
  515.0 3.0 copy.35
  519.7 1.3 copy.61
  (76 shorter events, 14.0 us)
Async XLA Ops:
  7.2 90.4 %copy-start = (bf16[512,1024]{1,0:T(8,128)(2,1)S(1)}, bf16[512,1024]{1,0:T(8,128)(2,1)}, u32[]{:S(2)}) copy-start(bf16[512,1024]{1,0:T(8,128)(2,1)} %param.17) | copy-start | bytes 3145732
  7.2 4.9 copy-start.14
  7.2 5.7 %copy-start.13 = (bf16[1,256,128]{2,1,0:T(8,128)(2,1)S(1)}, bf16[1,256,128]{2,1,0:T(8,128)(2,1)}, u32[]{:S(2)}) copy-start(bf16[1,256,128]{2,1,0:T(8,128)(2,1)} %param.12) | copy-start | bytes 196612
  7.2 8.7 %copy-start.10 = (bf16[1,256,1024]{2,1,0:T(8,128)(2,1)S(1)}, bf16[1,256,1024]{2,1,0:T(8,128)(2,1)}, u32[]{:S(2)}) copy-start(bf16[1,256,1024]{2,1,0:T(8,128)(2,1)} %param.11) | copy-start | bytes 1572868
  7.2 86.2 %all-reduce.11.cloned.1.call-start = ((), (), s32[]{:S(2)}) async-start(), calls=%async_computation.2 | async-start | bytes 1179648 | tf_op jit(solution)/shard_map/psum | solution.py:115
  12.0 187.2 %all-reduce.9.cloned.1.call-start = ((), (), s32[]{:S(2)}) async-start(), calls=%async_computation.1 | async-start | bytes 1179648 | tf_op jit(solution)/shard_map/psum | solution.py:203
  16.4 0.9 copy-start.11
  16.7 82.3 %copy-start.9 = (bf16[8,256,64]{2,1,0:T(8,128)(2,1)}, bf16[8,256,64]{2,1,0:T(8,128)(2,1)S(1)}, u32[]{:S(2)}) copy-start(bf16[8,256,64]{2,1,0:T(8,128)(2,1)S(1)} %get-tuple-element.54) | copy-start | bytes 786436
  22.0 74.8 %copy-start.4 = (bf16[512,512]{1,0:T(8,128)(2,1)S(1)}, bf16[512,512]{1,0:T(8,128)(2,1)}, u32[]{:S(2)}) copy-start(bf16[512,512]{1,0:T(8,128)(2,1)} %param.16) | copy-start | bytes 1572868
  98.0 5.0 copy-start.6
  103.0 2.2 copy-start.15
  103.0 2.3 copy-start.17
  105.3 1.6 copy-start.16
  106.9 1.3 copy-start.7
  113.5 4.2 copy-start.5
  119.1 81.1 %copy-start.1 = (f32[256,512]{1,0:T(8,128)S(1)}, f32[256,512]{1,0:T(8,128)}, u32[]{:S(2)}) copy-start(f32[256,512]{1,0:T(8,128)} %get-tuple-element.48) | copy-start | bytes 1572868
  119.1 396.0 %all-reduce.7.cloned.1.call-start = ((), (), s32[]{:S(2)}) async-start(), calls=%async_computation | async-start | bytes 11010048 | tf_op jit(solution)/shard_map/psum | solution.py:210
  120.5 80.9 %copy-start.2 = (bf16[1,256,1024]{2,1,0:T(8,128)(2,1)S(1)}, bf16[1,256,1024]{2,1,0:T(8,128)(2,1)}, u32[]{:S(2)}) copy-start(bf16[1,256,1024]{2,1,0:T(8,128)(2,1)} %param.9) | copy-start | bytes 1572868
  515.0 3.0 copy-start.12
  515.0 3.7 copy-start.8
  518.0 1.7 copy-start.3
Sparse Core Ops, SparseCore 0:
  12.1 81.2 all-reduce.10
  119.2 79.9 all-reduce.8
  205.4 309.5 all-reduce.6
where the time goes:
time: 528 us
  waiting for transfers between devices  457 us (87%)
  matrix products  31.9 us (6%)
  between operations  14.1 us (3%)
  other arithmetic  14 us (3%)
  local copies, waits for them, and re-layouts  10.9 us (2%)
    psum x1, waiting for transfers between devices, local(): lax.psum((grad_down, grad_rope, grad_kup, grad_vup), 'dp')  310 us
    psum x1, waiting for transfers between devices, local(): lax.psum((norm_grad_part, rope_grad_part), 'tensor')  76.9 us
    psum x1, waiting for transfers between devices, local(): latent_raw, rope_sum = lax.psum((latent_part, rope_part), 'tensor')  69.9 us
  transfers between devices with their start and end apart: 3, of which 3 were waited for; matrix products, arithmetic and copies ran while one was open for 3% of the time, Pallas kernels for 0%

commit v1 on v0

v1 whole, which is shorter than its diff:
```python
import math

import jax
import jax.numpy as jnp
from jax import lax
from jax.experimental import pallas as pl
from jax.experimental.pallas import tpu as pltpu
from jax.sharding import PartitionSpec as P


HEAD = 128
ROPE = 64
SEQ = 256
LATENT = 512
THETA = 500000.0
EPS = 1e-06
AXES = ("dp", "tensor")
F32 = jnp.float32
BF16 = jnp.bfloat16

NT = (((1,), (1,)), ((), ()))
TN = (((0,), (0,)), ((), ()))
PACKED = 144


def dot(a, b):
    return jnp.dot(a, b, preferred_element_type=F32)


def dot_nt(a, b):
    return lax.dot_general(a, b, NT, preferred_element_type=F32)


def dot_tn(a, b):
    return lax.dot_general(a, b, TN, preferred_element_type=F32)


def call(body, outs, *args, scalars=0, scratch=(), flops=0):
    spec = pl.BlockSpec(memory_space=pltpu.VMEM)
    smem = pl.BlockSpec(memory_space=pltpu.SMEM)
    size = sum(a.size * a.dtype.itemsize for a in args)
    size += sum(math.prod(o.shape) * o.dtype.itemsize for o in outs)
    return pl.pallas_call(
        body,
        out_shape=outs,
        in_specs=[smem] * scalars + [spec] * (len(args) - scalars),
        out_specs=[spec] * len(outs),
        scratch_shapes=list(scratch),
        compiler_params=pltpu.CompilerParams(vmem_limit_bytes=20 << 20),
        cost_estimate=pl.CostEstimate(flops=flops, bytes_accessed=size, transcendentals=0),
    )(*args)


def shape(*dims, dtype=F32):
    return jax.ShapeDtypeStruct(dims, dtype)


def low_lanes(rows):
    return lax.broadcasted_iota(jnp.int32, (rows, 128), 1) < 64


def pack_rest(first, second):
    return jnp.where(low_lanes(16), first, pltpu.roll(second, 64, 1))


def swap(value):
    lane = lax.broadcasted_iota(jnp.int32, value.shape, 1)
    return jnp.where(lane < 32, pltpu.roll(value, 96, 1), pltpu.roll(value, 32, 1))


def pack(out, k, rows, wide, rest):
    for j in range(4):
        out[k, 32 * j : 32 * j + 32, :] = wide[rows : rows + 32, 128 * j : 128 * j + 128]
    out[k, 128:PACKED, :] = pack_rest(rest[rows : rows + 16], rest[rows + 16 : rows + 32])


def unpack_rest(value, out, rows):
    out[rows : rows + 16, :] = value
    out[rows + 16 : rows + 32, :] = pltpu.roll(value, 64, 1)


def unpack(packed, wide, rest):
    for k in range(8):
        for j in range(4):
            wide[32 * k : 32 * k + 32, 128 * j : 128 * j + 128] = packed[
                k, 32 * j : 32 * j + 32, :
            ].astype(wide.dtype)
        unpack_rest(packed[k, 128:PACKED, :], rest, 32 * k)


def entry_kernel(tokens, down, rope, out):
    wide = dot(tokens[...], down[...])
    rest = dot_nt(tokens[...], rope[...])
    rest = jnp.concatenate([rest, jnp.zeros_like(rest)], axis=1)
    for k in range(8):
        pack(out, k, 32 * k, wide, rest)


def norm_kernel(parts, out, normed_out, inv_out):
    total = jnp.sum(parts[...], axis=0)
    square = jnp.zeros((32, 1), F32)
    for j in range(4):
        tile = total[32 * j : 32 * j + 32]
        square = square + jnp.sum(tile * tile, axis=1, keepdims=True)
    inv = lax.rsqrt(square * (1.0 / LATENT) + EPS)
    inv = jnp.broadcast_to(inv, (32, 128))
    inv_out[...] = inv
    normed = total[:128] * jnp.concatenate([inv] * 4, axis=0)
    normed_out[...] = normed
    for k in range(8):
        out[k, :128, :] = normed
        out[k, 128:, :] = total[128:]


def norm_grad_kernel(at, parts, normed, inv, table, out):
    total = jnp.sum(parts[...], axis=0)
    rows = pl.ds(pl.multiple_of(at[3] * 32, 32), 32)
    rest = jnp.concatenate([total[128:], pltpu.roll(total[128:], 64, 1)], axis=0)
    rest = rest * table[rows, 256:384] - swap(rest) * table[rows, 384:512]
    rest = pack_rest(rest[:16], rest[16:])
    grad = total[:128]
    product = grad * normed[...]
    mean = jnp.zeros((32, 1), F32)
    for j in range(4):
        mean = mean + jnp.sum(product[32 * j : 32 * j + 32], axis=1, keepdims=True)
    mean = jnp.broadcast_to(mean * (1.0 / LATENT), (32, 128))
    four = lambda v: jnp.concatenate([v] * 4, axis=0)
    grad = (grad - normed[...] * four(mean)) * four(inv[...])
    for k in range(8):
        out[k, :128, :] = grad
        out[k, 128:, :] = rest


def seen(seg_col, seg_row):
    i = lax.broadcasted_iota(jnp.int32, (SEQ, SEQ), 0)
    j = lax.broadcasted_iota(jnp.int32, (SEQ, SEQ), 1)
    return (seg_col == seg_row) & (j <= i)


def softmax(scores, mask):
    scores = jnp.where(mask, scores * (1.0 / math.sqrt(HEAD)), -3e38)
    weights = jnp.exp(scores - jnp.max(scores, axis=1, keepdims=True))
    return weights * (1.0 / jnp.sum(weights, axis=1, keepdims=True))


def lanes(h):
    return pl.ds(pl.multiple_of(h * 128, 128), 128)


def teacher_kernel(
    at, queries, keys, values, table, seg_col, seg_row, tokens, out, tokens_keep, tokens_send
):
    mask = seen(seg_col[...], seg_row[...])
    cos, sin = table[:, :128], table[:, 128:256]
    turn = lambda v: (v * cos + pltpu.roll(v, 64, 1) * sin).astype(BF16)
    key = turn(keys[...].astype(F32))
    value = values[...]

    def pair(p, carry):
        for h in (2 * p, 2 * p + 1):
            query = turn(queries[:, lanes(h)].astype(F32))
            weights = softmax(dot_nt(query, key), mask).astype(BF16)
            out[:, lanes(h)] = dot(weights, value)
        return carry

    lax.fori_loop(0, 4, pair, 0)
    half = lambda c: tokens[:, pl.ds(pl.multiple_of(c * 512, 512), 512)].T
    tokens_keep[...] = half(at[0])
    tokens_send[...] = half(1 - at[0]).astype(F32)


def student_kernel(
    at, packed, queries, key_up, value_up, teacher, table, seg_col, seg_row,
    grads_keep, grads_send, norm_out, latent, rest, nope, head_values, rest_sum, grads_out,
):
    unpack(packed, latent, rest)
    cos, sin = table[:, 256:384], table[:, 384:512]
    low = low_lanes(SEQ)
    turn = lambda v: v * cos + swap(v) * sin
    rope_key = turn(rest[...])
    nope[...] = dot(latent[...], key_up[...])
    head_values[...] = dot(latent[...], value_up[...]).astype(BF16)
    mask = seen(seg_col[...], seg_row[...])
    scale = 1.0 / math.sqrt(HEAD)
    rest_sum[...] = jnp.zeros_like(rest_sum)

    def head(h, key_part):
        query = turn(queries[:, lanes(h)].astype(F32)).astype(BF16)
        key = jnp.where(low, rope_key, key_part).astype(BF16)
        weights = softmax(dot_nt(query, key), mask)
        weights_low = weights.astype(BF16)
        value = head_values[:, lanes(h)]
        out_grad = (dot(weights_low, value) - teacher[:, lanes(h)]).astype(BF16)
        weight_grad = dot_nt(out_grad, value)
        row = jnp.sum(weights * weight_grad, axis=1, keepdims=True)
        score_grad = (weights * (weight_grad - row) * scale).astype(BF16)
        grads_out[:, lanes(4 + h)] = dot_tn(weights_low, out_grad).astype(BF16)
        return dot_tn(score_grad, query)

    def pair(p, carry):
        both = nope[:, lanes(p)]
        first = head(2 * p, pltpu.roll(both, 64, 1))
        second = head(2 * p + 1, both)
        rest_sum[...] += first + second
        grads_out[:, lanes(p)] = jnp.where(low, pltpu.roll(first, 64, 1), second).astype(BF16)
        return carry

    lax.fori_loop(0, 4, pair, 0)
    wide = dot_nt(grads_out[:, :512], key_up[...]) + dot_nt(grads_out[:, 512:], value_up[...])
    rest_all = rest_sum[...]
    for ref, c in ((grads_keep, at[0]), (grads_send, 1 - at[0])):
        keys = pl.ds(pl.multiple_of(c * 256, 256), 256)
        values = pl.ds(pl.multiple_of(512 + c * 512, 512), 512)
        ref[:, :256] = grads_out[:, keys].astype(ref.dtype)
        ref[:, 256:] = grads_out[:, values].astype(ref.dtype)
    for k in range(8):
        pack(norm_out, k, 32 * k, wide, rest_all)


def up_kernel(at, packed, other_packed, grads, other_grads, *outs):
    *outs, latent, rest = outs
    unpack(packed, latent, rest)
    whole = dot_tn(latent[...], grads[...])
    unpack(other_packed, latent, rest)
    whole = whole + dot_tn(latent[...], other_grads[...].astype(BF16))
    for quarter in range(4):
        for step in range(4):
            @pl.when((at[1] + step) % 4 == quarter)
            def _(quarter=quarter, step=step):
                outs[step][...] = whole[128 * quarter : 128 * quarter + 128]


def split_kernel(at, own, first, second, third, *outs):
    for step in range(4):
        rows = pl.ds(pl.multiple_of((at[2] + step) % 4 * 32, 32), 32)
        outs[step][...] = (own[rows, :] + first[rows, :]) + (second[rows, :] + third[rows, :])


def entry_grad_kernel(packed, other_packed, tokens, other_tokens, out, grads, rest):
    unpack(packed, grads, rest)
    grads[:, 512:] = jnp.where(low_lanes(SEQ), rest[...], 0.0).astype(BF16)
    whole = dot(tokens[...], grads[...])
    unpack(other_packed, grads, rest)
    grads[:, 512:] = jnp.where(low_lanes(SEQ), rest[...], 0.0).astype(BF16)
    whole = whole + dot(other_tokens[...].astype(BF16), grads[...])
    for k in range(16):
        pack(out, k, 32 * k, whole[:, :512], whole[:, 512:])


def up_out_kernel(at, *refs):
    *parts, key_out, value_out = refs
    for c in range(2):
        column = jnp.where(c == 0, at[0], 1 - at[0])
        keys = pl.ds(pl.multiple_of(column * 256, 256), 256)
        values = pl.ds(pl.multiple_of(column * 512, 512), 512)
        for step in range(4):
            ref = parts[4 * c + step]
            for depth in range(4):
                block = (at[1] - step + 4) % 4 * 4 + (at[2] - depth + 4) % 4
                rows = pl.ds(pl.multiple_of(block * 32, 32), 32)
                key_out[rows, keys] = ref[depth, :, :256]
                value_out[rows, values] = ref[depth, :, 256:]


def entry_out_kernel(at, own, other, down_out, rope_out, rest):
    c = at[0]
    for half, ref in ((c, own), (1 - c, other)):
        def group(g, carry, half=half, ref=ref):
            first = half * 4 + g
            for b in range(4):
                rows = pl.ds(pl.multiple_of(first * 128 + 32 * b, 32), 32)
                for j in range(4):
                    down_out[rows, 128 * j : 128 * j + 128] = ref[
                        4 * g + b, 32 * j : 32 * j + 32, :
                    ]
                unpack_rest(ref[4 * g + b, 128:PACKED, :], rest, 32 * b)
            rope_out[:, lanes(first)] = rest[...].T[:64]
            return carry

        lax.fori_loop(0, 4, group, 0)


def sum_kernel(parts, out):
    out[...] = (parts[0] + parts[1]) + (parts[2] + parts[3])


def sum_spread_kernel(parts, out):
    total = (parts[0] + parts[1]) + (parts[2] + parts[3])
    for k in range(4):
        out[k] = total


def spread_kernel(value, out):
    for k in range(4):
        out[k] = value[...]


def permute(value, move):
    pairs = []
    for i in range(256):
        d, t = divmod(i, 8)
        at = dict(x=d // 8, h=(d // 2) % 4, c=d % 2, y=t // 2, l=t % 2)
        to = {**at, **move(at)}
        j = (to["x"] * 8 + to["h"] * 2 + to["c"]) * 8 + to["y"] * 2 + to["l"]
        pairs.append((i, j))
    return lax.ppermute(value, AXES, pairs)


def other_core(value):
    return permute(value, lambda at: {"c": 1 - at["c"]})


def around(value, axis):
    values = value if isinstance(value, list) else [value] * 3
    moves = [lambda at, k=k: {axis: (at[axis] + k) % 4} for k in (1, 2, 3)]
    return [permute(v, move) for v, move in zip(values, moves)]


X_GROUPS = [[8 * x + r for x in range(4)] for r in range(8)]
H_GROUPS = [[8 * x + 2 * h + c for h in range(4)] for x in range(4) for c in range(2)]


def exchange(parts, groups=None):
    axis = "tensor" if groups is None else "dp"
    return lax.all_to_all(parts, axis, 0, 0, axis_index_groups=groups, tiled=True)


def tables(segments):
    index = jnp.arange(SEQ, dtype=jnp.int32)
    start = jnp.sum((segments[None, :] < segments[:, None]).astype(jnp.int32), axis=1)
    position = (index - start).astype(F32)

    def angles(width):
        exponent = jnp.arange(width // 2, dtype=F32) * (2.0 / width)
        return position[:, None] * jnp.exp(-exponent * jnp.log(F32(THETA)))[None, :]

    full, part = angles(HEAD), angles(ROPE)
    cos, sin = jnp.cos(full), jnp.sin(full)
    cos_part, sin_part = jnp.cos(part), jnp.sin(part)
    one, zero = jnp.ones((SEQ, 64), F32), jnp.zeros((SEQ, 64), F32)
    return jnp.concatenate(
        [cos, cos, -sin, sin, cos_part, cos_part, one, -sin_part, sin_part, zero], axis=1
    )


def local(tokens, segment_ids, queries, keys, values, down, rope, key_up, value_up):
    tokens, segments, queries = tokens[0], segment_ids[0], queries[0]
    d = lax.axis_index("dp")
    at = jnp.stack([d % 2, d // 8, d // 2 % 4, lax.axis_index("tensor")])
    seg_col, seg_row = segments[:, None], segments[None, :]
    chunks = shape(8, PACKED, 128)
    unpacked = [pltpu.VMEM((SEQ, LATENT), BF16), pltpu.VMEM((SEQ, 128), F32)]

    (part,) = call(entry_kernel, [chunks], tokens, down, rope, flops=2 * 256 * 1024 * 576)
    parts = exchange(part)
    table = tables(segments)
    teacher, tokens_keep, tokens_send = call(
        teacher_kernel,
        [shape(SEQ, 1024), shape(512, SEQ, dtype=BF16), shape(512, SEQ)],
        at, queries, keys[0], values[0], table, seg_col, seg_row, tokens,
        scalars=1, flops=4 * 8 * 256 * 256 * 128,
    )
    tokens_other = other_core(tokens_send)
    parts, teacher = lax.optimization_barrier((parts, teacher))
    replicas, normed, inv = call(norm_kernel, [chunks, shape(128, 128), shape(32, 128)], parts)
    packed = exchange(replicas)
    packed_other = other_core(packed)
    grads_keep, grads_send, part = call(
        student_kernel,
        [shape(SEQ, 768, dtype=BF16), shape(SEQ, 768), chunks],
        at, packed, queries, key_up, value_up, teacher, table, seg_col, seg_row,
        scalars=1,
        scratch=unpacked + [
            pltpu.VMEM((SEQ, 512), F32),
            pltpu.VMEM((SEQ, 1024), BF16),
            pltpu.VMEM((SEQ, 128), F32),
            pltpu.VMEM((SEQ, 1536), BF16),
        ],
        flops=10 * 8 * 256 * 256 * 128,
    )
    grads_other = other_core(grads_send)
    parts = exchange(part)
    quarters = call(
        up_kernel, [shape(128, 768)] * 4, at, packed, packed_other, grads_keep, grads_other,
        scalars=1, scratch=unpacked, flops=2 * 512 * 512 * 768,
    )
    received = around(list(quarters[1:]), "x")
    (replicas,) = call(norm_grad_kernel, [chunks], at, parts, normed, inv, table, scalars=1)
    packed = exchange(replicas)
    packed_other = other_core(packed)
    (entry,) = call(
        entry_grad_kernel, [shape(16, PACKED, 128)],
        packed, packed_other, tokens_keep, tokens_other,
        scratch=[pltpu.VMEM((SEQ, 640), BF16), pltpu.VMEM((SEQ, 128), F32)],
        flops=2 * 512 * 512 * 640,
    )
    entry = exchange(entry.reshape(4, 4, PACKED, 128), X_GROUPS)
    quarters = call(split_kernel, [shape(32, 768)] * 4, at, quarters[0], *received, scalars=1)
    received = around(list(quarters[1:]), "h")
    (entry,) = call(sum_kernel, [shape(4, PACKED, 128)], entry)
    entry = exchange(entry, H_GROUPS)
    up = (quarters[0] + received[0]) + (received[1] + received[2])
    up_all = jnp.stack([up] + around(up, "h"))
    (entry,) = call(sum_spread_kernel, [shape(4, PACKED, 128)], entry)
    entry = exchange(entry, H_GROUPS)
    received = [up_all] + around(up_all, "x")
    (entry,) = call(spread_kernel, [shape(4, 4, PACKED, 128)], entry)
    entry = exchange(entry, X_GROUPS).reshape(16, PACKED, 128)
    others = [other_core(v) for v in received]
    grad_key, grad_value = call(
        up_out_kernel, [shape(512, 512), shape(512, 1024)], at, *received, *others, scalars=1,
    )
    entry_other = other_core(entry)
    grad_down, grad_rope = call(
        entry_out_kernel, [shape(1024, 512), shape(64, 1024)], at, entry, entry_other,
        scalars=1, scratch=[pltpu.VMEM((128, 128), F32)],
    )
    return grad_down, grad_rope, grad_key, grad_value


def solution(mesh):
    token = P("dp", None, "tensor")
    rows, columns = P("tensor", None), P(None, "tensor")
    in_specs = (token, P("dp", None), token, token, token, rows, columns, columns, columns)
    out_specs = (rows, columns, columns, columns)
    return jax.shard_map(local, mesh=mesh, in_specs=in_specs, out_specs=out_specs, check_vma=False)
```

time: 528 us -> 216 us (0.41)
  the two profiles are of different devices: /device:TPU:32 before, /device:TPU:1 now
where the time goes in v1:
time: 216 us; the launch traced here: 215 us
  blocking collectives  70.2 us (32%)
  starting transfers between devices  60.1 us (28%)
  waiting for transfers between devices  47.8 us (22%)
  Pallas kernels  27.1 us (13%)
  local copies, waits for them, and re-layouts  7.54 us (3%)
    all_to_all x5, blocking collectives, exchange(): lax.all_to_all(parts, axis, 0, 0, axis_index_groups=groups, tiled=True)  70.2 us
    ppermute x21, starting transfers between devices, permute(): return lax.ppermute(value, AXES, pairs)  45.9 us
    ppermute x21, waiting for transfers between devices, permute(): return lax.ppermute(value, AXES, pairs)  42.3 us
    pallas_call x13, Pallas kernels, call(): pl.pallas_call(body, out_shape=outs, in_specs=[smem] * scalars + [spec] *...  27.1 us
    all_to_all x3, starting transfers between devices, exchange(): lax.all_to_all(parts, axis, 0, 0, axis_index_groups=groups, tiled=True)  14.3 us
    unnamed x36, local copies, waits for them, and re-layouts  7.03 us
    all_to_all x3, waiting for transfers between devices, exchange(): lax.all_to_all(parts, axis, 0, 0, axis_index_groups=groups, tiled=True)  5.52 us
  transfers between devices with their start and end apart: 24, of which 12 were waited for; matrix products, arithmetic and copies ran while one was open for 1% of the time, Pallas kernels for 5%

profile of v1, /device:TPU:1, one launch (start us, length us, event | category | flops | bytes accessed | tf_op | source)
XLA Modules:
  0.0 215.2 jit_solution(15146737766530324679)
XLA Ops:
  5.3 6.5 %all-to-all-start = ((f32[8,144,128]{2,1,0:T(8,128)}), f32[8,144,128]{2,1,0:T(8,128)S(1)}, u32[]{:S(2)}, u32[]{:S(2)}) async-start(f32[8,144,128]{2,1,0:T(8,128)} %shard_map.120), calls=%async_computation | async-start | bytes 1179648 | tf_op jit(solution)/shard_map/all_to_all | solution.py:325
  13.9 4.7 %shard_map.121 = (f32[256,1024]{1,0:T(8,128)S(1)}, bf16[512,256]{1,0:T(8,128)(2,1)S(1)}, f32[512,256]{1,0:T(8,128)S(1)}) custom-call(s32[4]{0:T(128)S(1)} %pad_add_fusion.at, bf16[256,1024]{1,0:T(8,128)(2,1)S(1)} %bitcast.19, bf16[256,128]{1,0:T(8,128)(2,1)S(1)} %bitcast.23, bf16[256,128]{1,0:T(8,128)(2,1)S(1)} %bitcast.24, ...), custom_call_target="tpu_custom_call" | custom-call | flops 268435456 | bytes 3541008 | tf_op jit(solution)/shard_map/pallas_call | solution.py:43
  21.8 13.9 %all_to_all.40.packed = f32[8,144,128]{2,1,0:T(8,128)S(1)} all-to-all(f32[8,144,128]{2,1,0:T(8,128)S(1)} %get-tuple-element.29), channel_id=1, replica_groups=mesh['dp'=32,'tensor'=8] {'tensor'}, dimensions={0} | all-to-all | bytes 1179648 | tf_op jit(solution)/shard_map/all_to_all | solution.py:325
  36.9 9.3 %shard_map.123 = (bf16[256,768]{1,0:T(8,128)(2,1)S(1)}, f32[256,768]{1,0:T(8,128)}, f32[8,144,128]{2,1,0:T(8,128)S(1)}) custom-call(s32[4]{0:T(128)S(1)} %pad_add_fusion.at, f32[8,144,128]{2,1,0:T(8,128)S(1)} %all_to_all.40.packed, bf16[256,1024]{1,0:T(8,128)(2,1)S(1)} %bitcast.20, bf16[512,512]{1,0:T(8,128)(2,1)S(1)} %copy-done.7, ...), custom_call_target="tpu_custom_call" | custom-call | flops 671088640 | bytes 6031376 | tf_op jit(solution)/shard_map/pallas_call | solution.py:43
  46.2 10.8 %all_to_all.41.parts = f32[8,144,128]{2,1,0:T(8,128)S(1)} all-to-all(f32[8,144,128]{2,1,0:T(8,128)S(1)} %get-tuple-element.31), channel_id=1, replica_groups=mesh['dp'=32,'tensor'=8] {'tensor'}, dimensions={0} | all-to-all | bytes 1179648 | tf_op jit(solution)/shard_map/all_to_all | solution.py:325
  57.8 10.5 %all_to_all.42.packed = f32[8,144,128]{2,1,0:T(8,128)S(1)} all-to-all(f32[8,144,128]{2,1,0:T(8,128)S(1)} %shard_map.124), channel_id=1, replica_groups=mesh['dp'=32,'tensor'=8] {'tensor'}, dimensions={0} | all-to-all | bytes 1179648 | tf_op jit(solution)/shard_map/all_to_all | solution.py:325
  68.4 4.5 %collective-permute-start = (f32[8,144,128]{2,1,0:T(8,128)S(1)}, f32[8,144,128]{2,1,0:T(8,128)S(1)}, u32[]{:S(2)}, u32[]{:S(2)}) collective-permute-start(f32[8,144,128]{2,1,0:T(8,128)S(1)} %all_to_all.42.packed), channel_id=1, source_target_pairs={{0,8},{1,9},{2,10},{3,11},{4,12},{5,13},{6,14},{7,15},{8,0},{9,1},... | collective-permute-start | bytes 1769480 | tf_op jit(solution)/shard_map/ppermute | solution.py:306
  76.0 19.5 %all_to_all.43.parts = f32[4,4,144,128]{3,2,1,0:T(8,128)S(1)} all-to-all(f32[4,4,144,128]{3,2,1,0:T(8,128)S(1)} %bitcast.18), channel_id=1, replica_groups={{0,64,128,192},{8,72,136,200},{16,80,144,208},{24,88,152,216},{32,96,16..., dimensions={0} | all-to-all | bytes 2359296 | tf_op jit(solution)/shard_map/all_to_all | solution.py:325
  95.5 15.5 %all_to_all.44.parts = f32[4,144,128]{2,1,0:T(8,128)S(1)} all-to-all(f32[4,144,128]{2,1,0:T(8,128)S(1)} %shard_map.126), channel_id=1, replica_groups={{0,16,32,48},{8,24,40,56},{64,80,96,112},{72,88,104,120},{128,144,160,1..., dimensions={0} | all-to-all | bytes 589824 | tf_op jit(solution)/shard_map/all_to_all | solution.py:325
  111.7 4.1 %all-to-all-start.6 = ((f32[4,144,128]{2,1,0:T(8,128)}), f32[4,144,128]{2,1,0:T(8,128)S(1)}, u32[]{:S(2)}, u32[]{:S(2)}) async-start(f32[4,144,128]{2,1,0:T(8,128)} %shard_map.127), calls=%async_computation.6 | async-start | bytes 589824 | tf_op jit(solution)/shard_map/all_to_all | solution.py:325
  115.9 3.2 %collective-permute-start.4 = (f32[256,768]{1,0:T(8,128)}, f32[256,768]{1,0:T(8,128)S(1)}, u32[]{:S(2)}, u32[]{:S(2)}) collective-permute-start(f32[256,768]{1,0:T(8,128)} %get-tuple-element.39), channel_id=1, source_target_pairs={{0,8},{1,9},{2,10},{3,11},{4,12},{5,13},{6,14},{7,15},{8,0},{9,1},... | collective-permute-start | bytes 2359304 | tf_op jit(solution)/shard_map/ppermute | solution.py:306
  119.1 5.0 %all-to-all-done.6.value = f32[4,144,128]{2,1,0:T(8,128)S(1)} async-done(((f32[4,144,128]{2,1,0:T(8,128)}), f32[4,144,128]{2,1,0:T(8,128)S(1)}, u32[]{:S(2)}, u32[]{:S(2)}) %all-to-all-start.6) | async-done | bytes 294944 | tf_op jit(solution)/shard_map/all_to_all | solution.py:325
  125.2 3.7 %all-to-all-start.7 = ((f32[4,4,144,128]{3,2,1,0:T(8,128)}), f32[4,4,144,128]{3,2,1,0:T(8,128)S(1)}, u32[]{:S(2)}, u32[]{:S(2)}) async-start(f32[4,4,144,128]{3,2,1,0:T(8,128)} %shard_map.128), calls=%async_computation.7 | async-start | bytes 2359296 | tf_op jit(solution)/shard_map/all_to_all | solution.py:325
  136.0 15.8 %collective-permute-done.5.first = f32[128,768]{1,0:T(8,128)S(1)} collective-permute-done((f32[128,768]{1,0:T(8,128)S(1)}, f32[128,768]{1,0:T(8,128)S(1)}, u32[]{:S(2)}, u32[]{:S(2)}) %collective-permute-start.5) | collective-permute-done | bytes 393248 | tf_op jit(solution)/shard_map/ppermute | solution.py:306
  151.7 5.6 %collective-permute-done.6.second = f32[128,768]{1,0:T(8,128)S(1)} collective-permute-done((f32[128,768]{1,0:T(8,128)S(1)}, f32[128,768]{1,0:T(8,128)S(1)}, u32[]{:S(2)}, u32[]{:S(2)}) %collective-permute-start.6) | collective-permute-done | bytes 393248 | tf_op jit(solution)/shard_map/ppermute | solution.py:306
  158.0 3.7 %collective-permute-start.8 = (f32[32,768]{1,0:T(8,128)S(1)}, f32[32,768]{1,0:T(8,128)S(1)}, u32[]{:S(2)}, u32[]{:S(2)}) collective-permute-start(f32[32,768]{1,0:T(8,128)S(1)} %get-tuple-element.45), channel_id=1, source_target_pairs={{0,16},{1,17},{2,18},{3,19},{4,20},{5,21},{6,22},{7,23},{8,24},{9,... | collective-permute-start | bytes 294920 | tf_op jit(solution)/shard_map/ppermute | solution.py:306
  161.7 3.4 %collective-permute-start.10 = (f32[32,768]{1,0:T(8,128)S(1)}, f32[32,768]{1,0:T(8,128)S(1)}, u32[]{:S(2)}, u32[]{:S(2)}) collective-permute-start(f32[32,768]{1,0:T(8,128)S(1)} %get-tuple-element.47), channel_id=1, source_target_pairs={{0,48},{1,49},{2,50},{3,51},{4,52},{5,53},{6,54},{7,55},{8,56},{9,... | collective-permute-start | bytes 294920 | tf_op jit(solution)/shard_map/ppermute | solution.py:306
  165.1 4.9 %collective-permute-start.2 = (f32[16,144,128]{2,1,0:T(8,128)S(1)}, f32[16,144,128]{2,1,0:T(8,128)S(1)}, u32[]{:S(2)}, u32[]{:S(2)}) collective-permute-start(f32[16,144,128]{2,1,0:T(8,128)S(1)} %bitcast.16), channel_id=1, source_target_pairs={{0,8},{1,9},{2,10},{3,11},{4,12},{5,13},{6,14},{7,15},{8,0},{9,1},... | collective-permute-start | bytes 3538952 | tf_op jit(solution)/shard_map/ppermute | solution.py:306
  176.2 2.4 %collective-permute-done.13 = f32[32,768]{1,0:T(8,128)S(1)} collective-permute-done((f32[32,768]{1,0:T(8,128)S(1)}, f32[32,768]{1,0:T(8,128)S(1)}, u32[]{:S(2)}, u32[]{:S(2)}) %collective-permute-start.13) | collective-permute-done | bytes 98336 | tf_op jit(solution)/shard_map/ppermute | solution.py:306
  180.9 6.3 %collective-permute-start.16 = (f32[4,32,768]{2,1,0:T(8,128)S(1)}, f32[4,32,768]{2,1,0:T(8,128)S(1)}, u32[]{:S(2)}, u32[]{:S(2)}) collective-permute-start(f32[4,32,768]{2,1,0:T(8,128)S(1)} %pad_maximum_fusion.refs_0_), channel_id=1, source_target_pairs={{0,192},{1,193},{2,194},{3,195},{4,196},{5,197},{6,198},{7,199},{8... | collective-permute-start | bytes 1179656 | tf_op jit(solution)/shard_map/ppermute | solution.py:306
  187.8 6.1 %collective-permute-start.17 = (f32[4,32,768]{2,1,0:T(8,128)S(1)}, f32[4,32,768]{2,1,0:T(8,128)S(1)}, u32[]{:S(2)}, u32[]{:S(2)}) collective-permute-start(f32[4,32,768]{2,1,0:T(8,128)S(1)} %pad_maximum_fusion.refs_0_), channel_id=1, source_target_pairs={{0,8},{1,9},{2,10},{3,11},{4,12},{5,13},{6,14},{7,15},{8,0},{9,1},... | collective-permute-start | bytes 1179656 | tf_op jit(solution)/shard_map/ppermute | solution.py:306
  193.9 10.1 %collective-permute-done.16.refs_3_ = f32[4,32,768]{2,1,0:T(8,128)S(1)} collective-permute-done((f32[4,32,768]{2,1,0:T(8,128)S(1)}, f32[4,32,768]{2,1,0:T(8,128)S(1)}, u32[]{:S(2)}, u32[]{:S(2)}) %collective-permute-start.16) | collective-permute-done | bytes 393248 | tf_op jit(solution)/shard_map/ppermute | solution.py:306
  209.7 2.5 %shard_map.132 = (f32[512,512]{1,0:T(8,128)}, f32[512,1024]{1,0:T(8,128)}) custom-call(s32[4]{0:T(128)S(1)} %pad_add_fusion.at, f32[4,32,768]{2,1,0:T(8,128)S(1)} %pad_maximum_fusion.refs_0_, f32[4,32,768]{2,1,0:T(8,128)S(1)} %collective-permute-done.14.refs_1_, f32[4,32,768]{2,1,0:T(8,128)S(1)} %collective-permute-done.15.refs_2_, ...), custom_call_target="tpu_custom_call" | custom-call | bytes 6291472 | tf_op jit(solution)/shard_map/pallas_call | solution.py:43
  212.2 3.0 %shard_map.129 = (f32[1024,512]{1,0:T(8,128)}, f32[64,1024]{1,0:T(8,128)}) custom-call(s32[4]{0:T(128)S(1)} %pad_add_fusion.at, f32[16,144,128]{2,1,0:T(8,128)S(1)} %bitcast.17, f32[16,144,128]{2,1,0:T(8,128)S(1)} %collective-permute-done.2.other), custom_call_target="tpu_custom_call" | custom-call | bytes 4718608 | tf_op jit(solution)/shard_map/pallas_call | solution.py:43
  (91 shorter events, 39.5 us)
Async XLA Ops:
  5.3 16.4 %all-to-all-start = ((f32[8,144,128]{2,1,0:T(8,128)}), f32[8,144,128]{2,1,0:T(8,128)S(1)}, u32[]{:S(2)}, u32[]{:S(2)}) async-start(f32[8,144,128]{2,1,0:T(8,128)} %shard_map.120), calls=%async_computation | async-start | bytes 1179648 | tf_op jit(solution)/shard_map/all_to_all | solution.py:325
  68.4 6.9 %collective-permute-start = (f32[8,144,128]{2,1,0:T(8,128)S(1)}, f32[8,144,128]{2,1,0:T(8,128)S(1)}, u32[]{:S(2)}, u32[]{:S(2)}) collective-permute-start(f32[8,144,128]{2,1,0:T(8,128)S(1)} %all_to_all.42.packed), channel_id=1, source_target_pairs={{0,8},{1,9},{2,10},{3,11},{4,12},{5,13},{6,14},{7,15},{8,0},{9,1},... | collective-permute-start | bytes 1769480 | tf_op jit(solution)/shard_map/ppermute | solution.py:306
  72.9 2.4 %collective-permute-start.1 = (f32[512,256]{1,0:T(8,128)S(1)}, f32[512,256]{1,0:T(8,128)S(1)}, u32[]{:S(2)}, u32[]{:S(2)}) collective-permute-start(f32[512,256]{1,0:T(8,128)S(1)} %copy-done.17), channel_id=1, source_target_pairs={{0,8},{1,9},{2,10},{3,11},{4,12},{5,13},{6,14},{7,15},{8,0},{9,1},... | collective-permute-start | bytes 1572872 | tf_op jit(solution)/shard_map/ppermute | solution.py:306
  111.7 12.4 %all-to-all-start.6 = ((f32[4,144,128]{2,1,0:T(8,128)}), f32[4,144,128]{2,1,0:T(8,128)S(1)}, u32[]{:S(2)}, u32[]{:S(2)}) async-start(f32[4,144,128]{2,1,0:T(8,128)} %shard_map.127), calls=%async_computation.6 | async-start | bytes 589824 | tf_op jit(solution)/shard_map/all_to_all | solution.py:325
  115.9 13.0 %collective-permute-start.4 = (f32[256,768]{1,0:T(8,128)}, f32[256,768]{1,0:T(8,128)S(1)}, u32[]{:S(2)}, u32[]{:S(2)}) collective-permute-start(f32[256,768]{1,0:T(8,128)} %get-tuple-element.39), channel_id=1, source_target_pairs={{0,8},{1,9},{2,10},{3,11},{4,12},{5,13},{6,14},{7,15},{8,0},{9,1},... | collective-permute-start | bytes 2359304 | tf_op jit(solution)/shard_map/ppermute | solution.py:306
  119.0 9.8 %collective-permute-start.3 = (f32[8,144,128]{2,1,0:T(8,128)S(1)}, f32[8,144,128]{2,1,0:T(8,128)}, u32[]{:S(2)}, u32[]{:S(2)}) collective-permute-start(f32[8,144,128]{2,1,0:T(8,128)S(1)} %all_to_all.40.packed), channel_id=1, source_target_pairs={{0,8},{1,9},{2,10},{3,11},{4,12},{5,13},{6,14},{7,15},{8,0},{9,1},... | collective-permute-start | bytes 1769480 | tf_op jit(solution)/shard_map/ppermute | solution.py:306
  125.2 39.9 %all-to-all-start.7 = ((f32[4,4,144,128]{3,2,1,0:T(8,128)}), f32[4,4,144,128]{3,2,1,0:T(8,128)S(1)}, u32[]{:S(2)}, u32[]{:S(2)}) async-start(f32[4,4,144,128]{3,2,1,0:T(8,128)} %shard_map.128), calls=%async_computation.7 | async-start | bytes 2359296 | tf_op jit(solution)/shard_map/all_to_all | solution.py:325
  130.9 20.8 %collective-permute-start.5 = (f32[128,768]{1,0:T(8,128)S(1)}, f32[128,768]{1,0:T(8,128)S(1)}, u32[]{:S(2)}, u32[]{:S(2)}) collective-permute-start(f32[128,768]{1,0:T(8,128)S(1)} %get-tuple-element.41), channel_id=1, source_target_pairs={{0,64},{1,65},{2,66},{3,67},{4,68},{5,69},{6,70},{7,71},{8,72},{9,... | collective-permute-start | bytes 1179656 | tf_op jit(solution)/shard_map/ppermute | solution.py:306
  132.4 24.9 %collective-permute-start.6 = (f32[128,768]{1,0:T(8,128)S(1)}, f32[128,768]{1,0:T(8,128)S(1)}, u32[]{:S(2)}, u32[]{:S(2)}) collective-permute-start(f32[128,768]{1,0:T(8,128)S(1)} %get-tuple-element.42), channel_id=1, source_target_pairs={{0,128},{1,129},{2,130},{3,131},{4,132},{5,133},{6,134},{7,135},{8... | collective-permute-start | bytes 1179656 | tf_op jit(solution)/shard_map/ppermute | solution.py:306
  134.8 22.5 %collective-permute-start.7 = (f32[128,768]{1,0:T(8,128)S(1)}, f32[128,768]{1,0:T(8,128)S(1)}, u32[]{:S(2)}, u32[]{:S(2)}) collective-permute-start(f32[128,768]{1,0:T(8,128)S(1)} %get-tuple-element.43), channel_id=1, source_target_pairs={{0,192},{1,193},{2,194},{3,195},{4,196},{5,197},{6,198},{7,199},{8... | collective-permute-start | bytes 1179656 | tf_op jit(solution)/shard_map/ppermute | solution.py:306
  158.0 12.0 %collective-permute-start.8 = (f32[32,768]{1,0:T(8,128)S(1)}, f32[32,768]{1,0:T(8,128)S(1)}, u32[]{:S(2)}, u32[]{:S(2)}) collective-permute-start(f32[32,768]{1,0:T(8,128)S(1)} %get-tuple-element.45), channel_id=1, source_target_pairs={{0,16},{1,17},{2,18},{3,19},{4,20},{5,21},{6,22},{7,23},{8,24},{9,... | collective-permute-start | bytes 294920 | tf_op jit(solution)/shard_map/ppermute | solution.py:306
  161.7 9.1 %collective-permute-start.9 = (f32[32,768]{1,0:T(8,128)S(1)}, f32[32,768]{1,0:T(8,128)S(1)}, u32[]{:S(2)}, u32[]{:S(2)}) collective-permute-start(f32[32,768]{1,0:T(8,128)S(1)} %get-tuple-element.46), channel_id=1, source_target_pairs={{0,32},{1,33},{2,34},{3,35},{4,36},{5,37},{6,38},{7,39},{8,40},{9,... | collective-permute-start | bytes 294920 | tf_op jit(solution)/shard_map/ppermute | solution.py:306
  161.7 9.1 %collective-permute-start.10 = (f32[32,768]{1,0:T(8,128)S(1)}, f32[32,768]{1,0:T(8,128)S(1)}, u32[]{:S(2)}, u32[]{:S(2)}) collective-permute-start(f32[32,768]{1,0:T(8,128)S(1)} %get-tuple-element.47), channel_id=1, source_target_pairs={{0,48},{1,49},{2,50},{3,51},{4,52},{5,53},{6,54},{7,55},{8,56},{9,... | collective-permute-start | bytes 294920 | tf_op jit(solution)/shard_map/ppermute | solution.py:306
  165.1 47.1 %collective-permute-start.2 = (f32[16,144,128]{2,1,0:T(8,128)S(1)}, f32[16,144,128]{2,1,0:T(8,128)S(1)}, u32[]{:S(2)}, u32[]{:S(2)}) collective-permute-start(f32[16,144,128]{2,1,0:T(8,128)S(1)} %bitcast.16), channel_id=1, source_target_pairs={{0,8},{1,9},{2,10},{3,11},{4,12},{5,13},{6,14},{7,15},{8,0},{9,1},... | collective-permute-start | bytes 3538952 | tf_op jit(solution)/shard_map/ppermute | solution.py:306
  170.9 7.8 %collective-permute-start.13 = (f32[32,768]{1,0:T(8,128)S(1)}, f32[32,768]{1,0:T(8,128)S(1)}, u32[]{:S(2)}, u32[]{:S(2)}) collective-permute-start(f32[32,768]{1,0:T(8,128)S(1)} %add_add_fusion), channel_id=1, source_target_pairs={{0,48},{1,49},{2,50},{3,51},{4,52},{5,53},{6,54},{7,55},{8,56},{9,... | collective-permute-start | bytes 294920 | tf_op jit(solution)/shard_map/ppermute | solution.py:306
  172.2 7.6 %collective-permute-start.12 = (f32[32,768]{1,0:T(8,128)S(1)}, f32[32,768]{1,0:T(8,128)S(1)}, u32[]{:S(2)}, u32[]{:S(2)}) collective-permute-start(f32[32,768]{1,0:T(8,128)S(1)} %add_add_fusion), channel_id=1, source_target_pairs={{0,32},{1,33},{2,34},{3,35},{4,36},{5,37},{6,38},{7,39},{8,40},{9,... | collective-permute-start | bytes 294920 | tf_op jit(solution)/shard_map/ppermute | solution.py:306
  174.5 6.3 %collective-permute-start.11 = (f32[32,768]{1,0:T(8,128)S(1)}, f32[32,768]{1,0:T(8,128)S(1)}, u32[]{:S(2)}, u32[]{:S(2)}) collective-permute-start(f32[32,768]{1,0:T(8,128)S(1)} %add_add_fusion), channel_id=1, source_target_pairs={{0,16},{1,17},{2,18},{3,19},{4,20},{5,21},{6,22},{7,23},{8,24},{9,... | collective-permute-start | bytes 294920 | tf_op jit(solution)/shard_map/ppermute | solution.py:306
  180.9 23.2 %collective-permute-start.16 = (f32[4,32,768]{2,1,0:T(8,128)S(1)}, f32[4,32,768]{2,1,0:T(8,128)S(1)}, u32[]{:S(2)}, u32[]{:S(2)}) collective-permute-start(f32[4,32,768]{2,1,0:T(8,128)S(1)} %pad_maximum_fusion.refs_0_), channel_id=1, source_target_pairs={{0,192},{1,193},{2,194},{3,195},{4,196},{5,197},{6,198},{7,199},{8... | collective-permute-start | bytes 1179656 | tf_op jit(solution)/shard_map/ppermute | solution.py:306
  187.2 17.8 %collective-permute-start.15 = (f32[4,32,768]{2,1,0:T(8,128)S(1)}, f32[4,32,768]{2,1,0:T(8,128)S(1)}, u32[]{:S(2)}, u32[]{:S(2)}) collective-permute-start(f32[4,32,768]{2,1,0:T(8,128)S(1)} %pad_maximum_fusion.refs_0_), channel_id=1, source_target_pairs={{0,128},{1,129},{2,130},{3,131},{4,132},{5,133},{6,134},{7,135},{8... | collective-permute-start | bytes 1179656 | tf_op jit(solution)/shard_map/ppermute | solution.py:306
  187.2 19.4 %collective-permute-start.14 = (f32[4,32,768]{2,1,0:T(8,128)S(1)}, f32[4,32,768]{2,1,0:T(8,128)S(1)}, u32[]{:S(2)}, u32[]{:S(2)}) collective-permute-start(f32[4,32,768]{2,1,0:T(8,128)S(1)} %pad_maximum_fusion.refs_0_), channel_id=1, source_target_pairs={{0,64},{1,65},{2,66},{3,67},{4,68},{5,69},{6,70},{7,71},{8,72},{9,... | collective-permute-start | bytes 1179656 | tf_op jit(solution)/shard_map/ppermute | solution.py:306
  187.8 20.5 %collective-permute-start.17 = (f32[4,32,768]{2,1,0:T(8,128)S(1)}, f32[4,32,768]{2,1,0:T(8,128)S(1)}, u32[]{:S(2)}, u32[]{:S(2)}) collective-permute-start(f32[4,32,768]{2,1,0:T(8,128)S(1)} %pad_maximum_fusion.refs_0_), channel_id=1, source_target_pairs={{0,8},{1,9},{2,10},{3,11},{4,12},{5,13},{6,14},{7,15},{8,0},{9,1},... | collective-permute-start | bytes 1179656 | tf_op jit(solution)/shard_map/ppermute | solution.py:306
  204.0 4.3 %collective-permute-start.20 = (f32[4,32,768]{2,1,0:T(8,128)S(1)}, f32[4,32,768]{2,1,0:T(8,128)S(1)}, u32[]{:S(2)}, u32[]{:S(2)}) collective-permute-start(f32[4,32,768]{2,1,0:T(8,128)S(1)} %collective-permute-done.16.refs_3_), channel_id=1, source_target_pairs={{0,8},{1,9},{2,10},{3,11},{4,12},{5,13},{6,14},{7,15},{8,0},{9,1},... | collective-permute-start | bytes 1179656 | tf_op jit(solution)/shard_map/ppermute | solution.py:306
  204.9 3.4 %collective-permute-start.19 = (f32[4,32,768]{2,1,0:T(8,128)S(1)}, f32[4,32,768]{2,1,0:T(8,128)S(1)}, u32[]{:S(2)}, u32[]{:S(2)}) collective-permute-start(f32[4,32,768]{2,1,0:T(8,128)S(1)} %collective-permute-done.15.refs_2_), channel_id=1, source_target_pairs={{0,8},{1,9},{2,10},{3,11},{4,12},{5,13},{6,14},{7,15},{8,0},{9,1},... | collective-permute-start | bytes 1179656 | tf_op jit(solution)/shard_map/ppermute | solution.py:306
  206.6 3.1 %collective-permute-start.18 = (f32[4,32,768]{2,1,0:T(8,128)S(1)}, f32[4,32,768]{2,1,0:T(8,128)S(1)}, u32[]{:S(2)}, u32[]{:S(2)}) collective-permute-start(f32[4,32,768]{2,1,0:T(8,128)S(1)} %collective-permute-done.14.refs_1_), channel_id=1, source_target_pairs={{0,8},{1,9},{2,10},{3,11},{4,12},{5,13},{6,14},{7,15},{8,0},{9,1},... | collective-permute-start | bytes 1179656 | tf_op jit(solution)/shard_map/ppermute | solution.py:306
  (18 other events, 96.5 us)

commit v2 on v1

--- a/solution.py
+++ b/solution.py
@@ -1,3 +1,4 @@
+import functools
 import math
 
 import jax
@@ -35,18 +36,23 @@
     return lax.dot_general(a, b, TN, preferred_element_type=F32)
 
 
-def call(body, outs, *args, scalars=0, scratch=(), flops=0):
+def call(body, outs, *args, scalars=0, scratch=(), flops=0, mib=20, aliases=None):
     spec = pl.BlockSpec(memory_space=pltpu.VMEM)
     smem = pl.BlockSpec(memory_space=pltpu.SMEM)
+    anywhere = pl.BlockSpec(memory_space=pl.ANY)
+    specs = [smem] * scalars + [spec] * (len(args) - scalars)
+    for k in aliases or {}:
+        specs[k] = anywhere
     size = sum(a.size * a.dtype.itemsize for a in args)
     size += sum(math.prod(o.shape) * o.dtype.itemsize for o in outs)
     return pl.pallas_call(
         body,
         out_shape=outs,
-        in_specs=[smem] * scalars + [spec] * (len(args) - scalars),
-        out_specs=[spec] * len(outs),
+        in_specs=specs,
+        out_specs=[anywhere if aliases is not None else spec] * len(outs),
         scratch_shapes=list(scratch),
-        compiler_params=pltpu.CompilerParams(vmem_limit_bytes=20 << 20),
+        input_output_aliases=aliases or {},
+        compiler_params=pltpu.CompilerParams(vmem_limit_bytes=mib << 20),
         cost_estimate=pl.CostEstimate(flops=flops, bytes_accessed=size, transcendentals=0),
     )(*args)
 
@@ -236,15 +242,27 @@
         outs[step][...] = (own[rows, :] + first[rows, :]) + (second[rows, :] + third[rows, :])
 
 
-def entry_grad_kernel(packed, other_packed, tokens, other_tokens, out, grads, rest):
-    unpack(packed, grads, rest)
-    grads[:, 512:] = jnp.where(low_lanes(SEQ), rest[...], 0.0).astype(BF16)
-    whole = dot(tokens[...], grads[...])
-    unpack(other_packed, grads, rest)
-    grads[:, 512:] = jnp.where(low_lanes(SEQ), rest[...], 0.0).astype(BF16)
-    whole = whole + dot(other_tokens[...].astype(BF16), grads[...])
-    for k in range(16):
-        pack(out, k, 32 * k, whole[:, :512], whole[:, 512:])
+def entry_grad_kernel(at, packed, other_packed, tokens, other_tokens, *refs):
+    *outs, grads, other_grads, rest = refs
+    for source, ref in ((packed, grads), (other_packed, other_grads)):
+        unpack(source, ref, rest)
+        ref[:, 512:] = jnp.where(low_lanes(SEQ), rest[...], 0.0).astype(BF16)
+    for step in range(4):
+        rows = pl.ds(pl.multiple_of((at[1] + step) % 4 * 128, 128), 128)
+        whole = dot(tokens[rows, :], grads[...])
+        whole = whole + dot(other_tokens[rows, :].astype(BF16), other_grads[...])
+        for k in range(4):
+            pack(outs[step], k, 32 * k, whole[:, :512], whole[:, 512:])
+
+
+def entry_split_kernel(at, own, first, second, third, *outs):
+    for step in range(4):
+        k = (at[2] + step) % 4
+        outs[step][...] = (own[k] + first[k]) + (second[k] + third[k])
+
+
+def entry_sum_kernel(own, first, second, third, out):
+    out[...] = (own[...] + first[...]) + (second[...] + third[...])
 
 
 def up_out_kernel(at, *refs):
@@ -262,37 +280,35 @@
                 value_out[rows, values] = ref[depth, :, 256:]
 
 
-def entry_out_kernel(at, own, other, down_out, rope_out, rest):
-    c = at[0]
-    for half, ref in ((c, own), (1 - c, other)):
-        def group(g, carry, half=half, ref=ref):
-            first = half * 4 + g
-            for b in range(4):
-                rows = pl.ds(pl.multiple_of(first * 128 + 32 * b, 32), 32)
-                for j in range(4):
-                    down_out[rows, 128 * j : 128 * j + 128] = ref[
-                        4 * g + b, 32 * j : 32 * j + 32, :
-                    ]
-                unpack_rest(ref[4 * g + b, 128:PACKED, :], rest, 32 * b)
-            rope_out[:, lanes(first)] = rest[...].T[:64]
-            return carry
-
-        lax.fori_loop(0, 4, group, 0)
-
-
-def sum_kernel(parts, out):
-    out[...] = (parts[0] + parts[1]) + (parts[2] + parts[3])
-
-
-def sum_spread_kernel(parts, out):
-    total = (parts[0] + parts[1]) + (parts[2] + parts[3])
-    for k in range(4):
-        out[k] = total
-
-
-def spread_kernel(value, out):
-    for k in range(4):
-        out[k] = value[...]
+def entry_out_kernel(own, at, *refs):
+    parts, (down_out, rope_out, down, rope, rest, sems) = refs[:4], refs[-6:]
+    half = at[0] if own else 1 - at[0]
+    for step in range(4):
+        first = (at[1] - step + 4) % 4
+        for depth in range(4):
+            spot = (at[2] - depth + 4) % 4 * 32
+            rows = pl.ds(pl.multiple_of(first * 128 + spot, 32), 32)
+            for j in range(4):
+                down[rows, 128 * j : 128 * j + 128] = parts[step][depth, 32 * j : 32 * j + 32, :]
+            value = parts[step][depth, 128:PACKED, :]
+            rest[pl.ds(pl.multiple_of(spot, 32), 16), :] = value
+            rest[pl.ds(pl.multiple_of(spot + 16, 16), 16), :] = pltpu.roll(value, 64, 1)
+        rope[:, lanes(first)] = rest[...].T[:64]
+    where = pl.ds(pl.multiple_of(half * 512, 512), 512)
+    copies = [
+        pltpu.make_async_copy(down, down_out.at[where, :], sems.at[0]),
+        pltpu.make_async_copy(rope, rope_out.at[:, where], sems.at[1]),
+    ]
+    for copy in copies:
+        copy.start()
+    for copy in copies:
+        copy.wait()
+
+
+def stack_kernel(*refs):
+    *parts, out = refs
+    for k, part in enumerate(parts):
+        out[k] = part[...]
 
 
 def permute(value, move):
@@ -316,13 +332,8 @@
     return [permute(v, move) for v, move in zip(values, moves)]
 
 
-X_GROUPS = [[8 * x + r for x in range(4)] for r in range(8)]
-H_GROUPS = [[8 * x + 2 * h + c for h in range(4)] for x in range(4) for c in range(2)]
-
-
-def exchange(parts, groups=None):
-    axis = "tensor" if groups is None else "dp"
-    return lax.all_to_all(parts, axis, 0, 0, axis_index_groups=groups, tiled=True)
+def exchange(parts):
+    return lax.all_to_all(parts, "tensor", 0, 0, tiled=True)
 
 
 def tables(segments):
@@ -351,14 +362,14 @@
     chunks = shape(8, PACKED, 128)
     unpacked = [pltpu.VMEM((SEQ, LATENT), BF16), pltpu.VMEM((SEQ, 128), F32)]
 
-    (part,) = call(entry_kernel, [chunks], tokens, down, rope, flops=2 * 256 * 1024 * 576)
+    (part,) = call(entry_kernel, [chunks], tokens, down, rope, flops=2 * 256 * 1024 * 576, mib=60)
     parts = exchange(part)
     table = tables(segments)
     teacher, tokens_keep, tokens_send = call(
         teacher_kernel,
         [shape(SEQ, 1024), shape(512, SEQ, dtype=BF16), shape(512, SEQ)],
         at, queries, keys[0], values[0], table, seg_col, seg_row, tokens,
-        scalars=1, flops=4 * 8 * 256 * 256 * 128,
+        scalars=1, flops=4 * 8 * 256 * 256 * 128, mib=60,
     )
     tokens_other = other_core(tokens_send)
     parts, teacher = lax.optimization_barrier((parts, teacher))
@@ -376,7 +387,7 @@
             pltpu.VMEM((SEQ, 128), F32),
             pltpu.VMEM((SEQ, 1536), BF16),
         ],
-        flops=10 * 8 * 256 * 256 * 128,
+        flops=10 * 8 * 256 * 256 * 128, mib=60,
     )
     grads_other = other_core(grads_send)
     parts = exchange(part)
@@ -388,32 +399,44 @@
     (replicas,) = call(norm_grad_kernel, [chunks], at, parts, normed, inv, table, scalars=1)
     packed = exchange(replicas)
     packed_other = other_core(packed)
-    (entry,) = call(
-        entry_grad_kernel, [shape(16, PACKED, 128)],
-        packed, packed_other, tokens_keep, tokens_other,
-        scratch=[pltpu.VMEM((SEQ, 640), BF16), pltpu.VMEM((SEQ, 128), F32)],
-        flops=2 * 512 * 512 * 640,
-    )
-    entry = exchange(entry.reshape(4, 4, PACKED, 128), X_GROUPS)
     quarters = call(split_kernel, [shape(32, 768)] * 4, at, quarters[0], *received, scalars=1)
     received = around(list(quarters[1:]), "h")
-    (entry,) = call(sum_kernel, [shape(4, PACKED, 128)], entry)
-    entry = exchange(entry, H_GROUPS)
+    entries = call(
+        entry_grad_kernel, [shape(4, PACKED, 128)] * 4,
+        at, packed, packed_other, tokens_keep, tokens_other, scalars=1,
+        scratch=[pltpu.VMEM((SEQ, 640), BF16)] * 2 + [pltpu.VMEM((SEQ, 128), F32)],
+        flops=2 * 512 * 512 * 640,
+    )
+    arrived = around(list(entries[1:]), "x")
     up = (quarters[0] + received[0]) + (received[1] + received[2])
-    up_all = jnp.stack([up] + around(up, "h"))
-    (entry,) = call(sum_spread_kernel, [shape(4, PACKED, 128)], entry)
-    entry = exchange(entry, H_GROUPS)
+    (up_all,) = call(stack_kernel, [shape(4, 32, 768)], up, *around(up, "h"))
+    entries = call(
+        entry_split_kernel, [shape(PACKED, 128)] * 4, at, entries[0], *arrived, scalars=1,
+    )
+    arrived = around(list(entries[1:]), "h")
     received = [up_all] + around(up_all, "x")
-    (entry,) = call(spread_kernel, [shape(4, 4, PACKED, 128)], entry)
-    entry = exchange(entry, X_GROUPS).reshape(16, PACKED, 128)
+    (entry,) = call(entry_sum_kernel, [shape(PACKED, 128)], entries[0], *arrived)
+    entry = jnp.stack([entry] + around(entry, "h"))
+    entries = [entry] + around(entry, "x")
     others = [other_core(v) for v in received]
     grad_key, grad_value = call(
         up_out_kernel, [shape(512, 512), shape(512, 1024)], at, *received, *others, scalars=1,
     )
-    entry_other = other_core(entry)
+    others = [other_core(v) for v in entries]
+    outs = [shape(1024, 512), shape(64, 1024)]
+    scratch = [
+        pltpu.VMEM((512, 512), F32),
+        pltpu.VMEM((64, 512), F32),
+        pltpu.VMEM((128, 128), F32),
+        pltpu.SemaphoreType.DMA((2,)),
+    ]
+    halves = call(
+        functools.partial(entry_out_kernel, True), outs, at, *entries, scalars=1,
+        scratch=scratch, aliases={},
+    )
     grad_down, grad_rope = call(
-        entry_out_kernel, [shape(1024, 512), shape(64, 1024)], at, entry, entry_other,
-        scalars=1, scratch=[pltpu.VMEM((128, 128), F32)],
+        functools.partial(entry_out_kernel, False), outs, at, *others, *halves, scalars=1,
+        scratch=scratch, aliases={5: 0, 6: 1},
     )
     return grad_down, grad_rope, grad_key, grad_value
 

time: 216 us -> 191 us (0.88)
  the two profiles are of different devices: /device:TPU:1 before, /device:TPU:32 now
where the time goes in v2:
time: 191 us; the launch traced here: 190 us
  starting transfers between devices  70.1 us (37%)
  waiting for transfers between devices  53.6 us (28%)
  Pallas kernels  33.4 us (17%)
  blocking collectives  27.6 us (14%)
  other arithmetic  2 us (1%)
  local copies, waits for them, and re-layouts  1.92 us (1%)
    ppermute x36, starting transfers between devices, permute(): return lax.ppermute(value, AXES, pairs)  59.5 us
    ppermute x36, waiting for transfers between devices, permute(): return lax.ppermute(value, AXES, pairs)  53.6 us
    pallas_call x14, Pallas kernels, call(): pl.pallas_call(body, out_shape=outs, in_specs=specs, out_specs=[anywhere...  33.4 us
    all_to_all x2, blocking collectives, exchange(): return lax.all_to_all(parts, 'tensor', 0, 0, tiled=True)  27.6 us
    all_to_all x2, starting transfers between devices, exchange(): return lax.all_to_all(parts, 'tensor', 0, 0, tiled=True)  10.7 us
  transfers between devices with their start and end apart: 38, of which 13 were waited for; matrix products, arithmetic and copies ran while one was open for 2% of the time, Pallas kernels for 8%

profile of v2, /device:TPU:32, one launch (start us, length us, event | category | flops | bytes accessed | tf_op | source)
XLA Modules:
  0.0 189.7 jit_solution(2204254567954366692)
XLA Ops:
  0.6 2.8 %shard_map.120 = f32[8,144,128]{2,1,0:T(8,128)} custom-call(bf16[256,1024]{1,0:T(8,128)(2,1)} %bitcast.17, bf16[1024,512]{1,0:T(8,128)(2,1)} %down.1, bf16[64,1024]{1,0:T(8,128)(2,1)} %rope.1), custom_call_target="tpu_custom_call" | custom-call | flops 301989888 | bytes 2293760 | tf_op jit(solution)/shard_map/pallas_call | solution.py:48
  3.5 5.9 %all-to-all-start = ((f32[8,144,128]{2,1,0:T(8,128)}), f32[8,144,128]{2,1,0:T(8,128)S(1)}, u32[]{:S(2)}, u32[]{:S(2)}) async-start(f32[8,144,128]{2,1,0:T(8,128)} %shard_map.120), calls=%async_computation | async-start | bytes 1179648 | tf_op jit(solution)/shard_map/all_to_all | solution.py:336
  13.3 6.7 %shard_map.121 = (f32[256,1024]{1,0:T(8,128)}, bf16[512,256]{1,0:T(8,128)(2,1)}, f32[512,256]{1,0:T(8,128)}) custom-call(s32[4]{0:T(128)} %pad_add_fusion.at, bf16[256,1024]{1,0:T(8,128)(2,1)} %bitcast.15, bf16[256,128]{1,0:T(8,128)(2,1)} %bitcast.22, bf16[256,128]{1,0:T(8,128)(2,1)} %bitcast.23, f32[256,512]{1,0:T(8,128)} %concatenate.3.table, ...), custom_call_target="tpu_custom_call" | custom-call | flops 268435456 | bytes 3541008 | tf_op jit(solution)/shard_map/pallas_call | solution.py:48
  20.2 14.7 %all_to_all.20.packed = f32[8,144,128]{2,1,0:T(8,128)} all-to-all(f32[8,144,128]{2,1,0:T(8,128)S(1)} %get-tuple-element.39), channel_id=1, replica_groups=mesh['dp'=32,'tensor'=8] {'tensor'}, dimensions={0} | all-to-all | bytes 1179648 | tf_op jit(solution)/shard_map/all_to_all | solution.py:336
  34.8 11.3 %shard_map.123 = (bf16[256,768]{1,0:T(8,128)(2,1)}, f32[256,768]{1,0:T(8,128)}, f32[8,144,128]{2,1,0:T(8,128)}) custom-call(s32[4]{0:T(128)} %pad_add_fusion.at, f32[8,144,128]{2,1,0:T(8,128)} %all_to_all.20.packed, bf16[256,1024]{1,0:T(8,128)(2,1)} %bitcast.16, bf16[512,512]{1,0:T(8,128)(2,1)} %key_up.1, bf16[512,1024]{1,0:T(8,128)(2,1)} %value_up.1, ...), custom_call_target="tpu_custom_call" | custom-call | flops 671088640 | bytes 6031376 | tf_op jit(solution)/shard_map/pallas_call | solution.py:48
  46.2 13.0 %all_to_all.21.parts = f32[8,144,128]{2,1,0:T(8,128)S(1)} all-to-all(f32[8,144,128]{2,1,0:T(8,128)} %get-tuple-element.41), channel_id=1, replica_groups=mesh['dp'=32,'tensor'=8] {'tensor'}, dimensions={0} | all-to-all | bytes 1179648 | tf_op jit(solution)/shard_map/all_to_all | solution.py:336
  60.7 4.7 %all-to-all-start.3 = ((f32[8,144,128]{2,1,0:T(8,128)}), f32[8,144,128]{2,1,0:T(8,128)S(1)}, u32[]{:S(2)}, u32[]{:S(2)}) async-start(f32[8,144,128]{2,1,0:T(8,128)} %shard_map.124), calls=%async_computation.3 | async-start | bytes 1179648 | tf_op jit(solution)/shard_map/all_to_all | solution.py:336
  72.3 2.7 %collective-permute-start.21 = (f32[128,768]{1,0:T(8,128)S(1)}, f32[128,768]{1,0:T(8,128)S(1)}, u32[]{:S(2)}, u32[]{:S(2)}) collective-permute-start(f32[128,768]{1,0:T(8,128)S(1)} %get-tuple-element.62), channel_id=1, source_target_pairs={{0,128},{1,129},{2,130},{3,131},{4,132},{5,133},{6,134},{7,135},{8... | collective-permute-start | bytes 1179656 | tf_op jit(solution)/shard_map/ppermute | solution.py:322
  77.0 6.4 %collective-permute-done.20.first = f32[128,768]{1,0:T(8,128)S(1)} collective-permute-done((f32[128,768]{1,0:T(8,128)}, f32[128,768]{1,0:T(8,128)S(1)}, u32[]{:S(2)}, u32[]{:S(2)}) %collective-permute-start.20) | collective-permute-done | bytes 393248 | tf_op jit(solution)/shard_map/ppermute | solution.py:322
  83.4 9.4 %collective-permute-done.21.second = f32[128,768]{1,0:T(8,128)S(1)} collective-permute-done((f32[128,768]{1,0:T(8,128)S(1)}, f32[128,768]{1,0:T(8,128)S(1)}, u32[]{:S(2)}, u32[]{:S(2)}) %collective-permute-start.21) | collective-permute-done | bytes 393248 | tf_op jit(solution)/shard_map/ppermute | solution.py:322
  93.5 6.4 %collective-permute-start.24 = (f32[32,768]{1,0:T(8,128)S(1)}, f32[32,768]{1,0:T(8,128)S(1)}, u32[]{:S(2)}, u32[]{:S(2)}) collective-permute-start(f32[32,768]{1,0:T(8,128)S(1)} %get-tuple-element.66), channel_id=1, source_target_pairs={{0,32},{1,33},{2,34},{3,35},{4,36},{5,37},{6,38},{7,39},{8,40},{9,... | collective-permute-start | bytes 294920 | tf_op jit(solution)/shard_map/ppermute | solution.py:322
  102.8 2.9 %collective-permute-done.24 = f32[32,768]{1,0:T(8,128)S(1)} collective-permute-done((f32[32,768]{1,0:T(8,128)S(1)}, f32[32,768]{1,0:T(8,128)S(1)}, u32[]{:S(2)}, u32[]{:S(2)}) %collective-permute-start.24) | collective-permute-done | bytes 98336 | tf_op jit(solution)/shard_map/ppermute | solution.py:322
  113.1 3.1 %collective-permute-start.3 = (f32[4,144,128]{2,1,0:T(8,128)S(1)}, f32[4,144,128]{2,1,0:T(8,128)S(1)}, u32[]{:S(2)}, u32[]{:S(2)}) collective-permute-start(f32[4,144,128]{2,1,0:T(8,128)S(1)} %get-tuple-element.48), channel_id=1, source_target_pairs={{0,128},{1,129},{2,130},{3,131},{4,132},{5,133},{6,134},{7,135},{8... | collective-permute-start | bytes 884744 | tf_op jit(solution)/shard_map/ppermute | solution.py:322
  116.8 4.1 %collective-permute-start.27 = (f32[32,768]{1,0:T(8,128)S(1)}, f32[32,768]{1,0:T(8,128)S(1)}, u32[]{:S(2)}, u32[]{:S(2)}) collective-permute-start(f32[32,768]{1,0:T(8,128)S(1)} %add_add_fusion.refs_0_), channel_id=1, source_target_pairs={{0,32},{1,33},{2,34},{3,35},{4,36},{5,37},{6,38},{7,39},{8,40},{9,... | collective-permute-start | bytes 294920 | tf_op jit(solution)/shard_map/ppermute | solution.py:322
  123.3 5.5 %collective-permute-done.27.refs_2_ = f32[32,768]{1,0:T(8,128)S(1)} collective-permute-done((f32[32,768]{1,0:T(8,128)S(1)}, f32[32,768]{1,0:T(8,128)S(1)}, u32[]{:S(2)}, u32[]{:S(2)}) %collective-permute-start.27) | collective-permute-done | bytes 98336 | tf_op jit(solution)/shard_map/ppermute | solution.py:322
  131.5 2.9 %collective-permute-start.5 = (f32[144,128]{1,0:T(8,128)S(1)}, f32[144,128]{1,0:T(8,128)S(1)}, u32[]{:S(2)}, u32[]{:S(2)}) collective-permute-start(f32[144,128]{1,0:T(8,128)S(1)} %get-tuple-element.51), channel_id=1, source_target_pairs={{0,16},{1,17},{2,18},{3,19},{4,20},{5,21},{6,22},{7,23},{8,24},{9,... | collective-permute-start | bytes 221192 | tf_op jit(solution)/shard_map/ppermute | solution.py:322
  134.4 3.3 %collective-permute-start.6 = (f32[144,128]{1,0:T(8,128)S(1)}, f32[144,128]{1,0:T(8,128)S(1)}, u32[]{:S(2)}, u32[]{:S(2)}) collective-permute-start(f32[144,128]{1,0:T(8,128)S(1)} %get-tuple-element.52), channel_id=1, source_target_pairs={{0,32},{1,33},{2,34},{3,35},{4,36},{5,37},{6,38},{7,39},{8,40},{9,... | collective-permute-start | bytes 221192 | tf_op jit(solution)/shard_map/ppermute | solution.py:322
  144.0 3.9 %collective-permute-done.7.third = f32[144,128]{1,0:T(8,128)S(1)} collective-permute-done((f32[144,128]{1,0:T(8,128)S(1)}, f32[144,128]{1,0:T(8,128)S(1)}, u32[]{:S(2)}, u32[]{:S(2)}) %collective-permute-start.7) | collective-permute-done | bytes 73760 | tf_op jit(solution)/shard_map/ppermute | solution.py:322
  147.9 2.7 %collective-permute-start.10 = (f32[144,128]{1,0:T(8,128)S(1)}, f32[144,128]{1,0:T(8,128)S(1)}, u32[]{:S(2)}, u32[]{:S(2)}) collective-permute-start(f32[144,128]{1,0:T(8,128)S(1)} %shard_map.127), channel_id=1, source_target_pairs={{0,48},{1,49},{2,50},{3,51},{4,52},{5,53},{6,54},{7,55},{8,56},{9,... | collective-permute-start | bytes 221192 | tf_op jit(solution)/shard_map/ppermute | solution.py:322
  150.6 4.5 %collective-permute-start.9 = (f32[144,128]{1,0:T(8,128)S(1)}, f32[144,128]{1,0:T(8,128)S(1)}, u32[]{:S(2)}, u32[]{:S(2)}) collective-permute-start(f32[144,128]{1,0:T(8,128)S(1)} %shard_map.127), channel_id=1, source_target_pairs={{0,32},{1,33},{2,34},{3,35},{4,36},{5,37},{6,38},{7,39},{8,40},{9,... | collective-permute-start | bytes 221192 | tf_op jit(solution)/shard_map/ppermute | solution.py:322
  157.8 3.1 %collective-permute-done.9 = f32[144,128]{1,0:T(8,128)S(1)} collective-permute-done((f32[144,128]{1,0:T(8,128)S(1)}, f32[144,128]{1,0:T(8,128)S(1)}, u32[]{:S(2)}, u32[]{:S(2)}) %collective-permute-start.9) | collective-permute-done | bytes 73760 | tf_op jit(solution)/shard_map/ppermute | solution.py:322
  160.8 4.4 %collective-permute-done.8 = f32[144,128]{1,0:T(8,128)S(1)} collective-permute-done((f32[144,128]{1,0:T(8,128)S(1)}, f32[144,128]{1,0:T(8,128)S(1)}, u32[]{:S(2)}, u32[]{:S(2)}) %collective-permute-start.8) | collective-permute-done | bytes 73760 | tf_op jit(solution)/shard_map/ppermute | solution.py:322
  172.6 2.9 %collective-permute-done.12.refs_1_ = f32[4,144,128]{2,1,0:T(8,128)S(1)} collective-permute-done((f32[4,144,128]{2,1,0:T(8,128)S(1)}, f32[4,144,128]{2,1,0:T(8,128)S(1)}, u32[]{:S(2)}, u32[]{:S(2)}) %collective-permute-start.12) | collective-permute-done | bytes 294944 | tf_op jit(solution)/shard_map/ppermute | solution.py:322
  175.5 7.4 %collective-permute-done.14.refs_2_ = f32[4,144,128]{2,1,0:T(8,128)S(1)} collective-permute-done((f32[4,144,128]{2,1,0:T(8,128)S(1)}, f32[4,144,128]{2,1,0:T(8,128)S(1)}, u32[]{:S(2)}, u32[]{:S(2)}) %collective-permute-start.14) | collective-permute-done | bytes 294944 | tf_op jit(solution)/shard_map/ppermute | solution.py:322
  (95 shorter events, 53.8 us)
Async XLA Ops:
  3.5 16.5 %all-to-all-start = ((f32[8,144,128]{2,1,0:T(8,128)}), f32[8,144,128]{2,1,0:T(8,128)S(1)}, u32[]{:S(2)}, u32[]{:S(2)}) async-start(f32[8,144,128]{2,1,0:T(8,128)} %shard_map.120), calls=%async_computation | async-start | bytes 1179648 | tf_op jit(solution)/shard_map/all_to_all | solution.py:336
  60.7 15.8 %all-to-all-start.3 = ((f32[8,144,128]{2,1,0:T(8,128)}), f32[8,144,128]{2,1,0:T(8,128)S(1)}, u32[]{:S(2)}, u32[]{:S(2)}) async-start(f32[8,144,128]{2,1,0:T(8,128)} %shard_map.124), calls=%async_computation.3 | async-start | bytes 1179648 | tf_op jit(solution)/shard_map/all_to_all | solution.py:336
  70.8 12.6 %collective-permute-start.20 = (f32[128,768]{1,0:T(8,128)}, f32[128,768]{1,0:T(8,128)S(1)}, u32[]{:S(2)}, u32[]{:S(2)}) collective-permute-start(f32[128,768]{1,0:T(8,128)} %get-tuple-element.61), channel_id=1, source_target_pairs={{0,64},{1,65},{2,66},{3,67},{4,68},{5,69},{6,70},{7,71},{8,72},{9,... | collective-permute-start | bytes 1179656 | tf_op jit(solution)/shard_map/ppermute | solution.py:322
  72.3 20.5 %collective-permute-start.21 = (f32[128,768]{1,0:T(8,128)S(1)}, f32[128,768]{1,0:T(8,128)S(1)}, u32[]{:S(2)}, u32[]{:S(2)}) collective-permute-start(f32[128,768]{1,0:T(8,128)S(1)} %get-tuple-element.62), channel_id=1, source_target_pairs={{0,128},{1,129},{2,130},{3,131},{4,132},{5,133},{6,134},{7,135},{8... | collective-permute-start | bytes 1179656 | tf_op jit(solution)/shard_map/ppermute | solution.py:322
  75.1 17.8 %collective-permute-start.22 = (f32[128,768]{1,0:T(8,128)S(1)}, f32[128,768]{1,0:T(8,128)S(1)}, u32[]{:S(2)}, u32[]{:S(2)}) collective-permute-start(f32[128,768]{1,0:T(8,128)S(1)} %get-tuple-element.63), channel_id=1, source_target_pairs={{0,192},{1,193},{2,194},{3,195},{4,196},{5,197},{6,198},{7,199},{8... | collective-permute-start | bytes 1179656 | tf_op jit(solution)/shard_map/ppermute | solution.py:322
  76.5 34.1 %collective-permute-start = (f32[8,144,128]{2,1,0:T(8,128)S(1)}, f32[8,144,128]{2,1,0:T(8,128)S(1)}, u32[]{:S(2)}, u32[]{:S(2)}) collective-permute-start(f32[8,144,128]{2,1,0:T(8,128)S(1)} %all-to-all-done.3.packed), channel_id=1, source_target_pairs={{0,8},{1,9},{2,10},{3,11},{4,12},{5,13},{6,14},{7,15},{8,0},{9,1},... | collective-permute-start | bytes 1769480 | tf_op jit(solution)/shard_map/ppermute | solution.py:322
  76.5 34.1 %collective-permute-start.1 = (f32[512,256]{1,0:T(8,128)}, f32[512,256]{1,0:T(8,128)S(1)}, u32[]{:S(2)}, u32[]{:S(2)}) collective-permute-start(f32[512,256]{1,0:T(8,128)} %get-tuple-element.45), channel_id=1, source_target_pairs={{0,8},{1,9},{2,10},{3,11},{4,12},{5,13},{6,14},{7,15},{8,0},{9,1},... | collective-permute-start | bytes 1572872 | tf_op jit(solution)/shard_map/ppermute | solution.py:322
  93.5 12.2 %collective-permute-start.24 = (f32[32,768]{1,0:T(8,128)S(1)}, f32[32,768]{1,0:T(8,128)S(1)}, u32[]{:S(2)}, u32[]{:S(2)}) collective-permute-start(f32[32,768]{1,0:T(8,128)S(1)} %get-tuple-element.66), channel_id=1, source_target_pairs={{0,32},{1,33},{2,34},{3,35},{4,36},{5,37},{6,38},{7,39},{8,40},{9,... | collective-permute-start | bytes 294920 | tf_op jit(solution)/shard_map/ppermute | solution.py:322
  108.2 12.7 %collective-permute-start.26 = (f32[32,768]{1,0:T(8,128)S(1)}, f32[32,768]{1,0:T(8,128)S(1)}, u32[]{:S(2)}, u32[]{:S(2)}) collective-permute-start(f32[32,768]{1,0:T(8,128)S(1)} %add_add_fusion.refs_0_), channel_id=1, source_target_pairs={{0,16},{1,17},{2,18},{3,19},{4,20},{5,21},{6,22},{7,23},{8,24},{9,... | collective-permute-start | bytes 294920 | tf_op jit(solution)/shard_map/ppermute | solution.py:322
  111.8 19.0 %collective-permute-start.2 = (f32[4,144,128]{2,1,0:T(8,128)S(1)}, f32[4,144,128]{2,1,0:T(8,128)S(1)}, u32[]{:S(2)}, u32[]{:S(2)}) collective-permute-start(f32[4,144,128]{2,1,0:T(8,128)S(1)} %get-tuple-element.47), channel_id=1, source_target_pairs={{0,64},{1,65},{2,66},{3,67},{4,68},{5,69},{6,70},{7,71},{8,72},{9,... | collective-permute-start | bytes 884744 | tf_op jit(solution)/shard_map/ppermute | solution.py:322
  113.1 17.8 %collective-permute-start.3 = (f32[4,144,128]{2,1,0:T(8,128)S(1)}, f32[4,144,128]{2,1,0:T(8,128)S(1)}, u32[]{:S(2)}, u32[]{:S(2)}) collective-permute-start(f32[4,144,128]{2,1,0:T(8,128)S(1)} %get-tuple-element.48), channel_id=1, source_target_pairs={{0,128},{1,129},{2,130},{3,131},{4,132},{5,133},{6,134},{7,135},{8... | collective-permute-start | bytes 884744 | tf_op jit(solution)/shard_map/ppermute | solution.py:322
  116.2 14.7 %collective-permute-start.4 = (f32[4,144,128]{2,1,0:T(8,128)S(1)}, f32[4,144,128]{2,1,0:T(8,128)S(1)}, u32[]{:S(2)}, u32[]{:S(2)}) collective-permute-start(f32[4,144,128]{2,1,0:T(8,128)S(1)} %get-tuple-element.49), channel_id=1, source_target_pairs={{0,192},{1,193},{2,194},{3,195},{4,196},{5,197},{6,198},{7,199},{8... | collective-permute-start | bytes 884744 | tf_op jit(solution)/shard_map/ppermute | solution.py:322
  116.8 12.1 %collective-permute-start.27 = (f32[32,768]{1,0:T(8,128)S(1)}, f32[32,768]{1,0:T(8,128)S(1)}, u32[]{:S(2)}, u32[]{:S(2)}) collective-permute-start(f32[32,768]{1,0:T(8,128)S(1)} %add_add_fusion.refs_0_), channel_id=1, source_target_pairs={{0,32},{1,33},{2,34},{3,35},{4,36},{5,37},{6,38},{7,39},{8,40},{9,... | collective-permute-start | bytes 294920 | tf_op jit(solution)/shard_map/ppermute | solution.py:322
  128.9 21.8 %collective-permute-start.29 = (f32[4,32,768]{2,1,0:T(8,128)S(1)}, f32[4,32,768]{2,1,0:T(8,128)S(1)}, u32[]{:S(2)}, u32[]{:S(2)}) collective-permute-start(f32[4,32,768]{2,1,0:T(8,128)S(1)} %shard_map.132.refs_0_), channel_id=1, source_target_pairs={{0,64},{1,65},{2,66},{3,67},{4,68},{5,69},{6,70},{7,71},{8,72},{9,... | collective-permute-start | bytes 1179656 | tf_op jit(solution)/shard_map/ppermute | solution.py:322
  130.8 19.8 %collective-permute-start.30 = (f32[4,32,768]{2,1,0:T(8,128)S(1)}, f32[4,32,768]{2,1,0:T(8,128)S(1)}, u32[]{:S(2)}, u32[]{:S(2)}) collective-permute-start(f32[4,32,768]{2,1,0:T(8,128)S(1)} %shard_map.132.refs_0_), channel_id=1, source_target_pairs={{0,128},{1,129},{2,130},{3,131},{4,132},{5,133},{6,134},{7,135},{8... | collective-permute-start | bytes 1179656 | tf_op jit(solution)/shard_map/ppermute | solution.py:322
  137.7 29.6 %collective-permute-start.31 = (f32[4,32,768]{2,1,0:T(8,128)S(1)}, f32[4,32,768]{2,1,0:T(8,128)S(1)}, u32[]{:S(2)}, u32[]{:S(2)}) collective-permute-start(f32[4,32,768]{2,1,0:T(8,128)S(1)} %shard_map.132.refs_0_), channel_id=1, source_target_pairs={{0,192},{1,193},{2,194},{3,195},{4,196},{5,197},{6,198},{7,199},{8... | collective-permute-start | bytes 1179656 | tf_op jit(solution)/shard_map/ppermute | solution.py:322
  140.1 29.4 %collective-permute-start.32 = (f32[4,32,768]{2,1,0:T(8,128)S(1)}, f32[4,32,768]{2,1,0:T(8,128)S(1)}, u32[]{:S(2)}, u32[]{:S(2)}) collective-permute-start(f32[4,32,768]{2,1,0:T(8,128)S(1)} %shard_map.132.refs_0_), channel_id=1, source_target_pairs={{0,8},{1,9},{2,10},{3,11},{4,12},{5,13},{6,14},{7,15},{8,0},{9,1},... | collective-permute-start | bytes 1179656 | tf_op jit(solution)/shard_map/ppermute | solution.py:322
  150.6 21.4 %collective-permute-start.33 = (f32[4,32,768]{2,1,0:T(8,128)S(1)}, f32[4,32,768]{2,1,0:T(8,128)S(1)}, u32[]{:S(2)}, u32[]{:S(2)}) collective-permute-start(f32[4,32,768]{2,1,0:T(8,128)S(1)} %collective-permute-done.29.refs_1_), channel_id=1, source_target_pairs={{0,8},{1,9},{2,10},{3,11},{4,12},{5,13},{6,14},{7,15},{8,0},{9,1},... | collective-permute-start | bytes 1179656 | tf_op jit(solution)/shard_map/ppermute | solution.py:322
  160.8 11.3 %collective-permute-start.34 = (f32[4,32,768]{2,1,0:T(8,128)S(1)}, f32[4,32,768]{2,1,0:T(8,128)S(1)}, u32[]{:S(2)}, u32[]{:S(2)}) collective-permute-start(f32[4,32,768]{2,1,0:T(8,128)S(1)} %collective-permute-done.30.refs_2_), channel_id=1, source_target_pairs={{0,8},{1,9},{2,10},{3,11},{4,12},{5,13},{6,14},{7,15},{8,0},{9,1},... | collective-permute-start | bytes 1179656 | tf_op jit(solution)/shard_map/ppermute | solution.py:322
  167.3 15.7 %collective-permute-start.14 = (f32[4,144,128]{2,1,0:T(8,128)S(1)}, f32[4,144,128]{2,1,0:T(8,128)S(1)}, u32[]{:S(2)}, u32[]{:S(2)}) collective-permute-start(f32[4,144,128]{2,1,0:T(8,128)S(1)} %pad_maximum_fusion.refs_0_), channel_id=1, source_target_pairs={{0,128},{1,129},{2,130},{3,131},{4,132},{5,133},{6,134},{7,135},{8... | collective-permute-start | bytes 884744 | tf_op jit(solution)/shard_map/ppermute | solution.py:322
  169.5 13.4 %collective-permute-start.16 = (f32[4,144,128]{2,1,0:T(8,128)S(1)}, f32[4,144,128]{2,1,0:T(8,128)S(1)}, u32[]{:S(2)}, u32[]{:S(2)}) collective-permute-start(f32[4,144,128]{2,1,0:T(8,128)S(1)} %pad_maximum_fusion.refs_0_), channel_id=1, source_target_pairs={{0,192},{1,193},{2,194},{3,195},{4,196},{5,197},{6,198},{7,199},{8... | collective-permute-start | bytes 884744 | tf_op jit(solution)/shard_map/ppermute | solution.py:322
  172.1 11.4 %collective-permute-start.35 = (f32[4,32,768]{2,1,0:T(8,128)S(1)}, f32[4,32,768]{2,1,0:T(8,128)S(1)}, u32[]{:S(2)}, u32[]{:S(2)}) collective-permute-start(f32[4,32,768]{2,1,0:T(8,128)S(1)} %collective-permute-done.31.refs_3_), channel_id=1, source_target_pairs={{0,8},{1,9},{2,10},{3,11},{4,12},{5,13},{6,14},{7,15},{8,0},{9,1},... | collective-permute-start | bytes 1179656 | tf_op jit(solution)/shard_map/ppermute | solution.py:322
  172.1 15.6 %collective-permute-start.11 = (f32[4,144,128]{2,1,0:T(8,128)S(1)}, f32[4,144,128]{2,1,0:T(8,128)S(1)}, u32[]{:S(2)}, u32[]{:S(2)}) collective-permute-start(f32[4,144,128]{2,1,0:T(8,128)S(1)} %pad_maximum_fusion.refs_0_), channel_id=1, source_target_pairs={{0,8},{1,9},{2,10},{3,11},{4,12},{5,13},{6,14},{7,15},{8,0},{9,1},... | collective-permute-start | bytes 884744 | tf_op jit(solution)/shard_map/ppermute | solution.py:322
  175.5 12.2 %collective-permute-start.13 = (f32[4,144,128]{2,1,0:T(8,128)S(1)}, f32[4,144,128]{2,1,0:T(8,128)S(1)}, u32[]{:S(2)}, u32[]{:S(2)}) collective-permute-start(f32[4,144,128]{2,1,0:T(8,128)S(1)} %collective-permute-done.12.refs_1_), channel_id=1, source_target_pairs={{0,8},{1,9},{2,10},{3,11},{4,12},{5,13},{6,14},{7,15},{8,0},{9,1},... | collective-permute-start | bytes 884744 | tf_op jit(solution)/shard_map/ppermute | solution.py:322
  (21 other events, 259.5 us)

commit v3 on v2

--- a/solution.py
+++ b/solution.py
@@ -118,11 +118,12 @@
         out[k, 128:, :] = total[128:]
 
 
-def norm_grad_kernel(at, parts, normed, inv, table, out):
+def norm_grad_kernel(at, parts, normed, inv, cos_part, sin_part, out):
     total = jnp.sum(parts[...], axis=0)
     rows = pl.ds(pl.multiple_of(at[3] * 32, 32), 32)
     rest = jnp.concatenate([total[128:], pltpu.roll(total[128:], 64, 1)], axis=0)
-    rest = rest * table[rows, 256:384] - swap(rest) * table[rows, 384:512]
+    cos, sin = part_table(cos_part[rows, :], sin_part[rows, :])
+    rest = rest * cos - swap(rest) * sin
     rest = pack_rest(rest[:16], rest[16:])
     grad = total[:128]
     product = grad * normed[...]
@@ -137,7 +138,17 @@
         out[k, 128:, :] = rest
 
 
-def seen(seg_col, seg_row):
+def full_table(cos, sin):
+    return jnp.concatenate([cos, cos], axis=1), jnp.concatenate([-sin, sin], axis=1)
+
+
+def part_table(cos, sin):
+    one, zero = jnp.ones((cos.shape[0], 64), F32), jnp.zeros((cos.shape[0], 64), F32)
+    return jnp.concatenate([cos, cos, one], axis=1), jnp.concatenate([-sin, sin, zero], axis=1)
+
+
+def seen(seg_row):
+    seg_col = jnp.broadcast_to(seg_row, (8, SEQ)).T[:, :1]
     i = lax.broadcasted_iota(jnp.int32, (SEQ, SEQ), 0)
     j = lax.broadcasted_iota(jnp.int32, (SEQ, SEQ), 1)
     return (seg_col == seg_row) & (j <= i)
@@ -154,10 +165,10 @@
 
 
 def teacher_kernel(
-    at, queries, keys, values, table, seg_col, seg_row, tokens, out, tokens_keep, tokens_send
+    at, queries, keys, values, cos_full, sin_full, segments, tokens, out, tokens_keep, tokens_send
 ):
-    mask = seen(seg_col[...], seg_row[...])
-    cos, sin = table[:, :128], table[:, 128:256]
+    mask = seen(segments[...])
+    cos, sin = full_table(cos_full[...], sin_full[...])
     turn = lambda v: (v * cos + pltpu.roll(v, 64, 1) * sin).astype(BF16)
     key = turn(keys[...].astype(F32))
     value = values[...]
@@ -176,17 +187,17 @@
 
 
 def student_kernel(
-    at, packed, queries, key_up, value_up, teacher, table, seg_col, seg_row,
+    at, packed, queries, key_up, value_up, teacher, cos_part, sin_part, segments,
     grads_keep, grads_send, norm_out, latent, rest, nope, head_values, rest_sum, grads_out,
 ):
     unpack(packed, latent, rest)
-    cos, sin = table[:, 256:384], table[:, 384:512]
+    cos, sin = part_table(cos_part[...], sin_part[...])
     low = low_lanes(SEQ)
     turn = lambda v: v * cos + swap(v) * sin
     rope_key = turn(rest[...])
     nope[...] = dot(latent[...], key_up[...])
     head_values[...] = dot(latent[...], value_up[...]).astype(BF16)
-    mask = seen(seg_col[...], seg_row[...])
+    mask = seen(segments[...])
     scale = 1.0 / math.sqrt(HEAD)
     rest_sum[...] = jnp.zeros_like(rest_sum)
 
@@ -346,29 +357,24 @@
         return position[:, None] * jnp.exp(-exponent * jnp.log(F32(THETA)))[None, :]
 
     full, part = angles(HEAD), angles(ROPE)
-    cos, sin = jnp.cos(full), jnp.sin(full)
-    cos_part, sin_part = jnp.cos(part), jnp.sin(part)
-    one, zero = jnp.ones((SEQ, 64), F32), jnp.zeros((SEQ, 64), F32)
-    return jnp.concatenate(
-        [cos, cos, -sin, sin, cos_part, cos_part, one, -sin_part, sin_part, zero], axis=1
-    )
+    return (jnp.cos(full), jnp.sin(full)), (jnp.cos(part), jnp.sin(part))
 
 
 def local(tokens, segment_ids, queries, keys, values, down, rope, key_up, value_up):
     tokens, segments, queries = tokens[0], segment_ids[0], queries[0]
     d = lax.axis_index("dp")
     at = jnp.stack([d % 2, d // 8, d // 2 % 4, lax.axis_index("tensor")])
-    seg_col, seg_row = segments[:, None], segments[None, :]
+    seg_row = segments[None, :]
     chunks = shape(8, PACKED, 128)
     unpacked = [pltpu.VMEM((SEQ, LATENT), BF16), pltpu.VMEM((SEQ, 128), F32)]
 
     (part,) = call(entry_kernel, [chunks], tokens, down, rope, flops=2 * 256 * 1024 * 576, mib=60)
     parts = exchange(part)
-    table = tables(segments)
+    full, partial = tables(segments)
     teacher, tokens_keep, tokens_send = call(
         teacher_kernel,
         [shape(SEQ, 1024), shape(512, SEQ, dtype=BF16), shape(512, SEQ)],
-        at, queries, keys[0], values[0], table, seg_col, seg_row, tokens,
+        at, queries, keys[0], values[0], *full, seg_row, tokens,
         scalars=1, flops=4 * 8 * 256 * 256 * 128, mib=60,
     )
     tokens_other = other_core(tokens_send)
@@ -379,7 +385,7 @@
     grads_keep, grads_send, part = call(
         student_kernel,
         [shape(SEQ, 768, dtype=BF16), shape(SEQ, 768), chunks],
-        at, packed, queries, key_up, value_up, teacher, table, seg_col, seg_row,
+        at, packed, queries, key_up, value_up, teacher, *partial, seg_row,
         scalars=1,
         scratch=unpacked + [
             pltpu.VMEM((SEQ, 512), F32),
@@ -393,10 +399,10 @@
     parts = exchange(part)
     quarters = call(
         up_kernel, [shape(128, 768)] * 4, at, packed, packed_other, grads_keep, grads_other,
-        scalars=1, scratch=unpacked, flops=2 * 512 * 512 * 768,
+        scalars=1, scratch=unpacked, flops=2 * 512 * 512 * 768, mib=60,
     )
     received = around(list(quarters[1:]), "x")
-    (replicas,) = call(norm_grad_kernel, [chunks], at, parts, normed, inv, table, scalars=1)
+    (replicas,) = call(norm_grad_kernel, [chunks], at, parts, normed, inv, *partial, scalars=1)
     packed = exchange(replicas)
     packed_other = other_core(packed)
     quarters = call(split_kernel, [shape(32, 768)] * 4, at, quarters[0], *received, scalars=1)

time: 191 us -> 195 us (1.021)
  blocking collectives: 27.6 us -> 13 us
  waiting for transfers between devices: 53.6 us -> 62.2 us
  starting transfers between devices: 70.1 us -> 75.3 us
  Pallas kernels: 33.4 us -> 35.7 us
    all_to_all x2 -> x1, blocking collectives: 27.6 us -> 13 us  [exchange(): return lax.all_to_all(parts, 'tensor', 0, 0, tiled=True)]
    all_to_all x2 -> x3, waiting for transfers between devices: 0.01 us -> 8.53 us  [exchange(): return lax.all_to_all(parts, 'tensor', 0, 0, tiled=True)]
    all_to_all x2 -> x3, starting transfers between devices: 10.7 us -> 15.8 us  [exchange(): return lax.all_to_all(parts, 'tensor', 0, 0, tiled=True)]
    unnamed x14 -> x24, local copies, waits for them, and re-layouts: 0.03 us -> 2.91 us
    pallas_call x14, Pallas kernels: 33.4 us -> 35.7 us  [call(): pl.pallas_call(body, out_shape=outs, in_specs=specs, out_specs=[anywhere...]
  transfers between devices with their start and end apart: 38 -> 39, of which waited for: 13 -> 15; matrix products, arithmetic and copies ran while one was open for 2% -> 2% of each run, Pallas kernels for 8% -> 9%
where the time goes in v3:
time: 195 us; the launch traced here: 193 us
  starting transfers between devices  75.3 us (39%)
  waiting for transfers between devices  62.2 us (32%)
  Pallas kernels  35.7 us (18%)
  blocking collectives  13 us (7%)
  other arithmetic  3.37 us (2%)
  local copies, waits for them, and re-layouts  2.91 us (1%)
    ppermute x36, starting transfers between devices, permute(): return lax.ppermute(value, AXES, pairs)  59.6 us
    ppermute x36, waiting for transfers between devices, permute(): return lax.ppermute(value, AXES, pairs)  53.6 us
    pallas_call x14, Pallas kernels, call(): pl.pallas_call(body, out_shape=outs, in_specs=specs, out_specs=[anywhere...  35.7 us
    all_to_all x3, starting transfers between devices, exchange(): return lax.all_to_all(parts, 'tensor', 0, 0, tiled=True)  15.8 us
    all_to_all x1, blocking collectives, exchange(): return lax.all_to_all(parts, 'tensor', 0, 0, tiled=True)  13 us
    all_to_all x3, waiting for transfers between devices, exchange(): return lax.all_to_all(parts, 'tensor', 0, 0, tiled=True)  8.53 us
  transfers between devices with their start and end apart: 39, of which 15 were waited for; matrix products, arithmetic and copies ran while one was open for 2% of the time, Pallas kernels for 9%

profile of v3, /device:TPU:32, one launch (start us, length us, event | category | flops | bytes accessed | tf_op | source)
XLA Modules:
  0.0 193.4 jit_solution(600171974935288424)
XLA Ops:
  0.6 2.8 %shard_map.120 = f32[8,144,128]{2,1,0:T(8,128)} custom-call(bf16[256,1024]{1,0:T(8,128)(2,1)} %bitcast.16, bf16[1024,512]{1,0:T(8,128)(2,1)} %down.1, bf16[64,1024]{1,0:T(8,128)(2,1)} %rope.1), custom_call_target="tpu_custom_call" | custom-call | flops 301989888 | bytes 2293760 | tf_op jit(solution)/shard_map/pallas_call | solution.py:48
  3.5 5.9 %all-to-all-start = ((f32[8,144,128]{2,1,0:T(8,128)}), f32[8,144,128]{2,1,0:T(8,128)S(1)}, u32[]{:S(2)}, u32[]{:S(2)}) async-start(f32[8,144,128]{2,1,0:T(8,128)} %shard_map.120), calls=%async_computation | async-start | bytes 1179648 | tf_op jit(solution)/shard_map/all_to_all | solution.py:347
  11.5 6.8 %shard_map.121 = (f32[256,1024]{1,0:T(8,128)}, bf16[512,256]{1,0:T(8,128)(2,1)}, f32[512,256]{1,0:T(8,128)}) custom-call(s32[4]{0:T(128)} %pad_add_fusion.at, bf16[256,1024]{1,0:T(8,128)(2,1)} %bitcast.14, bf16[256,128]{1,0:T(8,128)(2,1)} %bitcast.21, bf16[256,128]{1,0:T(8,128)(2,1)} %bitcast.22, f32[256,64]{1,0:T(8,128)} %get-tuple-element.73.cos_full, ...), custom_call_target="tpu_custom_call" | custom-call | flops 268435456 | bytes 3146768 | tf_op jit(solution)/shard_map/pallas_call | solution.py:48
  20.0 5.0 %all-to-all-start.1 = ((f32[8,144,128]{2,1,0:T(8,128)}), f32[8,144,128]{2,1,0:T(8,128)S(1)}, u32[]{:S(2)}, u32[]{:S(2)}) async-start(f32[8,144,128]{2,1,0:T(8,128)} %get-tuple-element.39), calls=%async_computation.1 | async-start | bytes 1179648 | tf_op jit(solution)/shard_map/all_to_all | solution.py:347
  26.2 7.8 %all-to-all-done.1.packed = f32[8,144,128]{2,1,0:T(8,128)S(1)} async-done(((f32[8,144,128]{2,1,0:T(8,128)}), f32[8,144,128]{2,1,0:T(8,128)S(1)}, u32[]{:S(2)}, u32[]{:S(2)}) %all-to-all-start.1) | async-done | bytes 589856 | tf_op jit(solution)/shard_map/all_to_all | solution.py:347
  34.9 11.2 %shard_map.123 = (bf16[256,768]{1,0:T(8,128)(2,1)}, f32[256,768]{1,0:T(8,128)}, f32[8,144,128]{2,1,0:T(8,128)}) custom-call(s32[4]{0:T(128)} %pad_add_fusion.at, f32[8,144,128]{2,1,0:T(8,128)} %copy-done.6, bf16[256,1024]{1,0:T(8,128)(2,1)} %bitcast.15, bf16[512,512]{1,0:T(8,128)(2,1)} %key_up.1, bf16[512,1024]{1,0:T(8,128)(2,1)} %value_up.1, ...), custom_call_target="tpu_custom_call" | custom-call | flops 671088640 | bytes 5571600 | tf_op jit(solution)/shard_map/pallas_call | solution.py:48
  46.1 13.0 %all_to_all.20.parts = f32[8,144,128]{2,1,0:T(8,128)S(1)} all-to-all(f32[8,144,128]{2,1,0:T(8,128)} %get-tuple-element.41), channel_id=1, replica_groups=mesh['dp'=32,'tensor'=8] {'tensor'}, dimensions={0} | all-to-all | bytes 1179648 | tf_op jit(solution)/shard_map/all_to_all | solution.py:347
  60.6 4.9 %all-to-all-start.3 = ((f32[8,144,128]{2,1,0:T(8,128)}), f32[8,144,128]{2,1,0:T(8,128)S(1)}, u32[]{:S(2)}, u32[]{:S(2)}) async-start(f32[8,144,128]{2,1,0:T(8,128)} %shard_map.124), calls=%async_computation.3 | async-start | bytes 1179648 | tf_op jit(solution)/shard_map/all_to_all | solution.py:347
  69.7 3.7 %shard_map.130 = (f32[128,768]{1,0:T(8,128)}, f32[128,768]{1,0:T(8,128)}, f32[128,768]{1,0:T(8,128)}, f32[128,768]{1,0:T(8,128)}) custom-call(s32[4]{0:T(128)} %pad_add_fusion.at, f32[8,144,128]{2,1,0:T(8,128)} %copy-done.6, f32[8,144,128]{2,1,0:T(8,128)} %copy-done.9, bf16[256,768]{1,0:T(8,128)(2,1)} %get-tuple-element.58.grads, f32[256,768]{1,0:T(8,128)} %copy-done.8), custom_call_target="tpu_custom_call" | custom-call | flops 402653184 | bytes 3932176 | tf_op jit(solution)/shard_map/pallas_call | solution.py:48
  79.6 6.4 %collective-permute-done.20.first = f32[128,768]{1,0:T(8,128)S(1)} collective-permute-done((f32[128,768]{1,0:T(8,128)}, f32[128,768]{1,0:T(8,128)S(1)}, u32[]{:S(2)}, u32[]{:S(2)}) %collective-permute-start.20) | collective-permute-done | bytes 393248 | tf_op jit(solution)/shard_map/ppermute | solution.py:333
  86.0 9.4 %collective-permute-done.21.second = f32[128,768]{1,0:T(8,128)S(1)} collective-permute-done((f32[128,768]{1,0:T(8,128)}, f32[128,768]{1,0:T(8,128)S(1)}, u32[]{:S(2)}, u32[]{:S(2)}) %collective-permute-start.21) | collective-permute-done | bytes 393248 | tf_op jit(solution)/shard_map/ppermute | solution.py:333
  97.1 6.4 %collective-permute-start.24 = (f32[32,768]{1,0:T(8,128)S(1)}, f32[32,768]{1,0:T(8,128)S(1)}, u32[]{:S(2)}, u32[]{:S(2)}) collective-permute-start(f32[32,768]{1,0:T(8,128)S(1)} %get-tuple-element.66), channel_id=1, source_target_pairs={{0,32},{1,33},{2,34},{3,35},{4,36},{5,37},{6,38},{7,39},{8,40},{9,... | collective-permute-start | bytes 294920 | tf_op jit(solution)/shard_map/ppermute | solution.py:333
  106.4 2.9 %collective-permute-done.24 = f32[32,768]{1,0:T(8,128)S(1)} collective-permute-done((f32[32,768]{1,0:T(8,128)S(1)}, f32[32,768]{1,0:T(8,128)S(1)}, u32[]{:S(2)}, u32[]{:S(2)}) %collective-permute-start.24) | collective-permute-done | bytes 98336 | tf_op jit(solution)/shard_map/ppermute | solution.py:333
  116.9 3.1 %collective-permute-start.3 = (f32[4,144,128]{2,1,0:T(8,128)S(1)}, f32[4,144,128]{2,1,0:T(8,128)S(1)}, u32[]{:S(2)}, u32[]{:S(2)}) collective-permute-start(f32[4,144,128]{2,1,0:T(8,128)S(1)} %get-tuple-element.48), channel_id=1, source_target_pairs={{0,128},{1,129},{2,130},{3,131},{4,132},{5,133},{6,134},{7,135},{8... | collective-permute-start | bytes 884744 | tf_op jit(solution)/shard_map/ppermute | solution.py:333
  120.6 4.1 %collective-permute-start.27 = (f32[32,768]{1,0:T(8,128)S(1)}, f32[32,768]{1,0:T(8,128)S(1)}, u32[]{:S(2)}, u32[]{:S(2)}) collective-permute-start(f32[32,768]{1,0:T(8,128)S(1)} %add_add_fusion.refs_0_), channel_id=1, source_target_pairs={{0,32},{1,33},{2,34},{3,35},{4,36},{5,37},{6,38},{7,39},{8,40},{9,... | collective-permute-start | bytes 294920 | tf_op jit(solution)/shard_map/ppermute | solution.py:333
  127.1 5.6 %collective-permute-done.27.refs_2_ = f32[32,768]{1,0:T(8,128)S(1)} collective-permute-done((f32[32,768]{1,0:T(8,128)S(1)}, f32[32,768]{1,0:T(8,128)S(1)}, u32[]{:S(2)}, u32[]{:S(2)}) %collective-permute-start.27) | collective-permute-done | bytes 98336 | tf_op jit(solution)/shard_map/ppermute | solution.py:333
  135.3 2.9 %collective-permute-start.5 = (f32[144,128]{1,0:T(8,128)S(1)}, f32[144,128]{1,0:T(8,128)S(1)}, u32[]{:S(2)}, u32[]{:S(2)}) collective-permute-start(f32[144,128]{1,0:T(8,128)S(1)} %get-tuple-element.51), channel_id=1, source_target_pairs={{0,16},{1,17},{2,18},{3,19},{4,20},{5,21},{6,22},{7,23},{8,24},{9,... | collective-permute-start | bytes 221192 | tf_op jit(solution)/shard_map/ppermute | solution.py:333
  138.2 3.3 %collective-permute-start.6 = (f32[144,128]{1,0:T(8,128)S(1)}, f32[144,128]{1,0:T(8,128)S(1)}, u32[]{:S(2)}, u32[]{:S(2)}) collective-permute-start(f32[144,128]{1,0:T(8,128)S(1)} %get-tuple-element.52), channel_id=1, source_target_pairs={{0,32},{1,33},{2,34},{3,35},{4,36},{5,37},{6,38},{7,39},{8,40},{9,... | collective-permute-start | bytes 221192 | tf_op jit(solution)/shard_map/ppermute | solution.py:333
  147.8 3.9 %collective-permute-done.7.third = f32[144,128]{1,0:T(8,128)S(1)} collective-permute-done((f32[144,128]{1,0:T(8,128)S(1)}, f32[144,128]{1,0:T(8,128)S(1)}, u32[]{:S(2)}, u32[]{:S(2)}) %collective-permute-start.7) | collective-permute-done | bytes 73760 | tf_op jit(solution)/shard_map/ppermute | solution.py:333
  154.5 4.5 %collective-permute-start.9 = (f32[144,128]{1,0:T(8,128)S(1)}, f32[144,128]{1,0:T(8,128)S(1)}, u32[]{:S(2)}, u32[]{:S(2)}) collective-permute-start(f32[144,128]{1,0:T(8,128)S(1)} %shard_map.127), channel_id=1, source_target_pairs={{0,32},{1,33},{2,34},{3,35},{4,36},{5,37},{6,38},{7,39},{8,40},{9,... | collective-permute-start | bytes 221192 | tf_op jit(solution)/shard_map/ppermute | solution.py:333
  161.6 3.1 %collective-permute-done.9 = f32[144,128]{1,0:T(8,128)S(1)} collective-permute-done((f32[144,128]{1,0:T(8,128)S(1)}, f32[144,128]{1,0:T(8,128)S(1)}, u32[]{:S(2)}, u32[]{:S(2)}) %collective-permute-start.9) | collective-permute-done | bytes 73760 | tf_op jit(solution)/shard_map/ppermute | solution.py:333
  164.7 4.4 %collective-permute-done.8 = f32[144,128]{1,0:T(8,128)S(1)} collective-permute-done((f32[144,128]{1,0:T(8,128)S(1)}, f32[144,128]{1,0:T(8,128)S(1)}, u32[]{:S(2)}, u32[]{:S(2)}) %collective-permute-start.8) | collective-permute-done | bytes 73760 | tf_op jit(solution)/shard_map/ppermute | solution.py:333
  176.3 3.0 %collective-permute-done.12.refs_1_ = f32[4,144,128]{2,1,0:T(8,128)S(1)} collective-permute-done((f32[4,144,128]{2,1,0:T(8,128)S(1)}, f32[4,144,128]{2,1,0:T(8,128)S(1)}, u32[]{:S(2)}, u32[]{:S(2)}) %collective-permute-start.12) | collective-permute-done | bytes 294944 | tf_op jit(solution)/shard_map/ppermute | solution.py:333
  179.3 7.4 %collective-permute-done.14.refs_2_ = f32[4,144,128]{2,1,0:T(8,128)S(1)} collective-permute-done((f32[4,144,128]{2,1,0:T(8,128)S(1)}, f32[4,144,128]{2,1,0:T(8,128)S(1)}, u32[]{:S(2)}, u32[]{:S(2)}) %collective-permute-start.14) | collective-permute-done | bytes 294944 | tf_op jit(solution)/shard_map/ppermute | solution.py:333
  (102 shorter events, 61.0 us)
Async XLA Ops:
  3.5 15.5 %all-to-all-start = ((f32[8,144,128]{2,1,0:T(8,128)}), f32[8,144,128]{2,1,0:T(8,128)S(1)}, u32[]{:S(2)}, u32[]{:S(2)}) async-start(f32[8,144,128]{2,1,0:T(8,128)} %shard_map.120), calls=%async_computation | async-start | bytes 1179648 | tf_op jit(solution)/shard_map/all_to_all | solution.py:347
  20.0 14.1 %all-to-all-start.1 = ((f32[8,144,128]{2,1,0:T(8,128)}), f32[8,144,128]{2,1,0:T(8,128)S(1)}, u32[]{:S(2)}, u32[]{:S(2)}) async-start(f32[8,144,128]{2,1,0:T(8,128)} %get-tuple-element.39), calls=%async_computation.1 | async-start | bytes 1179648 | tf_op jit(solution)/shard_map/all_to_all | solution.py:347
  60.6 18.5 %all-to-all-start.3 = ((f32[8,144,128]{2,1,0:T(8,128)}), f32[8,144,128]{2,1,0:T(8,128)S(1)}, u32[]{:S(2)}, u32[]{:S(2)}) async-start(f32[8,144,128]{2,1,0:T(8,128)} %shard_map.124), calls=%async_computation.3 | async-start | bytes 1179648 | tf_op jit(solution)/shard_map/all_to_all | solution.py:347
  73.4 12.6 %collective-permute-start.20 = (f32[128,768]{1,0:T(8,128)}, f32[128,768]{1,0:T(8,128)S(1)}, u32[]{:S(2)}, u32[]{:S(2)}) collective-permute-start(f32[128,768]{1,0:T(8,128)} %get-tuple-element.61), channel_id=1, source_target_pairs={{0,64},{1,65},{2,66},{3,67},{4,68},{5,69},{6,70},{7,71},{8,72},{9,... | collective-permute-start | bytes 1179656 | tf_op jit(solution)/shard_map/ppermute | solution.py:333
  74.9 20.5 %collective-permute-start.21 = (f32[128,768]{1,0:T(8,128)}, f32[128,768]{1,0:T(8,128)S(1)}, u32[]{:S(2)}, u32[]{:S(2)}) collective-permute-start(f32[128,768]{1,0:T(8,128)} %get-tuple-element.62), channel_id=1, source_target_pairs={{0,128},{1,129},{2,130},{3,131},{4,132},{5,133},{6,134},{7,135},{8... | collective-permute-start | bytes 1179656 | tf_op jit(solution)/shard_map/ppermute | solution.py:333
  77.7 17.8 %collective-permute-start.22 = (f32[128,768]{1,0:T(8,128)}, f32[128,768]{1,0:T(8,128)S(1)}, u32[]{:S(2)}, u32[]{:S(2)}) collective-permute-start(f32[128,768]{1,0:T(8,128)} %get-tuple-element.63), channel_id=1, source_target_pairs={{0,192},{1,193},{2,194},{3,195},{4,196},{5,197},{6,198},{7,199},{8... | collective-permute-start | bytes 1179656 | tf_op jit(solution)/shard_map/ppermute | solution.py:333
  79.1 35.1 %collective-permute-start = (f32[8,144,128]{2,1,0:T(8,128)S(1)}, f32[8,144,128]{2,1,0:T(8,128)S(1)}, u32[]{:S(2)}, u32[]{:S(2)}) collective-permute-start(f32[8,144,128]{2,1,0:T(8,128)S(1)} %all-to-all-done.3.packed), channel_id=1, source_target_pairs={{0,8},{1,9},{2,10},{3,11},{4,12},{5,13},{6,14},{7,15},{8,0},{9,1},... | collective-permute-start | bytes 1769480 | tf_op jit(solution)/shard_map/ppermute | solution.py:333
  79.1 35.1 %collective-permute-start.1 = (f32[512,256]{1,0:T(8,128)}, f32[512,256]{1,0:T(8,128)S(1)}, u32[]{:S(2)}, u32[]{:S(2)}) collective-permute-start(f32[512,256]{1,0:T(8,128)} %get-tuple-element.45), channel_id=1, source_target_pairs={{0,8},{1,9},{2,10},{3,11},{4,12},{5,13},{6,14},{7,15},{8,0},{9,1},... | collective-permute-start | bytes 1572872 | tf_op jit(solution)/shard_map/ppermute | solution.py:333
  97.1 12.2 %collective-permute-start.24 = (f32[32,768]{1,0:T(8,128)S(1)}, f32[32,768]{1,0:T(8,128)S(1)}, u32[]{:S(2)}, u32[]{:S(2)}) collective-permute-start(f32[32,768]{1,0:T(8,128)S(1)} %get-tuple-element.66), channel_id=1, source_target_pairs={{0,32},{1,33},{2,34},{3,35},{4,36},{5,37},{6,38},{7,39},{8,40},{9,... | collective-permute-start | bytes 294920 | tf_op jit(solution)/shard_map/ppermute | solution.py:333
  111.8 12.9 %collective-permute-start.26 = (f32[32,768]{1,0:T(8,128)S(1)}, f32[32,768]{1,0:T(8,128)S(1)}, u32[]{:S(2)}, u32[]{:S(2)}) collective-permute-start(f32[32,768]{1,0:T(8,128)S(1)} %add_add_fusion.refs_0_), channel_id=1, source_target_pairs={{0,16},{1,17},{2,18},{3,19},{4,20},{5,21},{6,22},{7,23},{8,24},{9,... | collective-permute-start | bytes 294920 | tf_op jit(solution)/shard_map/ppermute | solution.py:333
  115.5 19.2 %collective-permute-start.2 = (f32[4,144,128]{2,1,0:T(8,128)S(1)}, f32[4,144,128]{2,1,0:T(8,128)S(1)}, u32[]{:S(2)}, u32[]{:S(2)}) collective-permute-start(f32[4,144,128]{2,1,0:T(8,128)S(1)} %get-tuple-element.47), channel_id=1, source_target_pairs={{0,64},{1,65},{2,66},{3,67},{4,68},{5,69},{6,70},{7,71},{8,72},{9,... | collective-permute-start | bytes 884744 | tf_op jit(solution)/shard_map/ppermute | solution.py:333
  116.9 17.8 %collective-permute-start.3 = (f32[4,144,128]{2,1,0:T(8,128)S(1)}, f32[4,144,128]{2,1,0:T(8,128)S(1)}, u32[]{:S(2)}, u32[]{:S(2)}) collective-permute-start(f32[4,144,128]{2,1,0:T(8,128)S(1)} %get-tuple-element.48), channel_id=1, source_target_pairs={{0,128},{1,129},{2,130},{3,131},{4,132},{5,133},{6,134},{7,135},{8... | collective-permute-start | bytes 884744 | tf_op jit(solution)/shard_map/ppermute | solution.py:333
  120.0 14.7 %collective-permute-start.4 = (f32[4,144,128]{2,1,0:T(8,128)S(1)}, f32[4,144,128]{2,1,0:T(8,128)S(1)}, u32[]{:S(2)}, u32[]{:S(2)}) collective-permute-start(f32[4,144,128]{2,1,0:T(8,128)S(1)} %get-tuple-element.49), channel_id=1, source_target_pairs={{0,192},{1,193},{2,194},{3,195},{4,196},{5,197},{6,198},{7,199},{8... | collective-permute-start | bytes 884744 | tf_op jit(solution)/shard_map/ppermute | solution.py:333
  120.6 12.1 %collective-permute-start.27 = (f32[32,768]{1,0:T(8,128)S(1)}, f32[32,768]{1,0:T(8,128)S(1)}, u32[]{:S(2)}, u32[]{:S(2)}) collective-permute-start(f32[32,768]{1,0:T(8,128)S(1)} %add_add_fusion.refs_0_), channel_id=1, source_target_pairs={{0,32},{1,33},{2,34},{3,35},{4,36},{5,37},{6,38},{7,39},{8,40},{9,... | collective-permute-start | bytes 294920 | tf_op jit(solution)/shard_map/ppermute | solution.py:333
  132.7 21.7 %collective-permute-start.29 = (f32[4,32,768]{2,1,0:T(8,128)S(1)}, f32[4,32,768]{2,1,0:T(8,128)S(1)}, u32[]{:S(2)}, u32[]{:S(2)}) collective-permute-start(f32[4,32,768]{2,1,0:T(8,128)S(1)} %shard_map.132.refs_0_), channel_id=1, source_target_pairs={{0,64},{1,65},{2,66},{3,67},{4,68},{5,69},{6,70},{7,71},{8,72},{9,... | collective-permute-start | bytes 1179656 | tf_op jit(solution)/shard_map/ppermute | solution.py:333
  134.7 19.8 %collective-permute-start.30 = (f32[4,32,768]{2,1,0:T(8,128)S(1)}, f32[4,32,768]{2,1,0:T(8,128)S(1)}, u32[]{:S(2)}, u32[]{:S(2)}) collective-permute-start(f32[4,32,768]{2,1,0:T(8,128)S(1)} %shard_map.132.refs_0_), channel_id=1, source_target_pairs={{0,128},{1,129},{2,130},{3,131},{4,132},{5,133},{6,134},{7,135},{8... | collective-permute-start | bytes 1179656 | tf_op jit(solution)/shard_map/ppermute | solution.py:333
  141.5 29.7 %collective-permute-start.31 = (f32[4,32,768]{2,1,0:T(8,128)S(1)}, f32[4,32,768]{2,1,0:T(8,128)S(1)}, u32[]{:S(2)}, u32[]{:S(2)}) collective-permute-start(f32[4,32,768]{2,1,0:T(8,128)S(1)} %shard_map.132.refs_0_), channel_id=1, source_target_pairs={{0,192},{1,193},{2,194},{3,195},{4,196},{5,197},{6,198},{7,199},{8... | collective-permute-start | bytes 1179656 | tf_op jit(solution)/shard_map/ppermute | solution.py:333
  144.0 29.4 %collective-permute-start.32 = (f32[4,32,768]{2,1,0:T(8,128)S(1)}, f32[4,32,768]{2,1,0:T(8,128)S(1)}, u32[]{:S(2)}, u32[]{:S(2)}) collective-permute-start(f32[4,32,768]{2,1,0:T(8,128)S(1)} %shard_map.132.refs_0_), channel_id=1, source_target_pairs={{0,8},{1,9},{2,10},{3,11},{4,12},{5,13},{6,14},{7,15},{8,0},{9,1},... | collective-permute-start | bytes 1179656 | tf_op jit(solution)/shard_map/ppermute | solution.py:333
  154.5 21.4 %collective-permute-start.33 = (f32[4,32,768]{2,1,0:T(8,128)S(1)}, f32[4,32,768]{2,1,0:T(8,128)S(1)}, u32[]{:S(2)}, u32[]{:S(2)}) collective-permute-start(f32[4,32,768]{2,1,0:T(8,128)S(1)} %collective-permute-done.29.refs_1_), channel_id=1, source_target_pairs={{0,8},{1,9},{2,10},{3,11},{4,12},{5,13},{6,14},{7,15},{8,0},{9,1},... | collective-permute-start | bytes 1179656 | tf_op jit(solution)/shard_map/ppermute | solution.py:333
  171.2 15.5 %collective-permute-start.14 = (f32[4,144,128]{2,1,0:T(8,128)S(1)}, f32[4,144,128]{2,1,0:T(8,128)S(1)}, u32[]{:S(2)}, u32[]{:S(2)}) collective-permute-start(f32[4,144,128]{2,1,0:T(8,128)S(1)} %pad_maximum_fusion.refs_0_), channel_id=1, source_target_pairs={{0,128},{1,129},{2,130},{3,131},{4,132},{5,133},{6,134},{7,135},{8... | collective-permute-start | bytes 884744 | tf_op jit(solution)/shard_map/ppermute | solution.py:333
  173.4 13.3 %collective-permute-start.16 = (f32[4,144,128]{2,1,0:T(8,128)S(1)}, f32[4,144,128]{2,1,0:T(8,128)S(1)}, u32[]{:S(2)}, u32[]{:S(2)}) collective-permute-start(f32[4,144,128]{2,1,0:T(8,128)S(1)} %pad_maximum_fusion.refs_0_), channel_id=1, source_target_pairs={{0,192},{1,193},{2,194},{3,195},{4,196},{5,197},{6,198},{7,199},{8... | collective-permute-start | bytes 884744 | tf_op jit(solution)/shard_map/ppermute | solution.py:333
  175.8 11.4 %collective-permute-start.35 = (f32[4,32,768]{2,1,0:T(8,128)S(1)}, f32[4,32,768]{2,1,0:T(8,128)S(1)}, u32[]{:S(2)}, u32[]{:S(2)}) collective-permute-start(f32[4,32,768]{2,1,0:T(8,128)S(1)} %collective-permute-done.31.refs_3_), channel_id=1, source_target_pairs={{0,8},{1,9},{2,10},{3,11},{4,12},{5,13},{6,14},{7,15},{8,0},{9,1},... | collective-permute-start | bytes 1179656 | tf_op jit(solution)/shard_map/ppermute | solution.py:333
  175.8 15.6 %collective-permute-start.11 = (f32[4,144,128]{2,1,0:T(8,128)S(1)}, f32[4,144,128]{2,1,0:T(8,128)S(1)}, u32[]{:S(2)}, u32[]{:S(2)}) collective-permute-start(f32[4,144,128]{2,1,0:T(8,128)S(1)} %pad_maximum_fusion.refs_0_), channel_id=1, source_target_pairs={{0,8},{1,9},{2,10},{3,11},{4,12},{5,13},{6,14},{7,15},{8,0},{9,1},... | collective-permute-start | bytes 884744 | tf_op jit(solution)/shard_map/ppermute | solution.py:333
  179.3 12.2 %collective-permute-start.13 = (f32[4,144,128]{2,1,0:T(8,128)S(1)}, f32[4,144,128]{2,1,0:T(8,128)S(1)}, u32[]{:S(2)}, u32[]{:S(2)}) collective-permute-start(f32[4,144,128]{2,1,0:T(8,128)S(1)} %collective-permute-done.12.refs_1_), channel_id=1, source_target_pairs={{0,8},{1,9},{2,10},{3,11},{4,12},{5,13},{6,14},{7,15},{8,0},{9,1},... | collective-permute-start | bytes 884744 | tf_op jit(solution)/shard_map/ppermute | solution.py:333
  (27 other events, 314.1 us)

commit v4 on v3

--- a/solution.py
+++ b/solution.py
@@ -36,12 +36,13 @@
     return lax.dot_general(a, b, TN, preferred_element_type=F32)
 
 
-def call(body, outs, *args, scalars=0, scratch=(), flops=0, mib=20, aliases=None):
+def call(body, outs, *args, scalars=0, scratch=(), flops=0, mib=20,
+         aliases=None, hbm=(), hbm_out=False):
     spec = pl.BlockSpec(memory_space=pltpu.VMEM)
     smem = pl.BlockSpec(memory_space=pltpu.SMEM)
-    anywhere = pl.BlockSpec(memory_space=pl.ANY)
+    anywhere = pl.BlockSpec(memory_space=pltpu.HBM)
     specs = [smem] * scalars + [spec] * (len(args) - scalars)
-    for k in aliases or {}:
+    for k in (*(aliases or {}), *hbm):
         specs[k] = anywhere
     size = sum(a.size * a.dtype.itemsize for a in args)
     size += sum(math.prod(o.shape) * o.dtype.itemsize for o in outs)
@@ -49,7 +50,7 @@
         body,
         out_shape=outs,
         in_specs=specs,
-        out_specs=[anywhere if aliases is not None else spec] * len(outs),
+        out_specs=[anywhere if hbm_out else spec] * len(outs),
         scratch_shapes=list(scratch),
         input_output_aliases=aliases or {},
         compiler_params=pltpu.CompilerParams(vmem_limit_bytes=mib << 20),
@@ -94,9 +95,35 @@
         unpack_rest(packed[k, 128:PACKED, :], rest, 32 * k)
 
 
-def entry_kernel(tokens, down, rope, out):
-    wide = dot(tokens[...], down[...])
-    rest = dot_nt(tokens[...], rope[...])
+def start(*pairs):
+    copies = [pltpu.make_async_copy(source, target, sem) for source, target, sem in pairs]
+    for copy in copies:
+        copy.start()
+    return copies
+
+
+def wait(copies):
+    for copy in copies:
+        copy.wait()
+
+
+def entry_kernel(tokens_in, down_in, rope_in, out, tokens, down, rope, sems):
+    chunks = []
+    for k in range(4):
+        part = pl.ds(256 * k, 256)
+        chunks.append(
+            start(
+                (tokens_in.at[:, part], tokens.at[:, part], sems.at[k, 0]),
+                (down_in.at[part, :], down.at[part, :], sems.at[k, 1]),
+                (rope_in.at[:, part], rope.at[:, part], sems.at[k, 2]),
+            )
+        )
+    wide, rest = jnp.zeros((SEQ, LATENT), F32), jnp.zeros((SEQ, 64), F32)
+    for k in range(4):
+        wait(chunks[k])
+        part = pl.ds(256 * k, 256)
+        wide = wide + dot(tokens[:, part], down[part, :])
+        rest = rest + dot_nt(tokens[:, part], rope[:, part])
     rest = jnp.concatenate([rest, jnp.zeros_like(rest)], axis=1)
     for k in range(8):
         pack(out, k, 32 * k, wide, rest)
@@ -187,19 +214,29 @@
 
 
 def student_kernel(
-    at, packed, queries, key_up, value_up, teacher, cos_part, sin_part, segments,
-    grads_keep, grads_send, norm_out, latent, rest, nope, head_values, rest_sum, grads_out,
+    at, packed, queries_in, key_up_in, value_up_in, teacher_in, cos_part, sin_part, segments,
+    keep_out, send_out, norm_out, latent, rest, nope, head_values, rest_sum, grads,
+    queries, key_up, value_up, teacher, keep, send, norm, sems,
 ):
+    (get_keys, get_values, *get_others) = start(
+        (key_up_in, key_up, sems.at[0]),
+        (value_up_in, value_up, sems.at[1]),
+        (queries_in, queries, sems.at[2]),
+        (teacher_in, teacher, sems.at[3]),
+    )
     unpack(packed, latent, rest)
     cos, sin = part_table(cos_part[...], sin_part[...])
     low = low_lanes(SEQ)
     turn = lambda v: v * cos + swap(v) * sin
     rope_key = turn(rest[...])
+    wait([get_keys])
     nope[...] = dot(latent[...], key_up[...])
+    wait([get_values])
     head_values[...] = dot(latent[...], value_up[...]).astype(BF16)
     mask = seen(segments[...])
     scale = 1.0 / math.sqrt(HEAD)
     rest_sum[...] = jnp.zeros_like(rest_sum)
+    wait(get_others)
 
     def head(h, key_part):
         query = turn(queries[:, lanes(h)].astype(F32)).astype(BF16)
@@ -211,27 +248,30 @@
         weight_grad = dot_nt(out_grad, value)
         row = jnp.sum(weights * weight_grad, axis=1, keepdims=True)
         score_grad = (weights * (weight_grad - row) * scale).astype(BF16)
-        grads_out[:, lanes(4 + h)] = dot_tn(weights_low, out_grad).astype(BF16)
+        grads[:, lanes(4 + h)] = dot_tn(weights_low, out_grad).astype(BF16)
         return dot_tn(score_grad, query)
 
-    def pair(p, carry):
-        both = nope[:, lanes(p)]
-        first = head(2 * p, pltpu.roll(both, 64, 1))
-        second = head(2 * p + 1, both)
-        rest_sum[...] += first + second
-        grads_out[:, lanes(p)] = jnp.where(low, pltpu.roll(first, 64, 1), second).astype(BF16)
+    def heads(step, carry):
+        for p in (2 * step, 2 * step + 1):
+            both = nope[:, lanes(p)]
+            first = head(2 * p, pltpu.roll(both, 64, 1))
+            second = head(2 * p + 1, both)
+            rest_sum[...] += first + second
+            grads[:, lanes(p)] = jnp.where(low, pltpu.roll(first, 64, 1), second).astype(BF16)
         return carry
 
-    lax.fori_loop(0, 4, pair, 0)
-    wide = dot_nt(grads_out[:, :512], key_up[...]) + dot_nt(grads_out[:, 512:], value_up[...])
-    rest_all = rest_sum[...]
-    for ref, c in ((grads_keep, at[0]), (grads_send, 1 - at[0])):
+    lax.fori_loop(0, 2, heads, 0)
+    for ref, c in ((send, 1 - at[0]), (keep, at[0])):
         keys = pl.ds(pl.multiple_of(c * 256, 256), 256)
         values = pl.ds(pl.multiple_of(512 + c * 512, 512), 512)
-        ref[:, :256] = grads_out[:, keys].astype(ref.dtype)
-        ref[:, 256:] = grads_out[:, values].astype(ref.dtype)
+        ref[:, :256] = grads[:, keys].astype(ref.dtype)
+        ref[:, 256:] = grads[:, values].astype(ref.dtype)
+    puts = start((send, send_out, sems.at[4]), (keep, keep_out, sems.at[5]))
+    wide = dot_nt(grads[:, :512], key_up[...]) + dot_nt(grads[:, 512:], value_up[...])
+    rest_all = rest_sum[...]
     for k in range(8):
-        pack(norm_out, k, 32 * k, wide, rest_all)
+        pack(norm, k, 32 * k, wide, rest_all)
+    wait(puts + start((norm, norm_out, sems.at[6])))
 
 
 def up_kernel(at, packed, other_packed, grads, other_grads, *outs):
@@ -294,6 +334,7 @@
 def entry_out_kernel(own, at, *refs):
     parts, (down_out, rope_out, down, rope, rest, sems) = refs[:4], refs[-6:]
     half = at[0] if own else 1 - at[0]
+    copies = []
     for step in range(4):
         first = (at[1] - step + 4) % 4
         for depth in range(4):
@@ -305,15 +346,13 @@
             rest[pl.ds(pl.multiple_of(spot, 32), 16), :] = value
             rest[pl.ds(pl.multiple_of(spot + 16, 16), 16), :] = pltpu.roll(value, 64, 1)
         rope[:, lanes(first)] = rest[...].T[:64]
-    where = pl.ds(pl.multiple_of(half * 512, 512), 512)
-    copies = [
-        pltpu.make_async_copy(down, down_out.at[where, :], sems.at[0]),
-        pltpu.make_async_copy(rope, rope_out.at[:, where], sems.at[1]),
-    ]
-    for copy in copies:
-        copy.start()
-    for copy in copies:
-        copy.wait()
+        group = pl.ds(pl.multiple_of(first * 128, 128), 128)
+        where = pl.ds(pl.multiple_of(half * 512 + first * 128, 128), 128)
+        copies += start(
+            (down.at[group, :], down_out.at[where, :], sems.at[step, 0]),
+            (rope.at[:, group], rope_out.at[:, where], sems.at[step, 1]),
+        )
+    wait(copies)
 
 
 def stack_kernel(*refs):
@@ -368,7 +407,16 @@
     chunks = shape(8, PACKED, 128)
     unpacked = [pltpu.VMEM((SEQ, LATENT), BF16), pltpu.VMEM((SEQ, 128), F32)]
 
-    (part,) = call(entry_kernel, [chunks], tokens, down, rope, flops=2 * 256 * 1024 * 576, mib=60)
+    (part,) = call(
+        entry_kernel, [chunks], tokens, down, rope, hbm=(0, 1, 2),
+        scratch=[
+            pltpu.VMEM((SEQ, 1024), BF16),
+            pltpu.VMEM((1024, LATENT), BF16),
+            pltpu.VMEM((64, 1024), BF16),
+            pltpu.SemaphoreType.DMA((4, 3)),
+        ],
+        flops=2 * 256 * 1024 * 576, mib=60,
+    )
     parts = exchange(part)
     full, partial = tables(segments)
     teacher, tokens_keep, tokens_send = call(
@@ -392,7 +440,16 @@
             pltpu.VMEM((SEQ, 1024), BF16),
             pltpu.VMEM((SEQ, 128), F32),
             pltpu.VMEM((SEQ, 1536), BF16),
+            pltpu.VMEM((SEQ, 1024), BF16),
+            pltpu.VMEM((LATENT, 512), BF16),
+            pltpu.VMEM((LATENT, 1024), BF16),
+            pltpu.VMEM((SEQ, 1024), F32),
+            pltpu.VMEM((SEQ, 768), BF16),
+            pltpu.VMEM((SEQ, 768), F32),
+            pltpu.VMEM((8, PACKED, 128), F32),
+            pltpu.SemaphoreType.DMA((7,)),
         ],
+        hbm=(2, 3, 4, 5), hbm_out=True,
         flops=10 * 8 * 256 * 256 * 128, mib=60,
     )
     grads_other = other_core(grads_send)
@@ -434,15 +491,15 @@
         pltpu.VMEM((512, 512), F32),
         pltpu.VMEM((64, 512), F32),
         pltpu.VMEM((128, 128), F32),
-        pltpu.SemaphoreType.DMA((2,)),
+        pltpu.SemaphoreType.DMA((4, 2)),
     ]
     halves = call(
         functools.partial(entry_out_kernel, True), outs, at, *entries, scalars=1,
-        scratch=scratch, aliases={},
+        scratch=scratch, hbm_out=True,
     )
     grad_down, grad_rope = call(
         functools.partial(entry_out_kernel, False), outs, at, *others, *halves, scalars=1,
-        scratch=scratch, aliases={5: 0, 6: 1},
+        scratch=scratch, hbm_out=True, aliases={5: 0, 6: 1},
     )
     return grad_down, grad_rope, grad_key, grad_value
 

time: 195 us -> 194 us (level)
  no operation moved by 1% of the time
where the time goes in v4:
time: 194 us; the launch traced here: 193 us
  starting transfers between devices  73.7 us (38%)
  waiting for transfers between devices  63.7 us (33%)
  Pallas kernels  35.4 us (18%)
  blocking collectives  13 us (7%)
  other arithmetic  3.37 us (2%)
  local copies, waits for them, and re-layouts  2.91 us (2%)
    ppermute x36, starting transfers between devices, permute(): return lax.ppermute(value, AXES, pairs)  57.9 us
    ppermute x36, waiting for transfers between devices, permute(): return lax.ppermute(value, AXES, pairs)  55.2 us
    pallas_call x14, Pallas kernels, call(): pl.pallas_call(body, out_shape=outs, in_specs=specs, out_specs=[anywhere...  35.4 us
    all_to_all x3, starting transfers between devices, exchange(): return lax.all_to_all(parts, 'tensor', 0, 0, tiled=True)  15.8 us
    all_to_all x1, blocking collectives, exchange(): return lax.all_to_all(parts, 'tensor', 0, 0, tiled=True)  13 us
    all_to_all x3, waiting for transfers between devices, exchange(): return lax.all_to_all(parts, 'tensor', 0, 0, tiled=True)  8.54 us
  transfers between devices with their start and end apart: 39, of which 15 were waited for; matrix products, arithmetic and copies ran while one was open for 2% of the time, Pallas kernels for 9%

profile of v4, /device:TPU:32, one launch (start us, length us, event | category | flops | bytes accessed | tf_op | source)
XLA Modules:
  0.0 193.0 jit_solution(4447934861164148157)
XLA Ops:
  0.6 3.0 %shard_map.120 = f32[8,144,128]{2,1,0:T(8,128)} custom-call(bf16[256,1024]{1,0:T(8,128)(2,1)} %bitcast.16, bf16[1024,512]{1,0:T(8,128)(2,1)} %down_in.1, bf16[64,1024]{1,0:T(8,128)(2,1)} %rope_in.1), custom_call_target="tpu_custom_call" | custom-call | flops 301989888 | bytes 2293760 | tf_op jit(solution)/shard_map/pallas_call | solution.py:49
  3.6 5.9 %all-to-all-start = ((f32[8,144,128]{2,1,0:T(8,128)}), f32[8,144,128]{2,1,0:T(8,128)S(1)}, u32[]{:S(2)}, u32[]{:S(2)}) async-start(f32[8,144,128]{2,1,0:T(8,128)} %shard_map.120), calls=%async_computation | async-start | bytes 1179648 | tf_op jit(solution)/shard_map/all_to_all | solution.py:386
  11.7 6.8 %shard_map.121 = (f32[256,1024]{1,0:T(8,128)}, bf16[512,256]{1,0:T(8,128)(2,1)}, f32[512,256]{1,0:T(8,128)}) custom-call(s32[4]{0:T(128)} %pad_add_fusion.at, bf16[256,1024]{1,0:T(8,128)(2,1)} %bitcast.14, bf16[256,128]{1,0:T(8,128)(2,1)} %bitcast.21, bf16[256,128]{1,0:T(8,128)(2,1)} %bitcast.22, f32[256,64]{1,0:T(8,128)} %get-tuple-element.73.cos_full, ...), custom_call_target="tpu_custom_call" | custom-call | flops 268435456 | bytes 3146768 | tf_op jit(solution)/shard_map/pallas_call | solution.py:49
  20.2 5.0 %all-to-all-start.1 = ((f32[8,144,128]{2,1,0:T(8,128)}), f32[8,144,128]{2,1,0:T(8,128)S(1)}, u32[]{:S(2)}, u32[]{:S(2)}) async-start(f32[8,144,128]{2,1,0:T(8,128)} %get-tuple-element.39), calls=%async_computation.1 | async-start | bytes 1179648 | tf_op jit(solution)/shard_map/all_to_all | solution.py:386
  26.4 7.8 %all-to-all-done.1.packed = f32[8,144,128]{2,1,0:T(8,128)S(1)} async-done(((f32[8,144,128]{2,1,0:T(8,128)}), f32[8,144,128]{2,1,0:T(8,128)S(1)}, u32[]{:S(2)}, u32[]{:S(2)}) %all-to-all-start.1) | async-done | bytes 589856 | tf_op jit(solution)/shard_map/all_to_all | solution.py:386
  35.1 10.8 %shard_map.123 = (bf16[256,768]{1,0:T(8,128)(2,1)}, f32[256,768]{1,0:T(8,128)}, f32[8,144,128]{2,1,0:T(8,128)}) custom-call(s32[4]{0:T(128)} %pad_add_fusion.at, f32[8,144,128]{2,1,0:T(8,128)} %copy-done.6, bf16[256,1024]{1,0:T(8,128)(2,1)} %bitcast.15, bf16[512,512]{1,0:T(8,128)(2,1)} %key_up_in.1, bf16[512,1024]{1,0:T(8,128)(2,1)} %value_up_in.1, ...), custom_call_target="tpu_custom_call" | custom-call | flops 671088640 | bytes 5571600 | tf_op jit(solution)/shard_map/pallas_call | solution.py:49
  45.9 13.0 %all_to_all.20.parts = f32[8,144,128]{2,1,0:T(8,128)S(1)} all-to-all(f32[8,144,128]{2,1,0:T(8,128)} %get-tuple-element.41), channel_id=1, replica_groups=mesh['dp'=32,'tensor'=8] {'tensor'}, dimensions={0} | all-to-all | bytes 1179648 | tf_op jit(solution)/shard_map/all_to_all | solution.py:386
  60.4 4.9 %all-to-all-start.3 = ((f32[8,144,128]{2,1,0:T(8,128)}), f32[8,144,128]{2,1,0:T(8,128)S(1)}, u32[]{:S(2)}, u32[]{:S(2)}) async-start(f32[8,144,128]{2,1,0:T(8,128)} %shard_map.124), calls=%async_computation.3 | async-start | bytes 1179648 | tf_op jit(solution)/shard_map/all_to_all | solution.py:386
  69.5 3.7 %shard_map.130 = (f32[128,768]{1,0:T(8,128)}, f32[128,768]{1,0:T(8,128)}, f32[128,768]{1,0:T(8,128)}, f32[128,768]{1,0:T(8,128)}) custom-call(s32[4]{0:T(128)} %pad_add_fusion.at, f32[8,144,128]{2,1,0:T(8,128)} %copy-done.6, f32[8,144,128]{2,1,0:T(8,128)} %copy-done.9, bf16[256,768]{1,0:T(8,128)(2,1)} %get-tuple-element.58.grads, f32[256,768]{1,0:T(8,128)} %copy-done.8), custom_call_target="tpu_custom_call" | custom-call | flops 402653184 | bytes 3932176 | tf_op jit(solution)/shard_map/pallas_call | solution.py:49
  79.4 6.4 %collective-permute-done.20.first = f32[128,768]{1,0:T(8,128)S(1)} collective-permute-done((f32[128,768]{1,0:T(8,128)}, f32[128,768]{1,0:T(8,128)S(1)}, u32[]{:S(2)}, u32[]{:S(2)}) %collective-permute-start.20) | collective-permute-done | bytes 393248 | tf_op jit(solution)/shard_map/ppermute | solution.py:372
  85.8 9.4 %collective-permute-done.21.second = f32[128,768]{1,0:T(8,128)S(1)} collective-permute-done((f32[128,768]{1,0:T(8,128)}, f32[128,768]{1,0:T(8,128)S(1)}, u32[]{:S(2)}, u32[]{:S(2)}) %collective-permute-start.21) | collective-permute-done | bytes 393248 | tf_op jit(solution)/shard_map/ppermute | solution.py:372
  96.8 6.4 %collective-permute-start.24 = (f32[32,768]{1,0:T(8,128)S(1)}, f32[32,768]{1,0:T(8,128)S(1)}, u32[]{:S(2)}, u32[]{:S(2)}) collective-permute-start(f32[32,768]{1,0:T(8,128)S(1)} %get-tuple-element.66), channel_id=1, source_target_pairs={{0,32},{1,33},{2,34},{3,35},{4,36},{5,37},{6,38},{7,39},{8,40},{9,... | collective-permute-start | bytes 294920 | tf_op jit(solution)/shard_map/ppermute | solution.py:372
  106.1 2.9 %collective-permute-done.24 = f32[32,768]{1,0:T(8,128)S(1)} collective-permute-done((f32[32,768]{1,0:T(8,128)S(1)}, f32[32,768]{1,0:T(8,128)S(1)}, u32[]{:S(2)}, u32[]{:S(2)}) %collective-permute-start.24) | collective-permute-done | bytes 98336 | tf_op jit(solution)/shard_map/ppermute | solution.py:372
  116.7 3.1 %collective-permute-start.3 = (f32[4,144,128]{2,1,0:T(8,128)S(1)}, f32[4,144,128]{2,1,0:T(8,128)S(1)}, u32[]{:S(2)}, u32[]{:S(2)}) collective-permute-start(f32[4,144,128]{2,1,0:T(8,128)S(1)} %get-tuple-element.48), channel_id=1, source_target_pairs={{0,128},{1,129},{2,130},{3,131},{4,132},{5,133},{6,134},{7,135},{8... | collective-permute-start | bytes 884744 | tf_op jit(solution)/shard_map/ppermute | solution.py:372
  120.4 4.1 %collective-permute-start.27 = (f32[32,768]{1,0:T(8,128)S(1)}, f32[32,768]{1,0:T(8,128)S(1)}, u32[]{:S(2)}, u32[]{:S(2)}) collective-permute-start(f32[32,768]{1,0:T(8,128)S(1)} %add_add_fusion.refs_0_), channel_id=1, source_target_pairs={{0,32},{1,33},{2,34},{3,35},{4,36},{5,37},{6,38},{7,39},{8,40},{9,... | collective-permute-start | bytes 294920 | tf_op jit(solution)/shard_map/ppermute | solution.py:372
  126.9 5.3 %collective-permute-done.27.refs_2_ = f32[32,768]{1,0:T(8,128)S(1)} collective-permute-done((f32[32,768]{1,0:T(8,128)S(1)}, f32[32,768]{1,0:T(8,128)S(1)}, u32[]{:S(2)}, u32[]{:S(2)}) %collective-permute-start.27) | collective-permute-done | bytes 98336 | tf_op jit(solution)/shard_map/ppermute | solution.py:372
  134.8 3.3 %collective-permute-start.5 = (f32[144,128]{1,0:T(8,128)S(1)}, f32[144,128]{1,0:T(8,128)S(1)}, u32[]{:S(2)}, u32[]{:S(2)}) collective-permute-start(f32[144,128]{1,0:T(8,128)S(1)} %get-tuple-element.51), channel_id=1, source_target_pairs={{0,16},{1,17},{2,18},{3,19},{4,20},{5,21},{6,22},{7,23},{8,24},{9,... | collective-permute-start | bytes 221192 | tf_op jit(solution)/shard_map/ppermute | solution.py:372
  138.1 3.2 %collective-permute-start.6 = (f32[144,128]{1,0:T(8,128)S(1)}, f32[144,128]{1,0:T(8,128)S(1)}, u32[]{:S(2)}, u32[]{:S(2)}) collective-permute-start(f32[144,128]{1,0:T(8,128)S(1)} %get-tuple-element.52), channel_id=1, source_target_pairs={{0,32},{1,33},{2,34},{3,35},{4,36},{5,37},{6,38},{7,39},{8,40},{9,... | collective-permute-start | bytes 221192 | tf_op jit(solution)/shard_map/ppermute | solution.py:372
  147.3 4.3 %collective-permute-done.7.third = f32[144,128]{1,0:T(8,128)S(1)} collective-permute-done((f32[144,128]{1,0:T(8,128)S(1)}, f32[144,128]{1,0:T(8,128)S(1)}, u32[]{:S(2)}, u32[]{:S(2)}) %collective-permute-start.7) | collective-permute-done | bytes 73760 | tf_op jit(solution)/shard_map/ppermute | solution.py:372
  153.9 4.7 %collective-permute-start.9 = (f32[144,128]{1,0:T(8,128)S(1)}, f32[144,128]{1,0:T(8,128)S(1)}, u32[]{:S(2)}, u32[]{:S(2)}) collective-permute-start(f32[144,128]{1,0:T(8,128)S(1)} %shard_map.127), channel_id=1, source_target_pairs={{0,32},{1,33},{2,34},{3,35},{4,36},{5,37},{6,38},{7,39},{8,40},{9,... | collective-permute-start | bytes 221192 | tf_op jit(solution)/shard_map/ppermute | solution.py:372
  158.6 2.8 %collective-permute-start.8 = (f32[144,128]{1,0:T(8,128)S(1)}, f32[144,128]{1,0:T(8,128)S(1)}, u32[]{:S(2)}, u32[]{:S(2)}) collective-permute-start(f32[144,128]{1,0:T(8,128)S(1)} %shard_map.127), channel_id=1, source_target_pairs={{0,16},{1,17},{2,18},{3,19},{4,20},{5,21},{6,22},{7,23},{8,24},{9,... | collective-permute-start | bytes 221192 | tf_op jit(solution)/shard_map/ppermute | solution.py:372
  164.1 4.5 %collective-permute-done.8 = f32[144,128]{1,0:T(8,128)S(1)} collective-permute-done((f32[144,128]{1,0:T(8,128)S(1)}, f32[144,128]{1,0:T(8,128)S(1)}, u32[]{:S(2)}, u32[]{:S(2)}) %collective-permute-start.8) | collective-permute-done | bytes 73760 | tf_op jit(solution)/shard_map/ppermute | solution.py:372
  174.4 4.4 %collective-permute-done.12.refs_1_ = f32[4,144,128]{2,1,0:T(8,128)S(1)} collective-permute-done((f32[4,144,128]{2,1,0:T(8,128)S(1)}, f32[4,144,128]{2,1,0:T(8,128)S(1)}, u32[]{:S(2)}, u32[]{:S(2)}) %collective-permute-start.12) | collective-permute-done | bytes 294944 | tf_op jit(solution)/shard_map/ppermute | solution.py:372
  178.9 7.4 %collective-permute-done.14.refs_2_ = f32[4,144,128]{2,1,0:T(8,128)S(1)} collective-permute-done((f32[4,144,128]{2,1,0:T(8,128)S(1)}, f32[4,144,128]{2,1,0:T(8,128)S(1)}, u32[]{:S(2)}, u32[]{:S(2)}) %collective-permute-start.14) | collective-permute-done | bytes 294944 | tf_op jit(solution)/shard_map/ppermute | solution.py:372
  (102 shorter events, 59.0 us)
Async XLA Ops:
  3.6 15.6 %all-to-all-start = ((f32[8,144,128]{2,1,0:T(8,128)}), f32[8,144,128]{2,1,0:T(8,128)S(1)}, u32[]{:S(2)}, u32[]{:S(2)}) async-start(f32[8,144,128]{2,1,0:T(8,128)} %shard_map.120), calls=%async_computation | async-start | bytes 1179648 | tf_op jit(solution)/shard_map/all_to_all | solution.py:386
  20.2 14.1 %all-to-all-start.1 = ((f32[8,144,128]{2,1,0:T(8,128)}), f32[8,144,128]{2,1,0:T(8,128)S(1)}, u32[]{:S(2)}, u32[]{:S(2)}) async-start(f32[8,144,128]{2,1,0:T(8,128)} %get-tuple-element.39), calls=%async_computation.1 | async-start | bytes 1179648 | tf_op jit(solution)/shard_map/all_to_all | solution.py:386
  60.4 18.5 %all-to-all-start.3 = ((f32[8,144,128]{2,1,0:T(8,128)}), f32[8,144,128]{2,1,0:T(8,128)S(1)}, u32[]{:S(2)}, u32[]{:S(2)}) async-start(f32[8,144,128]{2,1,0:T(8,128)} %shard_map.124), calls=%async_computation.3 | async-start | bytes 1179648 | tf_op jit(solution)/shard_map/all_to_all | solution.py:386
  73.2 12.6 %collective-permute-start.20 = (f32[128,768]{1,0:T(8,128)}, f32[128,768]{1,0:T(8,128)S(1)}, u32[]{:S(2)}, u32[]{:S(2)}) collective-permute-start(f32[128,768]{1,0:T(8,128)} %get-tuple-element.61), channel_id=1, source_target_pairs={{0,64},{1,65},{2,66},{3,67},{4,68},{5,69},{6,70},{7,71},{8,72},{9,... | collective-permute-start | bytes 1179656 | tf_op jit(solution)/shard_map/ppermute | solution.py:372
  74.7 20.5 %collective-permute-start.21 = (f32[128,768]{1,0:T(8,128)}, f32[128,768]{1,0:T(8,128)S(1)}, u32[]{:S(2)}, u32[]{:S(2)}) collective-permute-start(f32[128,768]{1,0:T(8,128)} %get-tuple-element.62), channel_id=1, source_target_pairs={{0,128},{1,129},{2,130},{3,131},{4,132},{5,133},{6,134},{7,135},{8... | collective-permute-start | bytes 1179656 | tf_op jit(solution)/shard_map/ppermute | solution.py:372
  77.4 17.8 %collective-permute-start.22 = (f32[128,768]{1,0:T(8,128)}, f32[128,768]{1,0:T(8,128)S(1)}, u32[]{:S(2)}, u32[]{:S(2)}) collective-permute-start(f32[128,768]{1,0:T(8,128)} %get-tuple-element.63), channel_id=1, source_target_pairs={{0,192},{1,193},{2,194},{3,195},{4,196},{5,197},{6,198},{7,199},{8... | collective-permute-start | bytes 1179656 | tf_op jit(solution)/shard_map/ppermute | solution.py:372
  78.9 35.1 %collective-permute-start = (f32[8,144,128]{2,1,0:T(8,128)S(1)}, f32[8,144,128]{2,1,0:T(8,128)S(1)}, u32[]{:S(2)}, u32[]{:S(2)}) collective-permute-start(f32[8,144,128]{2,1,0:T(8,128)S(1)} %all-to-all-done.3.packed), channel_id=1, source_target_pairs={{0,8},{1,9},{2,10},{3,11},{4,12},{5,13},{6,14},{7,15},{8,0},{9,1},... | collective-permute-start | bytes 1769480 | tf_op jit(solution)/shard_map/ppermute | solution.py:372
  78.9 35.1 %collective-permute-start.1 = (f32[512,256]{1,0:T(8,128)}, f32[512,256]{1,0:T(8,128)S(1)}, u32[]{:S(2)}, u32[]{:S(2)}) collective-permute-start(f32[512,256]{1,0:T(8,128)} %get-tuple-element.45), channel_id=1, source_target_pairs={{0,8},{1,9},{2,10},{3,11},{4,12},{5,13},{6,14},{7,15},{8,0},{9,1},... | collective-permute-start | bytes 1572872 | tf_op jit(solution)/shard_map/ppermute | solution.py:372
  96.8 12.2 %collective-permute-start.24 = (f32[32,768]{1,0:T(8,128)S(1)}, f32[32,768]{1,0:T(8,128)S(1)}, u32[]{:S(2)}, u32[]{:S(2)}) collective-permute-start(f32[32,768]{1,0:T(8,128)S(1)} %get-tuple-element.66), channel_id=1, source_target_pairs={{0,32},{1,33},{2,34},{3,35},{4,36},{5,37},{6,38},{7,39},{8,40},{9,... | collective-permute-start | bytes 294920 | tf_op jit(solution)/shard_map/ppermute | solution.py:372
  111.5 12.9 %collective-permute-start.26 = (f32[32,768]{1,0:T(8,128)S(1)}, f32[32,768]{1,0:T(8,128)S(1)}, u32[]{:S(2)}, u32[]{:S(2)}) collective-permute-start(f32[32,768]{1,0:T(8,128)S(1)} %add_add_fusion.refs_0_), channel_id=1, source_target_pairs={{0,16},{1,17},{2,18},{3,19},{4,20},{5,21},{6,22},{7,23},{8,24},{9,... | collective-permute-start | bytes 294920 | tf_op jit(solution)/shard_map/ppermute | solution.py:372
  115.2 19.0 %collective-permute-start.2 = (f32[4,144,128]{2,1,0:T(8,128)S(1)}, f32[4,144,128]{2,1,0:T(8,128)S(1)}, u32[]{:S(2)}, u32[]{:S(2)}) collective-permute-start(f32[4,144,128]{2,1,0:T(8,128)S(1)} %get-tuple-element.47), channel_id=1, source_target_pairs={{0,64},{1,65},{2,66},{3,67},{4,68},{5,69},{6,70},{7,71},{8,72},{9,... | collective-permute-start | bytes 884744 | tf_op jit(solution)/shard_map/ppermute | solution.py:372
  116.7 17.5 %collective-permute-start.3 = (f32[4,144,128]{2,1,0:T(8,128)S(1)}, f32[4,144,128]{2,1,0:T(8,128)S(1)}, u32[]{:S(2)}, u32[]{:S(2)}) collective-permute-start(f32[4,144,128]{2,1,0:T(8,128)S(1)} %get-tuple-element.48), channel_id=1, source_target_pairs={{0,128},{1,129},{2,130},{3,131},{4,132},{5,133},{6,134},{7,135},{8... | collective-permute-start | bytes 884744 | tf_op jit(solution)/shard_map/ppermute | solution.py:372
  119.8 14.4 %collective-permute-start.4 = (f32[4,144,128]{2,1,0:T(8,128)S(1)}, f32[4,144,128]{2,1,0:T(8,128)S(1)}, u32[]{:S(2)}, u32[]{:S(2)}) collective-permute-start(f32[4,144,128]{2,1,0:T(8,128)S(1)} %get-tuple-element.49), channel_id=1, source_target_pairs={{0,192},{1,193},{2,194},{3,195},{4,196},{5,197},{6,198},{7,199},{8... | collective-permute-start | bytes 884744 | tf_op jit(solution)/shard_map/ppermute | solution.py:372
  120.4 11.8 %collective-permute-start.27 = (f32[32,768]{1,0:T(8,128)S(1)}, f32[32,768]{1,0:T(8,128)S(1)}, u32[]{:S(2)}, u32[]{:S(2)}) collective-permute-start(f32[32,768]{1,0:T(8,128)S(1)} %add_add_fusion.refs_0_), channel_id=1, source_target_pairs={{0,32},{1,33},{2,34},{3,35},{4,36},{5,37},{6,38},{7,39},{8,40},{9,... | collective-permute-start | bytes 294920 | tf_op jit(solution)/shard_map/ppermute | solution.py:372
  132.2 21.7 %collective-permute-start.29 = (f32[4,32,768]{2,1,0:T(8,128)S(1)}, f32[4,32,768]{2,1,0:T(8,128)S(1)}, u32[]{:S(2)}, u32[]{:S(2)}) collective-permute-start(f32[4,32,768]{2,1,0:T(8,128)S(1)} %shard_map.132.refs_0_), channel_id=1, source_target_pairs={{0,64},{1,65},{2,66},{3,67},{4,68},{5,69},{6,70},{7,71},{8,72},{9,... | collective-permute-start | bytes 1179656 | tf_op jit(solution)/shard_map/ppermute | solution.py:372
  134.2 19.7 %collective-permute-start.30 = (f32[4,32,768]{2,1,0:T(8,128)S(1)}, f32[4,32,768]{2,1,0:T(8,128)S(1)}, u32[]{:S(2)}, u32[]{:S(2)}) collective-permute-start(f32[4,32,768]{2,1,0:T(8,128)S(1)} %shard_map.132.refs_0_), channel_id=1, source_target_pairs={{0,128},{1,129},{2,130},{3,131},{4,132},{5,133},{6,134},{7,135},{8... | collective-permute-start | bytes 1179656 | tf_op jit(solution)/shard_map/ppermute | solution.py:372
  141.3 29.8 %collective-permute-start.31 = (f32[4,32,768]{2,1,0:T(8,128)S(1)}, f32[4,32,768]{2,1,0:T(8,128)S(1)}, u32[]{:S(2)}, u32[]{:S(2)}) collective-permute-start(f32[4,32,768]{2,1,0:T(8,128)S(1)} %shard_map.132.refs_0_), channel_id=1, source_target_pairs={{0,192},{1,193},{2,194},{3,195},{4,196},{5,197},{6,198},{7,199},{8... | collective-permute-start | bytes 1179656 | tf_op jit(solution)/shard_map/ppermute | solution.py:372
  143.7 29.4 %collective-permute-start.32 = (f32[4,32,768]{2,1,0:T(8,128)S(1)}, f32[4,32,768]{2,1,0:T(8,128)S(1)}, u32[]{:S(2)}, u32[]{:S(2)}) collective-permute-start(f32[4,32,768]{2,1,0:T(8,128)S(1)} %shard_map.132.refs_0_), channel_id=1, source_target_pairs={{0,8},{1,9},{2,10},{3,11},{4,12},{5,13},{6,14},{7,15},{8,0},{9,1},... | collective-permute-start | bytes 1179656 | tf_op jit(solution)/shard_map/ppermute | solution.py:372
  153.9 20.0 %collective-permute-start.33 = (f32[4,32,768]{2,1,0:T(8,128)S(1)}, f32[4,32,768]{2,1,0:T(8,128)S(1)}, u32[]{:S(2)}, u32[]{:S(2)}) collective-permute-start(f32[4,32,768]{2,1,0:T(8,128)S(1)} %collective-permute-done.29.refs_1_), channel_id=1, source_target_pairs={{0,8},{1,9},{2,10},{3,11},{4,12},{5,13},{6,14},{7,15},{8,0},{9,1},... | collective-permute-start | bytes 1179656 | tf_op jit(solution)/shard_map/ppermute | solution.py:372
  171.0 15.2 %collective-permute-start.14 = (f32[4,144,128]{2,1,0:T(8,128)S(1)}, f32[4,144,128]{2,1,0:T(8,128)S(1)}, u32[]{:S(2)}, u32[]{:S(2)}) collective-permute-start(f32[4,144,128]{2,1,0:T(8,128)S(1)} %pad_maximum_fusion.refs_0_), channel_id=1, source_target_pairs={{0,128},{1,129},{2,130},{3,131},{4,132},{5,133},{6,134},{7,135},{8... | collective-permute-start | bytes 884744 | tf_op jit(solution)/shard_map/ppermute | solution.py:372
  173.2 13.1 %collective-permute-start.16 = (f32[4,144,128]{2,1,0:T(8,128)S(1)}, f32[4,144,128]{2,1,0:T(8,128)S(1)}, u32[]{:S(2)}, u32[]{:S(2)}) collective-permute-start(f32[4,144,128]{2,1,0:T(8,128)S(1)} %pad_maximum_fusion.refs_0_), channel_id=1, source_target_pairs={{0,192},{1,193},{2,194},{3,195},{4,196},{5,197},{6,198},{7,199},{8... | collective-permute-start | bytes 884744 | tf_op jit(solution)/shard_map/ppermute | solution.py:372
  173.9 12.9 %collective-permute-start.35 = (f32[4,32,768]{2,1,0:T(8,128)S(1)}, f32[4,32,768]{2,1,0:T(8,128)S(1)}, u32[]{:S(2)}, u32[]{:S(2)}) collective-permute-start(f32[4,32,768]{2,1,0:T(8,128)S(1)} %collective-permute-done.31.refs_3_), channel_id=1, source_target_pairs={{0,8},{1,9},{2,10},{3,11},{4,12},{5,13},{6,14},{7,15},{8,0},{9,1},... | collective-permute-start | bytes 1179656 | tf_op jit(solution)/shard_map/ppermute | solution.py:372
  173.9 17.1 %collective-permute-start.11 = (f32[4,144,128]{2,1,0:T(8,128)S(1)}, f32[4,144,128]{2,1,0:T(8,128)S(1)}, u32[]{:S(2)}, u32[]{:S(2)}) collective-permute-start(f32[4,144,128]{2,1,0:T(8,128)S(1)} %pad_maximum_fusion.refs_0_), channel_id=1, source_target_pairs={{0,8},{1,9},{2,10},{3,11},{4,12},{5,13},{6,14},{7,15},{8,0},{9,1},... | collective-permute-start | bytes 884744 | tf_op jit(solution)/shard_map/ppermute | solution.py:372
  178.9 12.2 %collective-permute-start.13 = (f32[4,144,128]{2,1,0:T(8,128)S(1)}, f32[4,144,128]{2,1,0:T(8,128)S(1)}, u32[]{:S(2)}, u32[]{:S(2)}) collective-permute-start(f32[4,144,128]{2,1,0:T(8,128)S(1)} %collective-permute-done.12.refs_1_), channel_id=1, source_target_pairs={{0,8},{1,9},{2,10},{3,11},{4,12},{5,13},{6,14},{7,15},{8,0},{9,1},... | collective-permute-start | bytes 884744 | tf_op jit(solution)/shard_map/ppermute | solution.py:372
  (27 other events, 311.4 us)

commit v5 on v4

--- a/solution.py
+++ b/solution.py
@@ -107,23 +107,21 @@
         copy.wait()
 
 
-def entry_kernel(tokens_in, down_in, rope_in, out, tokens, down, rope, sems):
-    chunks = []
-    for k in range(4):
-        part = pl.ds(256 * k, 256)
-        chunks.append(
-            start(
-                (tokens_in.at[:, part], tokens.at[:, part], sems.at[k, 0]),
-                (down_in.at[part, :], down.at[part, :], sems.at[k, 1]),
-                (rope_in.at[:, part], rope.at[:, part], sems.at[k, 2]),
-            )
-        )
-    wide, rest = jnp.zeros((SEQ, LATENT), F32), jnp.zeros((SEQ, 64), F32)
-    for k in range(4):
-        wait(chunks[k])
-        part = pl.ds(256 * k, 256)
-        wide = wide + dot(tokens[:, part], down[part, :])
-        rest = rest + dot_nt(tokens[:, part], rope[:, part])
+def start(*pairs):
+    copies = [pltpu.make_async_copy(source, target, sem) for source, target, sem in pairs]
+    for copy in copies:
+        copy.start()
+    return copies
+
+
+def wait(copies):
+    for copy in copies:
+        copy.wait()
+
+
+def entry_kernel(tokens, down, rope, out):
+    wide = dot(tokens[...], down[...])
+    rest = dot_nt(tokens[...], rope[...])
     rest = jnp.concatenate([rest, jnp.zeros_like(rest)], axis=1)
     for k in range(8):
         pack(out, k, 32 * k, wide, rest)
@@ -214,16 +212,18 @@
 
 
 def student_kernel(
-    at, packed, queries_in, key_up_in, value_up_in, teacher_in, cos_part, sin_part, segments,
+    at, packed_in, queries_in, key_up_in, value_up_in, teacher_in, cos_part, sin_part, segments,
     keep_out, send_out, norm_out, latent, rest, nope, head_values, rest_sum, grads,
-    queries, key_up, value_up, teacher, keep, send, norm, sems,
+    packed, queries, key_up, value_up, teacher, keep, send, norm, sems,
 ):
-    (get_keys, get_values, *get_others) = start(
+    (get_packed, get_keys, get_values, *get_others) = start(
+        (packed_in, packed, sems.at[8]),
         (key_up_in, key_up, sems.at[0]),
         (value_up_in, value_up, sems.at[1]),
         (queries_in, queries, sems.at[2]),
         (teacher_in, teacher, sems.at[3]),
     )
+    wait([get_packed])
     unpack(packed, latent, rest)
     cos, sin = part_table(cos_part[...], sin_part[...])
     low = low_lanes(SEQ)
@@ -267,30 +267,56 @@
         ref[:, :256] = grads[:, keys].astype(ref.dtype)
         ref[:, 256:] = grads[:, values].astype(ref.dtype)
     puts = start((send, send_out, sems.at[4]), (keep, keep_out, sems.at[5]))
-    wide = dot_nt(grads[:, :512], key_up[...]) + dot_nt(grads[:, 512:], value_up[...])
-    rest_all = rest_sum[...]
-    for k in range(8):
-        pack(norm, k, 32 * k, wide, rest_all)
-    wait(puts + start((norm, norm_out, sems.at[6])))
-
-
-def up_kernel(at, packed, other_packed, grads, other_grads, *outs):
-    *outs, latent, rest = outs
+    for r in range(2):
+        rows = slice(128 * r, 128 * r + 128)
+        wide = dot_nt(grads[rows, :512], key_up[...]) + dot_nt(grads[rows, 512:], value_up[...])
+        rest_half = rest_sum[rows]
+        for k in range(4):
+            pack(norm, 4 * r + k, 32 * k, wide, rest_half)
+        part = pl.ds(4 * r, 4)
+        puts += start((norm.at[part], norm_out.at[part], sems.at[6 + r]))
+    wait(puts)
+
+
+def up_kernel(at, packed_in, other_packed_in, grads_in, other_grads_in, *refs):
+    *outs, latent, rest, packed, other_packed, grads, other_grads, whole, sems = refs
+    gets = start(
+        (packed_in, packed, sems.at[0]),
+        (grads_in, grads, sems.at[1]),
+        (other_packed_in, other_packed, sems.at[2]),
+        (other_grads_in, other_grads, sems.at[3]),
+    )
+    wait(gets[:1])
     unpack(packed, latent, rest)
-    whole = dot_tn(latent[...], grads[...])
+    wait(gets[1:2])
+    whole[...] = dot_tn(latent[...], grads[...])
+    wait(gets[2:3])
     unpack(other_packed, latent, rest)
-    whole = whole + dot_tn(latent[...], other_grads[...].astype(BF16))
-    for quarter in range(4):
-        for step in range(4):
-            @pl.when((at[1] + step) % 4 == quarter)
-            def _(quarter=quarter, step=step):
-                outs[step][...] = whole[128 * quarter : 128 * quarter + 128]
-
-
-def split_kernel(at, own, first, second, third, *outs):
+    wait(gets[3:])
+    whole[...] += dot_tn(latent[...], other_grads[...].astype(BF16))
+    puts = []
     for step in range(4):
-        rows = pl.ds(pl.multiple_of((at[2] + step) % 4 * 32, 32), 32)
-        outs[step][...] = (own[rows, :] + first[rows, :]) + (second[rows, :] + third[rows, :])
+        rows = pl.ds(pl.multiple_of((at[1] + step) % 4 * 128, 128), 128)
+        puts += start((whole.at[rows, :], outs[step], sems.at[step]))
+    wait(puts)
+
+
+def halves_kernel(own, first, second, third, *outs):
+    n = outs[0].shape[0]
+    for k, out in enumerate(outs):
+        rows = slice(n * k, n * k + n)
+        out[...] = (own[rows] + first[rows]) + (second[rows] + third[rows])
+
+
+def add_kernel(a, b, got_a, got_b, a_out, b_out):
+    a_out[...] = a[...] + got_a[...]
+    b_out[...] = b[...] + got_b[...]
+
+
+def add_stack_kernel(a, b, got_a, got_b, out):
+    n = a.shape[0]
+    out[:n] = a[...] + got_a[...]
+    out[n:] = b[...] + got_b[...]
 
 
 def entry_grad_kernel(at, packed, other_packed, tokens, other_tokens, *refs):
@@ -306,16 +332,6 @@
             pack(outs[step], k, 32 * k, whole[:, :512], whole[:, 512:])
 
 
-def entry_split_kernel(at, own, first, second, third, *outs):
-    for step in range(4):
-        k = (at[2] + step) % 4
-        outs[step][...] = (own[k] + first[k]) + (second[k] + third[k])
-
-
-def entry_sum_kernel(own, first, second, third, out):
-    out[...] = (own[...] + first[...]) + (second[...] + third[...])
-
-
 def up_out_kernel(at, *refs):
     *parts, key_out, value_out = refs
     for c in range(2):
@@ -324,41 +340,30 @@
         values = pl.ds(pl.multiple_of(column * 512, 512), 512)
         for step in range(4):
             ref = parts[4 * c + step]
-            for depth in range(4):
-                block = (at[1] - step + 4) % 4 * 4 + (at[2] - depth + 4) % 4
-                rows = pl.ds(pl.multiple_of(block * 32, 32), 32)
-                key_out[rows, keys] = ref[depth, :, :256]
-                value_out[rows, values] = ref[depth, :, 256:]
-
-
-def entry_out_kernel(own, at, *refs):
-    parts, (down_out, rope_out, down, rope, rest, sems) = refs[:4], refs[-6:]
-    half = at[0] if own else 1 - at[0]
+            rows = pl.ds(pl.multiple_of((at[1] - step + 4) % 4 * 128, 128), 128)
+            key_out[rows, keys] = ref[:, :256]
+            value_out[rows, values] = ref[:, 256:]
+
+
+def entry_out_kernel(blocks, at, *refs):
+    parts, (down_out, rope_out, down, rope, rest, sems) = refs[: len(blocks)], refs[-6:]
     copies = []
-    for step in range(4):
-        first = (at[1] - step + 4) % 4
+    for b, (own, step) in enumerate(blocks):
+        half = at[0] if own else 1 - at[0]
         for depth in range(4):
-            spot = (at[2] - depth + 4) % 4 * 32
-            rows = pl.ds(pl.multiple_of(first * 128 + spot, 32), 32)
             for j in range(4):
-                down[rows, 128 * j : 128 * j + 128] = parts[step][depth, 32 * j : 32 * j + 32, :]
-            value = parts[step][depth, 128:PACKED, :]
-            rest[pl.ds(pl.multiple_of(spot, 32), 16), :] = value
-            rest[pl.ds(pl.multiple_of(spot + 16, 16), 16), :] = pltpu.roll(value, 64, 1)
-        rope[:, lanes(first)] = rest[...].T[:64]
-        group = pl.ds(pl.multiple_of(first * 128, 128), 128)
-        where = pl.ds(pl.multiple_of(half * 512 + first * 128, 128), 128)
+                down[b, 32 * depth : 32 * depth + 32, 128 * j : 128 * j + 128] = parts[b][
+                    depth, 32 * j : 32 * j + 32, :
+                ]
+            unpack_rest(parts[b][depth, 128:PACKED, :], rest, 32 * depth)
+        rope[b] = rest[...].T[:64]
+        first = half * 512 + (at[1] - step + 4) % 4 * 128
+        where = pl.ds(pl.multiple_of(first, 128), 128)
         copies += start(
-            (down.at[group, :], down_out.at[where, :], sems.at[step, 0]),
-            (rope.at[:, group], rope_out.at[:, where], sems.at[step, 1]),
+            (down.at[b], down_out.at[where, :], sems.at[b, 0]),
+            (rope.at[b], rope_out.at[:, where], sems.at[b, 1]),
         )
     wait(copies)
-
-
-def stack_kernel(*refs):
-    *parts, out = refs
-    for k, part in enumerate(parts):
-        out[k] = part[...]
 
 
 def permute(value, move):
@@ -378,8 +383,14 @@
 
 def around(value, axis):
     values = value if isinstance(value, list) else [value] * 3
-    moves = [lambda at, k=k: {axis: (at[axis] + k) % 4} for k in (1, 2, 3)]
-    return [permute(v, move) for v, move in zip(values, moves)]
+    out = []
+    for k in (1, 2, 3):
+        out.append(permute(values[k - 1], lambda at: {axis: (at[axis] + k) % 4}))
+    return out
+
+
+def partners(a, b, masks):
+    return [permute(v, lambda at, m=m: {"h": at["h"] ^ m}) for v, m in zip((a, b), masks)]
 
 
 def exchange(parts):
@@ -407,16 +418,7 @@
     chunks = shape(8, PACKED, 128)
     unpacked = [pltpu.VMEM((SEQ, LATENT), BF16), pltpu.VMEM((SEQ, 128), F32)]
 
-    (part,) = call(
-        entry_kernel, [chunks], tokens, down, rope, hbm=(0, 1, 2),
-        scratch=[
-            pltpu.VMEM((SEQ, 1024), BF16),
-            pltpu.VMEM((1024, LATENT), BF16),
-            pltpu.VMEM((64, 1024), BF16),
-            pltpu.SemaphoreType.DMA((4, 3)),
-        ],
-        flops=2 * 256 * 1024 * 576, mib=60,
-    )
+    (part,) = call(entry_kernel, [chunks], tokens, down, rope, flops=2 * 256 * 1024 * 576, mib=60)
     parts = exchange(part)
     full, partial = tables(segments)
     teacher, tokens_keep, tokens_send = call(
@@ -440,6 +442,7 @@
             pltpu.VMEM((SEQ, 1024), BF16),
             pltpu.VMEM((SEQ, 128), F32),
             pltpu.VMEM((SEQ, 1536), BF16),
+            pltpu.VMEM((8, PACKED, 128), F32),
             pltpu.VMEM((SEQ, 1024), BF16),
             pltpu.VMEM((LATENT, 512), BF16),
             pltpu.VMEM((LATENT, 1024), BF16),
@@ -447,23 +450,32 @@
             pltpu.VMEM((SEQ, 768), BF16),
             pltpu.VMEM((SEQ, 768), F32),
             pltpu.VMEM((8, PACKED, 128), F32),
-            pltpu.SemaphoreType.DMA((7,)),
+            pltpu.SemaphoreType.DMA((9,)),
         ],
-        hbm=(2, 3, 4, 5), hbm_out=True,
+        hbm=(1, 2, 3, 4, 5), hbm_out=True,
         flops=10 * 8 * 256 * 256 * 128, mib=60,
     )
     grads_other = other_core(grads_send)
     parts = exchange(part)
     quarters = call(
         up_kernel, [shape(128, 768)] * 4, at, packed, packed_other, grads_keep, grads_other,
-        scalars=1, scratch=unpacked, flops=2 * 512 * 512 * 768, mib=60,
+        scalars=1, hbm=(1, 2, 3, 4), hbm_out=True,
+        scratch=unpacked + [
+            pltpu.VMEM((8, PACKED, 128), F32),
+            pltpu.VMEM((8, PACKED, 128), F32),
+            pltpu.VMEM((SEQ, 768), BF16),
+            pltpu.VMEM((SEQ, 768), F32),
+            pltpu.VMEM((LATENT, 768), F32),
+            pltpu.SemaphoreType.DMA((4,)),
+        ],
+        flops=2 * 512 * 512 * 768, mib=60,
     )
     received = around(list(quarters[1:]), "x")
     (replicas,) = call(norm_grad_kernel, [chunks], at, parts, normed, inv, *partial, scalars=1)
     packed = exchange(replicas)
     packed_other = other_core(packed)
-    quarters = call(split_kernel, [shape(32, 768)] * 4, at, quarters[0], *received, scalars=1)
-    received = around(list(quarters[1:]), "h")
+    halves = call(halves_kernel, [shape(64, 768)] * 2, quarters[0], *received)
+    received = partners(*halves, (1, 3))
     entries = call(
         entry_grad_kernel, [shape(4, PACKED, 128)] * 4,
         at, packed, packed_other, tokens_keep, tokens_other, scalars=1,
@@ -471,36 +483,41 @@
         flops=2 * 512 * 512 * 640,
     )
     arrived = around(list(entries[1:]), "x")
-    up = (quarters[0] + received[0]) + (received[1] + received[2])
-    (up_all,) = call(stack_kernel, [shape(4, 32, 768)], up, *around(up, "h"))
-    entries = call(
-        entry_split_kernel, [shape(PACKED, 128)] * 4, at, entries[0], *arrived, scalars=1,
-    )
-    arrived = around(list(entries[1:]), "h")
-    received = [up_all] + around(up_all, "x")
-    (entry,) = call(entry_sum_kernel, [shape(PACKED, 128)], entries[0], *arrived)
-    entry = jnp.stack([entry] + around(entry, "h"))
+    halves = call(add_kernel, [shape(64, 768)] * 2, *halves, *received)
+    received = partners(*halves, (3, 1))
+    entry = call(halves_kernel, [shape(2, PACKED, 128)] * 2, entries[0], *arrived)
+    arrived = partners(*entry, (1, 3))
+    (up,) = call(add_stack_kernel, [shape(128, 768)], *halves, *received)
+    received = [up] + around(up, "x")
+    entry = call(add_kernel, [shape(2, PACKED, 128)] * 2, *entry, *arrived)
+    arrived = partners(*entry, (3, 1))
+    (entry,) = call(add_stack_kernel, [shape(4, PACKED, 128)], *entry, *arrived)
     entries = [entry] + around(entry, "x")
     others = [other_core(v) for v in received]
     grad_key, grad_value = call(
         up_out_kernel, [shape(512, 512), shape(512, 1024)], at, *received, *others, scalars=1,
     )
     others = [other_core(v) for v in entries]
-    outs = [shape(1024, 512), shape(64, 1024)]
-    scratch = [
-        pltpu.VMEM((512, 512), F32),
-        pltpu.VMEM((64, 512), F32),
-        pltpu.VMEM((128, 128), F32),
-        pltpu.SemaphoreType.DMA((4, 2)),
-    ]
-    halves = call(
-        functools.partial(entry_out_kernel, True), outs, at, *entries, scalars=1,
-        scratch=scratch, hbm_out=True,
-    )
-    grad_down, grad_rope = call(
-        functools.partial(entry_out_kernel, False), outs, at, *others, *halves, scalars=1,
-        scratch=scratch, hbm_out=True, aliases={5: 0, 6: 1},
-    )
+    done = []
+    for blocks in (
+        ((True, 0), (True, 1), (True, 2), (False, 0), (False, 1)),
+        ((True, 3), (False, 2)),
+        ((False, 3),),
+    ):
+        count = len(blocks)
+        done = call(
+            functools.partial(entry_out_kernel, blocks),
+            [shape(1024, 512), shape(64, 1024)],
+            at, *[(entries if own else others)[k] for own, k in blocks], *done, scalars=1,
+            scratch=[
+                pltpu.VMEM((count, 128, 512), F32),
+                pltpu.VMEM((count, 64, 128), F32),
+                pltpu.VMEM((128, 128), F32),
+                pltpu.SemaphoreType.DMA((count, 2)),
+            ],
+            hbm_out=True, aliases={count + 1: 0, count + 2: 1} if done else None,
+        )
+    grad_down, grad_rope = done
     return grad_down, grad_rope, grad_key, grad_value
 
 

time: 194 us -> 186 us (0.959)
  starting transfers between devices: 73.7 us -> 51.3 us
  waiting for transfers between devices: 63.7 us -> 75.8 us
    ppermute x36 -> x32, starting transfers between devices: 57.9 us -> 35.6 us  [permute(): return lax.ppermute(value, AXES, pairs)]
    all_to_all x3, waiting for transfers between devices: 8.54 us -> 15.9 us  [exchange(): return lax.all_to_all(parts, 'tensor', 0, 0, tiled=True)]
    ppermute x36 -> x32, waiting for transfers between devices: 55.2 us -> 59.9 us  [permute(): return lax.ppermute(value, AXES, pairs)]
    pallas_call x14 -> x17, Pallas kernels: 35.4 us -> 36 us  [call(): pl.pallas_call(body, out_shape=outs, in_specs=specs, out_specs=[anywhere...]
  transfers between devices with their start and end apart: 39 -> 35, of which waited for: 15 -> 14; matrix products, arithmetic and copies ran while one was open for 2% -> 2% of each run, Pallas kernels for 9% -> 10%
where the time goes in v5:
time: 186 us; the launch traced here: 183 us
  waiting for transfers between devices  75.8 us (41%)
  starting transfers between devices  51.3 us (28%)
  Pallas kernels  36 us (19%)
  blocking collectives  13 us (7%)
  other arithmetic  3.35 us (2%)
  local copies, waits for them, and re-layouts  2.9 us (2%)
    ppermute x32, waiting for transfers between devices, permute(): return lax.ppermute(value, AXES, pairs)  59.9 us
    pallas_call x17, Pallas kernels, call(): pl.pallas_call(body, out_shape=outs, in_specs=specs, out_specs=[anywhere...  36 us
    ppermute x32, starting transfers between devices, permute(): return lax.ppermute(value, AXES, pairs)  35.6 us
    all_to_all x3, waiting for transfers between devices, exchange(): return lax.all_to_all(parts, 'tensor', 0, 0, tiled=True)  15.9 us
    all_to_all x3, starting transfers between devices, exchange(): return lax.all_to_all(parts, 'tensor', 0, 0, tiled=True)  15.7 us
    all_to_all x1, blocking collectives, exchange(): return lax.all_to_all(parts, 'tensor', 0, 0, tiled=True)  13 us
  transfers between devices with their start and end apart: 35, of which 14 were waited for; matrix products, arithmetic and copies ran while one was open for 2% of the time, Pallas kernels for 10%

profile of v5, /device:TPU:32, one launch (start us, length us, event | category | flops | bytes accessed | tf_op | source)
XLA Modules:
  0.0 183.3 jit_solution(2323941188102970958)
XLA Ops:
  0.6 2.8 %shard_map.120 = f32[8,144,128]{2,1,0:T(8,128)} custom-call(bf16[256,1024]{1,0:T(8,128)(2,1)} %bitcast.11, bf16[1024,512]{1,0:T(8,128)(2,1)} %down.1, bf16[64,1024]{1,0:T(8,128)(2,1)} %rope.1), custom_call_target="tpu_custom_call" | custom-call | flops 301989888 | bytes 2293760 | tf_op jit(solution)/shard_map/pallas_call | solution.py:49
  3.5 5.9 %all-to-all-start = ((f32[8,144,128]{2,1,0:T(8,128)}), f32[8,144,128]{2,1,0:T(8,128)S(1)}, u32[]{:S(2)}, u32[]{:S(2)}) async-start(f32[8,144,128]{2,1,0:T(8,128)} %shard_map.120), calls=%async_computation | async-start | bytes 1179648 | tf_op jit(solution)/shard_map/all_to_all | solution.py:397
  11.5 6.8 %shard_map.121 = (f32[256,1024]{1,0:T(8,128)}, bf16[512,256]{1,0:T(8,128)(2,1)}, f32[512,256]{1,0:T(8,128)}) custom-call(s32[4]{0:T(128)} %pad_add_fusion.at, bf16[256,1024]{1,0:T(8,128)(2,1)} %bitcast.9, bf16[256,128]{1,0:T(8,128)(2,1)} %bitcast.13, bf16[256,128]{1,0:T(8,128)(2,1)} %bitcast.14, f32[256,64]{1,0:T(8,128)} %get-tuple-element.77.cos_full, ...), custom_call_target="tpu_custom_call" | custom-call | flops 268435456 | bytes 3146768 | tf_op jit(solution)/shard_map/pallas_call | solution.py:49
  20.0 5.0 %all-to-all-start.1 = ((f32[8,144,128]{2,1,0:T(8,128)}), f32[8,144,128]{2,1,0:T(8,128)S(1)}, u32[]{:S(2)}, u32[]{:S(2)}) async-start(f32[8,144,128]{2,1,0:T(8,128)} %get-tuple-element.41), calls=%async_computation.1 | async-start | bytes 1179648 | tf_op jit(solution)/shard_map/all_to_all | solution.py:397
  26.3 7.8 %all-to-all-done.1.packed_in = f32[8,144,128]{2,1,0:T(8,128)S(1)} async-done(((f32[8,144,128]{2,1,0:T(8,128)}), f32[8,144,128]{2,1,0:T(8,128)S(1)}, u32[]{:S(2)}, u32[]{:S(2)}) %all-to-all-start.1) | async-done | bytes 589856 | tf_op jit(solution)/shard_map/all_to_all | solution.py:397
  34.9 11.3 %shard_map.123 = (bf16[256,768]{1,0:T(8,128)(2,1)}, f32[256,768]{1,0:T(8,128)}, f32[8,144,128]{2,1,0:T(8,128)}) custom-call(s32[4]{0:T(128)} %pad_add_fusion.at, f32[8,144,128]{2,1,0:T(8,128)} %copy-done.6, bf16[256,1024]{1,0:T(8,128)(2,1)} %bitcast.10, bf16[512,512]{1,0:T(8,128)(2,1)} %key_up_in.1, bf16[512,1024]{1,0:T(8,128)(2,1)} %value_up_in.1, ...), custom_call_target="tpu_custom_call" | custom-call | flops 671088640 | bytes 5571600 | tf_op jit(solution)/shard_map/pallas_call | solution.py:49
  46.2 13.0 %all_to_all.20.parts = f32[8,144,128]{2,1,0:T(8,128)S(1)} all-to-all(f32[8,144,128]{2,1,0:T(8,128)} %get-tuple-element.43), channel_id=1, replica_groups=mesh['dp'=32,'tensor'=8] {'tensor'}, dimensions={0} | all-to-all | bytes 1179648 | tf_op jit(solution)/shard_map/all_to_all | solution.py:397
  60.8 4.7 %all-to-all-start.3 = ((f32[8,144,128]{2,1,0:T(8,128)}), f32[8,144,128]{2,1,0:T(8,128)S(1)}, u32[]{:S(2)}, u32[]{:S(2)}) async-start(f32[8,144,128]{2,1,0:T(8,128)} %shard_map.124), calls=%async_computation.3 | async-start | bytes 1179648 | tf_op jit(solution)/shard_map/all_to_all | solution.py:397
  66.0 7.4 %all-to-all-done.3.packed = f32[8,144,128]{2,1,0:T(8,128)S(1)} async-done(((f32[8,144,128]{2,1,0:T(8,128)}), f32[8,144,128]{2,1,0:T(8,128)S(1)}, u32[]{:S(2)}, u32[]{:S(2)}) %all-to-all-start.3) | async-done | bytes 589856 | tf_op jit(solution)/shard_map/all_to_all | solution.py:397
  75.0 3.9 %shard_map.132 = (f32[128,768]{1,0:T(8,128)}, f32[128,768]{1,0:T(8,128)}, f32[128,768]{1,0:T(8,128)}, f32[128,768]{1,0:T(8,128)}) custom-call(s32[4]{0:T(128)} %pad_add_fusion.at, f32[8,144,128]{2,1,0:T(8,128)} %copy-done.6, f32[8,144,128]{2,1,0:T(8,128)} %copy-done.9, bf16[256,768]{1,0:T(8,128)(2,1)} %get-tuple-element.62.grads_in, f32[256,768]{1,0:T(8,128)} %copy-done.8), custom_call_target="tpu_custom_call" | custom-call | flops 402653184 | bytes 3932176 | tf_op jit(solution)/shard_map/pallas_call | solution.py:49
  80.4 2.7 %collective-permute-start.19 = (f32[128,768]{1,0:T(8,128)}, f32[128,768]{1,0:T(8,128)S(1)}, u32[]{:S(2)}, u32[]{:S(2)}) collective-permute-start(f32[128,768]{1,0:T(8,128)} %get-tuple-element.66), channel_id=1, source_target_pairs={{0,128},{1,129},{2,130},{3,131},{4,132},{5,133},{6,134},{7,135},{8... | collective-permute-start | bytes 1179656 | tf_op jit(solution)/shard_map/ppermute | solution.py:377
  84.6 6.8 %collective-permute-done.18.first = f32[128,768]{1,0:T(8,128)S(1)} collective-permute-done((f32[128,768]{1,0:T(8,128)}, f32[128,768]{1,0:T(8,128)S(1)}, u32[]{:S(2)}, u32[]{:S(2)}) %collective-permute-start.18) | collective-permute-done | bytes 393248 | tf_op jit(solution)/shard_map/ppermute | solution.py:377
  91.4 9.4 %collective-permute-done.19.second = f32[128,768]{1,0:T(8,128)S(1)} collective-permute-done((f32[128,768]{1,0:T(8,128)}, f32[128,768]{1,0:T(8,128)S(1)}, u32[]{:S(2)}, u32[]{:S(2)}) %collective-permute-start.19) | collective-permute-done | bytes 393248 | tf_op jit(solution)/shard_map/ppermute | solution.py:377
  101.9 3.4 %collective-permute-start.21 = (f32[64,768]{1,0:T(8,128)S(1)}, f32[64,768]{1,0:T(8,128)S(1)}, u32[]{:S(2)}, u32[]{:S(2)}) collective-permute-start(f32[64,768]{1,0:T(8,128)S(1)} %get-tuple-element.68.a), channel_id=1, source_target_pairs={{0,16},{1,17},{2,18},{3,19},{4,20},{5,21},{6,22},{7,23},{8,24},{9,... | collective-permute-start | bytes 589832 | tf_op jit(solution)/shard_map/ppermute | solution.py:377
  105.2 3.6 %collective-permute-start.22 = (f32[64,768]{1,0:T(8,128)S(1)}, f32[64,768]{1,0:T(8,128)S(1)}, u32[]{:S(2)}, u32[]{:S(2)}) collective-permute-start(f32[64,768]{1,0:T(8,128)S(1)} %get-tuple-element.69.b), channel_id=1, source_target_pairs={{0,48},{1,49},{2,50},{3,51},{4,52},{5,53},{6,54},{7,55},{8,56},{9,... | collective-permute-start | bytes 589832 | tf_op jit(solution)/shard_map/ppermute | solution.py:377
  117.3 3.4 %collective-permute-start.23 = (f32[64,768]{1,0:T(8,128)S(1)}, f32[64,768]{1,0:T(8,128)S(1)}, u32[]{:S(2)}, u32[]{:S(2)}) collective-permute-start(f32[64,768]{1,0:T(8,128)S(1)} %get-tuple-element.70.a), channel_id=1, source_target_pairs={{0,48},{1,49},{2,50},{3,51},{4,52},{5,53},{6,54},{7,55},{8,56},{9,... | collective-permute-start | bytes 589832 | tf_op jit(solution)/shard_map/ppermute | solution.py:377
  120.7 7.9 %collective-permute-done.23.got_a = f32[64,768]{1,0:T(8,128)S(1)} collective-permute-done((f32[64,768]{1,0:T(8,128)S(1)}, f32[64,768]{1,0:T(8,128)S(1)}, u32[]{:S(2)}, u32[]{:S(2)}) %collective-permute-start.23) | collective-permute-done | bytes 196640 | tf_op jit(solution)/shard_map/ppermute | solution.py:377
  128.5 3.0 %collective-permute-done.24.got_b = f32[64,768]{1,0:T(8,128)S(1)} collective-permute-done((f32[64,768]{1,0:T(8,128)S(1)}, f32[64,768]{1,0:T(8,128)S(1)}, u32[]{:S(2)}, u32[]{:S(2)}) %collective-permute-start.24) | collective-permute-done | bytes 196640 | tf_op jit(solution)/shard_map/ppermute | solution.py:377
  133.2 3.1 %collective-permute-start.26 = (f32[128,768]{1,0:T(8,128)S(1)}, f32[128,768]{1,0:T(8,128)S(1)}, u32[]{:S(2)}, u32[]{:S(2)}) collective-permute-start(f32[128,768]{1,0:T(8,128)S(1)} %shard_map.135.refs_0_), channel_id=1, source_target_pairs={{0,128},{1,129},{2,130},{3,131},{4,132},{5,133},{6,134},{7,135},{8... | collective-permute-start | bytes 1179656 | tf_op jit(solution)/shard_map/ppermute | solution.py:377
  138.6 7.0 %collective-permute-done.5.got_a = f32[2,144,128]{2,1,0:T(8,128)S(1)} collective-permute-done((f32[2,144,128]{2,1,0:T(8,128)S(1)}, f32[2,144,128]{2,1,0:T(8,128)S(1)}, u32[]{:S(2)}, u32[]{:S(2)}) %collective-permute-start.5) | collective-permute-done | bytes 147488 | tf_op jit(solution)/shard_map/ppermute | solution.py:377
  147.5 5.2 %collective-permute-done.26.refs_2_ = f32[128,768]{1,0:T(8,128)S(1)} collective-permute-done((f32[128,768]{1,0:T(8,128)S(1)}, f32[128,768]{1,0:T(8,128)S(1)}, u32[]{:S(2)}, u32[]{:S(2)}) %collective-permute-start.26) | collective-permute-done | bytes 393248 | tf_op jit(solution)/shard_map/ppermute | solution.py:377
  152.6 4.7 %collective-permute-done.7.got_a = f32[2,144,128]{2,1,0:T(8,128)S(1)} collective-permute-done((f32[2,144,128]{2,1,0:T(8,128)S(1)}, f32[2,144,128]{2,1,0:T(8,128)S(1)}, u32[]{:S(2)}, u32[]{:S(2)}) %collective-permute-start.7) | collective-permute-done | bytes 147488 | tf_op jit(solution)/shard_map/ppermute | solution.py:377
  160.6 2.7 %collective-permute-start.9 = (f32[4,144,128]{2,1,0:T(8,128)S(1)}, f32[4,144,128]{2,1,0:T(8,128)S(1)}, u32[]{:S(2)}, u32[]{:S(2)}) collective-permute-start(f32[4,144,128]{2,1,0:T(8,128)S(1)} %shard_map.128.refs_0_), channel_id=1, source_target_pairs={{0,192},{1,193},{2,194},{3,195},{4,196},{5,197},{6,198},{7,199},{8... | collective-permute-start | bytes 884744 | tf_op jit(solution)/shard_map/ppermute | solution.py:377
  163.8 11.6 %collective-permute-done.13.refs_1_ = f32[4,144,128]{2,1,0:T(8,128)S(1)} collective-permute-done((f32[4,144,128]{2,1,0:T(8,128)S(1)}, f32[4,144,128]{2,1,0:T(8,128)S(1)}, u32[]{:S(2)}, u32[]{:S(2)}) %collective-permute-start.13) | collective-permute-done | bytes 294944 | tf_op jit(solution)/shard_map/ppermute | solution.py:377
  (93 shorter events, 39.2 us)
Async XLA Ops:
  3.5 15.5 %all-to-all-start = ((f32[8,144,128]{2,1,0:T(8,128)}), f32[8,144,128]{2,1,0:T(8,128)S(1)}, u32[]{:S(2)}, u32[]{:S(2)}) async-start(f32[8,144,128]{2,1,0:T(8,128)} %shard_map.120), calls=%async_computation | async-start | bytes 1179648 | tf_op jit(solution)/shard_map/all_to_all | solution.py:397
  20.0 14.1 %all-to-all-start.1 = ((f32[8,144,128]{2,1,0:T(8,128)}), f32[8,144,128]{2,1,0:T(8,128)S(1)}, u32[]{:S(2)}, u32[]{:S(2)}) async-start(f32[8,144,128]{2,1,0:T(8,128)} %get-tuple-element.41), calls=%async_computation.1 | async-start | bytes 1179648 | tf_op jit(solution)/shard_map/all_to_all | solution.py:397
  60.8 12.6 %all-to-all-start.3 = ((f32[8,144,128]{2,1,0:T(8,128)}), f32[8,144,128]{2,1,0:T(8,128)S(1)}, u32[]{:S(2)}, u32[]{:S(2)}) async-start(f32[8,144,128]{2,1,0:T(8,128)} %shard_map.124), calls=%async_computation.3 | async-start | bytes 1179648 | tf_op jit(solution)/shard_map/all_to_all | solution.py:397
  73.4 35.4 %collective-permute-start = (f32[8,144,128]{2,1,0:T(8,128)S(1)}, f32[8,144,128]{2,1,0:T(8,128)S(1)}, u32[]{:S(2)}, u32[]{:S(2)}) collective-permute-start(f32[8,144,128]{2,1,0:T(8,128)S(1)} %all-to-all-done.3.packed), channel_id=1, source_target_pairs={{0,8},{1,9},{2,10},{3,11},{4,12},{5,13},{6,14},{7,15},{8,0},{9,1},... | collective-permute-start | bytes 1769480 | tf_op jit(solution)/shard_map/ppermute | solution.py:377
  73.4 35.4 %collective-permute-start.1 = (f32[512,256]{1,0:T(8,128)}, f32[512,256]{1,0:T(8,128)S(1)}, u32[]{:S(2)}, u32[]{:S(2)}) collective-permute-start(f32[512,256]{1,0:T(8,128)} %get-tuple-element.47), channel_id=1, source_target_pairs={{0,8},{1,9},{2,10},{3,11},{4,12},{5,13},{6,14},{7,15},{8,0},{9,1},... | collective-permute-start | bytes 1572872 | tf_op jit(solution)/shard_map/ppermute | solution.py:377
  78.9 12.5 %collective-permute-start.18 = (f32[128,768]{1,0:T(8,128)}, f32[128,768]{1,0:T(8,128)S(1)}, u32[]{:S(2)}, u32[]{:S(2)}) collective-permute-start(f32[128,768]{1,0:T(8,128)} %get-tuple-element.65), channel_id=1, source_target_pairs={{0,64},{1,65},{2,66},{3,67},{4,68},{5,69},{6,70},{7,71},{8,72},{9,... | collective-permute-start | bytes 1179656 | tf_op jit(solution)/shard_map/ppermute | solution.py:377
  80.4 20.4 %collective-permute-start.19 = (f32[128,768]{1,0:T(8,128)}, f32[128,768]{1,0:T(8,128)S(1)}, u32[]{:S(2)}, u32[]{:S(2)}) collective-permute-start(f32[128,768]{1,0:T(8,128)} %get-tuple-element.66), channel_id=1, source_target_pairs={{0,128},{1,129},{2,130},{3,131},{4,132},{5,133},{6,134},{7,135},{8... | collective-permute-start | bytes 1179656 | tf_op jit(solution)/shard_map/ppermute | solution.py:377
  83.2 17.6 %collective-permute-start.20 = (f32[128,768]{1,0:T(8,128)}, f32[128,768]{1,0:T(8,128)S(1)}, u32[]{:S(2)}, u32[]{:S(2)}) collective-permute-start(f32[128,768]{1,0:T(8,128)} %get-tuple-element.67), channel_id=1, source_target_pairs={{0,192},{1,193},{2,194},{3,195},{4,196},{5,197},{6,198},{7,199},{8... | collective-permute-start | bytes 1179656 | tf_op jit(solution)/shard_map/ppermute | solution.py:377
  101.9 13.6 %collective-permute-start.21 = (f32[64,768]{1,0:T(8,128)S(1)}, f32[64,768]{1,0:T(8,128)S(1)}, u32[]{:S(2)}, u32[]{:S(2)}) collective-permute-start(f32[64,768]{1,0:T(8,128)S(1)} %get-tuple-element.68.a), channel_id=1, source_target_pairs={{0,16},{1,17},{2,18},{3,19},{4,20},{5,21},{6,22},{7,23},{8,24},{9,... | collective-permute-start | bytes 589832 | tf_op jit(solution)/shard_map/ppermute | solution.py:377
  105.2 12.0 %collective-permute-start.22 = (f32[64,768]{1,0:T(8,128)S(1)}, f32[64,768]{1,0:T(8,128)S(1)}, u32[]{:S(2)}, u32[]{:S(2)}) collective-permute-start(f32[64,768]{1,0:T(8,128)S(1)} %get-tuple-element.69.b), channel_id=1, source_target_pairs={{0,48},{1,49},{2,50},{3,51},{4,52},{5,53},{6,54},{7,55},{8,56},{9,... | collective-permute-start | bytes 589832 | tf_op jit(solution)/shard_map/ppermute | solution.py:377
  110.1 26.2 %collective-permute-start.2 = (f32[4,144,128]{2,1,0:T(8,128)S(1)}, f32[4,144,128]{2,1,0:T(8,128)S(1)}, u32[]{:S(2)}, u32[]{:S(2)}) collective-permute-start(f32[4,144,128]{2,1,0:T(8,128)S(1)} %get-tuple-element.49), channel_id=1, source_target_pairs={{0,64},{1,65},{2,66},{3,67},{4,68},{5,69},{6,70},{7,71},{8,72},{9,... | collective-permute-start | bytes 884744 | tf_op jit(solution)/shard_map/ppermute | solution.py:377
  111.5 24.8 %collective-permute-start.3 = (f32[4,144,128]{2,1,0:T(8,128)S(1)}, f32[4,144,128]{2,1,0:T(8,128)S(1)}, u32[]{:S(2)}, u32[]{:S(2)}) collective-permute-start(f32[4,144,128]{2,1,0:T(8,128)S(1)} %get-tuple-element.50), channel_id=1, source_target_pairs={{0,128},{1,129},{2,130},{3,131},{4,132},{5,133},{6,134},{7,135},{8... | collective-permute-start | bytes 884744 | tf_op jit(solution)/shard_map/ppermute | solution.py:377
  113.9 22.4 %collective-permute-start.4 = (f32[4,144,128]{2,1,0:T(8,128)S(1)}, f32[4,144,128]{2,1,0:T(8,128)S(1)}, u32[]{:S(2)}, u32[]{:S(2)}) collective-permute-start(f32[4,144,128]{2,1,0:T(8,128)S(1)} %get-tuple-element.51), channel_id=1, source_target_pairs={{0,192},{1,193},{2,194},{3,195},{4,196},{5,197},{6,198},{7,199},{8... | collective-permute-start | bytes 884744 | tf_op jit(solution)/shard_map/ppermute | solution.py:377
  131.6 15.9 %collective-permute-start.25 = (f32[128,768]{1,0:T(8,128)S(1)}, f32[128,768]{1,0:T(8,128)S(1)}, u32[]{:S(2)}, u32[]{:S(2)}) collective-permute-start(f32[128,768]{1,0:T(8,128)S(1)} %shard_map.135.refs_0_), channel_id=1, source_target_pairs={{0,64},{1,65},{2,66},{3,67},{4,68},{5,69},{6,70},{7,71},{8,72},{9,... | collective-permute-start | bytes 1179656 | tf_op jit(solution)/shard_map/ppermute | solution.py:377
  133.2 19.5 %collective-permute-start.26 = (f32[128,768]{1,0:T(8,128)S(1)}, f32[128,768]{1,0:T(8,128)S(1)}, u32[]{:S(2)}, u32[]{:S(2)}) collective-permute-start(f32[128,768]{1,0:T(8,128)S(1)} %shard_map.135.refs_0_), channel_id=1, source_target_pairs={{0,128},{1,129},{2,130},{3,131},{4,132},{5,133},{6,134},{7,135},{8... | collective-permute-start | bytes 1179656 | tf_op jit(solution)/shard_map/ppermute | solution.py:377
  138.1 21.9 %collective-permute-start.27 = (f32[128,768]{1,0:T(8,128)S(1)}, f32[128,768]{1,0:T(8,128)S(1)}, u32[]{:S(2)}, u32[]{:S(2)}) collective-permute-start(f32[128,768]{1,0:T(8,128)S(1)} %shard_map.135.refs_0_), channel_id=1, source_target_pairs={{0,192},{1,193},{2,194},{3,195},{4,196},{5,197},{6,198},{7,199},{8... | collective-permute-start | bytes 1179656 | tf_op jit(solution)/shard_map/ppermute | solution.py:377
  145.6 15.0 %collective-permute-start.28 = (f32[128,768]{1,0:T(8,128)S(1)}, f32[128,768]{1,0:T(8,128)S(1)}, u32[]{:S(2)}, u32[]{:S(2)}) collective-permute-start(f32[128,768]{1,0:T(8,128)S(1)} %shard_map.135.refs_0_), channel_id=1, source_target_pairs={{0,8},{1,9},{2,10},{3,11},{4,12},{5,13},{6,14},{7,15},{8,0},{9,1},... | collective-permute-start | bytes 1179656 | tf_op jit(solution)/shard_map/ppermute | solution.py:377
  145.7 11.7 %collective-permute-start.7 = (f32[2,144,128]{2,1,0:T(8,128)S(1)}, f32[2,144,128]{2,1,0:T(8,128)S(1)}, u32[]{:S(2)}, u32[]{:S(2)}) collective-permute-start(f32[2,144,128]{2,1,0:T(8,128)S(1)} %get-tuple-element.54.a), channel_id=1, source_target_pairs={{0,48},{1,49},{2,50},{3,51},{4,52},{5,53},{6,54},{7,55},{8,56},{9,... | collective-permute-start | bytes 442376 | tf_op jit(solution)/shard_map/ppermute | solution.py:377
  147.5 15.8 %collective-permute-start.29 = (f32[128,768]{1,0:T(8,128)S(1)}, f32[128,768]{1,0:T(8,128)S(1)}, u32[]{:S(2)}, u32[]{:S(2)}) collective-permute-start(f32[128,768]{1,0:T(8,128)S(1)} %collective-permute-done.25.refs_1_), channel_id=1, source_target_pairs={{0,8},{1,9},{2,10},{3,11},{4,12},{5,13},{6,14},{7,15},{8,0},{9,1},... | collective-permute-start | bytes 1179656 | tf_op jit(solution)/shard_map/ppermute | solution.py:377
  159.9 15.5 %collective-permute-start.13 = (f32[4,144,128]{2,1,0:T(8,128)S(1)}, f32[4,144,128]{2,1,0:T(8,128)S(1)}, u32[]{:S(2)}, u32[]{:S(2)}) collective-permute-start(f32[4,144,128]{2,1,0:T(8,128)S(1)} %shard_map.128.refs_0_), channel_id=1, source_target_pairs={{0,64},{1,65},{2,66},{3,67},{4,68},{5,69},{6,70},{7,71},{8,72},{9,... | collective-permute-start | bytes 884744 | tf_op jit(solution)/shard_map/ppermute | solution.py:377
  160.0 15.4 %collective-permute-start.11 = (f32[4,144,128]{2,1,0:T(8,128)S(1)}, f32[4,144,128]{2,1,0:T(8,128)S(1)}, u32[]{:S(2)}, u32[]{:S(2)}) collective-permute-start(f32[4,144,128]{2,1,0:T(8,128)S(1)} %shard_map.128.refs_0_), channel_id=1, source_target_pairs={{0,128},{1,129},{2,130},{3,131},{4,132},{5,133},{6,134},{7,135},{8... | collective-permute-start | bytes 884744 | tf_op jit(solution)/shard_map/ppermute | solution.py:377
  160.6 15.4 %collective-permute-start.9 = (f32[4,144,128]{2,1,0:T(8,128)S(1)}, f32[4,144,128]{2,1,0:T(8,128)S(1)}, u32[]{:S(2)}, u32[]{:S(2)}) collective-permute-start(f32[4,144,128]{2,1,0:T(8,128)S(1)} %shard_map.128.refs_0_), channel_id=1, source_target_pairs={{0,192},{1,193},{2,194},{3,195},{4,196},{5,197},{6,198},{7,199},{8... | collective-permute-start | bytes 884744 | tf_op jit(solution)/shard_map/ppermute | solution.py:377
  163.3 12.7 %collective-permute-start.31 = (f32[128,768]{1,0:T(8,128)S(1)}, f32[128,768]{1,0:T(8,128)S(1)}, u32[]{:S(2)}, u32[]{:S(2)}) collective-permute-start(f32[128,768]{1,0:T(8,128)S(1)} %collective-permute-done.27.refs_3_), channel_id=1, source_target_pairs={{0,8},{1,9},{2,10},{3,11},{4,12},{5,13},{6,14},{7,15},{8,0},{9,1},... | collective-permute-start | bytes 1179656 | tf_op jit(solution)/shard_map/ppermute | solution.py:377
  163.3 15.2 %collective-permute-start.14 = (f32[4,144,128]{2,1,0:T(8,128)S(1)}, f32[4,144,128]{2,1,0:T(8,128)S(1)}, u32[]{:S(2)}, u32[]{:S(2)}) collective-permute-start(f32[4,144,128]{2,1,0:T(8,128)S(1)} %shard_map.128.refs_0_), channel_id=1, source_target_pairs={{0,8},{1,9},{2,10},{3,11},{4,12},{5,13},{6,14},{7,15},{8,0},{9,1},... | collective-permute-start | bytes 884744 | tf_op jit(solution)/shard_map/ppermute | solution.py:377
  (22 other events, 276.1 us)

commit v6 on v4

--- a/solution.py
+++ b/solution.py
@@ -107,23 +107,9 @@
         copy.wait()
 
 
-def entry_kernel(tokens_in, down_in, rope_in, out, tokens, down, rope, sems):
-    chunks = []
-    for k in range(4):
-        part = pl.ds(256 * k, 256)
-        chunks.append(
-            start(
-                (tokens_in.at[:, part], tokens.at[:, part], sems.at[k, 0]),
-                (down_in.at[part, :], down.at[part, :], sems.at[k, 1]),
-                (rope_in.at[:, part], rope.at[:, part], sems.at[k, 2]),
-            )
-        )
-    wide, rest = jnp.zeros((SEQ, LATENT), F32), jnp.zeros((SEQ, 64), F32)
-    for k in range(4):
-        wait(chunks[k])
-        part = pl.ds(256 * k, 256)
-        wide = wide + dot(tokens[:, part], down[part, :])
-        rest = rest + dot_nt(tokens[:, part], rope[:, part])
+def entry_kernel(tokens, down, rope, out):
+    wide = dot(tokens[...], down[...])
+    rest = dot_nt(tokens[...], rope[...])
     rest = jnp.concatenate([rest, jnp.zeros_like(rest)], axis=1)
     for k in range(8):
         pack(out, k, 32 * k, wide, rest)
@@ -265,7 +251,8 @@
         keys = pl.ds(pl.multiple_of(c * 256, 256), 256)
         values = pl.ds(pl.multiple_of(512 + c * 512, 512), 512)
         ref[:, :256] = grads[:, keys].astype(ref.dtype)
-        ref[:, 256:] = grads[:, values].astype(ref.dtype)
+        ref[:, 256:768] = grads[:, values].astype(ref.dtype)
+        ref[:, 768:] = latent[...].astype(ref.dtype)
     puts = start((send, send_out, sems.at[4]), (keep, keep_out, sems.at[5]))
     wide = dot_nt(grads[:, :512], key_up[...]) + dot_nt(grads[:, 512:], value_up[...])
     rest_all = rest_sum[...]
@@ -274,12 +261,9 @@
     wait(puts + start((norm, norm_out, sems.at[6])))
 
 
-def up_kernel(at, packed, other_packed, grads, other_grads, *outs):
-    *outs, latent, rest = outs
-    unpack(packed, latent, rest)
-    whole = dot_tn(latent[...], grads[...])
-    unpack(other_packed, latent, rest)
-    whole = whole + dot_tn(latent[...], other_grads[...].astype(BF16))
+def up_kernel(at, own, other, *outs):
+    whole = dot_tn(own[:, 768:], own[:, :768])
+    whole = whole + dot_tn(other[:, 768:].astype(BF16), other[:, :768].astype(BF16))
     for quarter in range(4):
         for step in range(4):
             @pl.when((at[1] + step) % 4 == quarter)
@@ -287,10 +271,22 @@
                 outs[step][...] = whole[128 * quarter : 128 * quarter + 128]
 
 
-def split_kernel(at, own, first, second, third, *outs):
-    for step in range(4):
-        rows = pl.ds(pl.multiple_of((at[2] + step) % 4 * 32, 32), 32)
-        outs[step][...] = (own[rows, :] + first[rows, :]) + (second[rows, :] + third[rows, :])
+def halves_kernel(own, first, second, third, *outs):
+    n = outs[0].shape[0]
+    for k, out in enumerate(outs):
+        rows = slice(n * k, n * k + n)
+        out[...] = (own[rows] + first[rows]) + (second[rows] + third[rows])
+
+
+def add_kernel(a, b, got_a, got_b, a_out, b_out):
+    a_out[...] = a[...] + got_a[...]
+    b_out[...] = b[...] + got_b[...]
+
+
+def add_stack_kernel(a, b, got_a, got_b, out):
+    n = a.shape[0]
+    out[:n] = a[...] + got_a[...]
+    out[n:] = b[...] + got_b[...]
 
 
 def entry_grad_kernel(at, packed, other_packed, tokens, other_tokens, *refs):
@@ -306,16 +302,6 @@
             pack(outs[step], k, 32 * k, whole[:, :512], whole[:, 512:])
 
 
-def entry_split_kernel(at, own, first, second, third, *outs):
-    for step in range(4):
-        k = (at[2] + step) % 4
-        outs[step][...] = (own[k] + first[k]) + (second[k] + third[k])
-
-
-def entry_sum_kernel(own, first, second, third, out):
-    out[...] = (own[...] + first[...]) + (second[...] + third[...])
-
-
 def up_out_kernel(at, *refs):
     *parts, key_out, value_out = refs
     for c in range(2):
@@ -324,11 +310,9 @@
         values = pl.ds(pl.multiple_of(column * 512, 512), 512)
         for step in range(4):
             ref = parts[4 * c + step]
-            for depth in range(4):
-                block = (at[1] - step + 4) % 4 * 4 + (at[2] - depth + 4) % 4
-                rows = pl.ds(pl.multiple_of(block * 32, 32), 32)
-                key_out[rows, keys] = ref[depth, :, :256]
-                value_out[rows, values] = ref[depth, :, 256:]
+            rows = pl.ds(pl.multiple_of((at[1] - step + 4) % 4 * 128, 128), 128)
+            key_out[rows, keys] = ref[:, :256]
+            value_out[rows, values] = ref[:, 256:]
 
 
 def entry_out_kernel(own, at, *refs):
@@ -338,13 +322,12 @@
     for step in range(4):
         first = (at[1] - step + 4) % 4
         for depth in range(4):
-            spot = (at[2] - depth + 4) % 4 * 32
+            spot = depth * 32
             rows = pl.ds(pl.multiple_of(first * 128 + spot, 32), 32)
             for j in range(4):
                 down[rows, 128 * j : 128 * j + 128] = parts[step][depth, 32 * j : 32 * j + 32, :]
             value = parts[step][depth, 128:PACKED, :]
-            rest[pl.ds(pl.multiple_of(spot, 32), 16), :] = value
-            rest[pl.ds(pl.multiple_of(spot + 16, 16), 16), :] = pltpu.roll(value, 64, 1)
+            unpack_rest(value, rest, spot)
         rope[:, lanes(first)] = rest[...].T[:64]
         group = pl.ds(pl.multiple_of(first * 128, 128), 128)
         where = pl.ds(pl.multiple_of(half * 512 + first * 128, 128), 128)
@@ -353,12 +336,6 @@
             (rope.at[:, group], rope_out.at[:, where], sems.at[step, 1]),
         )
     wait(copies)
-
-
-def stack_kernel(*refs):
-    *parts, out = refs
-    for k, part in enumerate(parts):
-        out[k] = part[...]
 
 
 def permute(value, move):
@@ -382,6 +359,10 @@
     return [permute(v, move) for v, move in zip(values, moves)]
 
 
+def partners(a, b, masks):
+    return [permute(v, lambda at, m=m: {"h": at["h"] ^ m}) for v, m in zip((a, b), masks)]
+
+
 def exchange(parts):
     return lax.all_to_all(parts, "tensor", 0, 0, tiled=True)
 
@@ -407,16 +388,7 @@
     chunks = shape(8, PACKED, 128)
     unpacked = [pltpu.VMEM((SEQ, LATENT), BF16), pltpu.VMEM((SEQ, 128), F32)]
 
-    (part,) = call(
-        entry_kernel, [chunks], tokens, down, rope, hbm=(0, 1, 2),
-        scratch=[
-            pltpu.VMEM((SEQ, 1024), BF16),
-            pltpu.VMEM((1024, LATENT), BF16),
-            pltpu.VMEM((64, 1024), BF16),
-            pltpu.SemaphoreType.DMA((4, 3)),
-        ],
-        flops=2 * 256 * 1024 * 576, mib=60,
-    )
+    (part,) = call(entry_kernel, [chunks], tokens, down, rope, flops=2 * 256 * 1024 * 576, mib=60)
     parts = exchange(part)
     full, partial = tables(segments)
     teacher, tokens_keep, tokens_send = call(
@@ -429,10 +401,9 @@
     parts, teacher = lax.optimization_barrier((parts, teacher))
     replicas, normed, inv = call(norm_kernel, [chunks, shape(128, 128), shape(32, 128)], parts)
     packed = exchange(replicas)
-    packed_other = other_core(packed)
     grads_keep, grads_send, part = call(
         student_kernel,
-        [shape(SEQ, 768, dtype=BF16), shape(SEQ, 768), chunks],
+        [shape(SEQ, 1280, dtype=BF16), shape(SEQ, 1280), chunks],
         at, packed, queries, key_up, value_up, teacher, *partial, seg_row,
         scalars=1,
         scratch=unpacked + [
@@ -444,8 +415,8 @@
             pltpu.VMEM((LATENT, 512), BF16),
             pltpu.VMEM((LATENT, 1024), BF16),
             pltpu.VMEM((SEQ, 1024), F32),
-            pltpu.VMEM((SEQ, 768), BF16),
-            pltpu.VMEM((SEQ, 768), F32),
+            pltpu.VMEM((SEQ, 1280), BF16),
+            pltpu.VMEM((SEQ, 1280), F32),
             pltpu.VMEM((8, PACKED, 128), F32),
             pltpu.SemaphoreType.DMA((7,)),
         ],
@@ -455,15 +426,15 @@
     grads_other = other_core(grads_send)
     parts = exchange(part)
     quarters = call(
-        up_kernel, [shape(128, 768)] * 4, at, packed, packed_other, grads_keep, grads_other,
-        scalars=1, scratch=unpacked, flops=2 * 512 * 512 * 768, mib=60,
+        up_kernel, [shape(128, 768)] * 4, at, grads_keep, grads_other,
+        scalars=1, flops=2 * 512 * 512 * 768, mib=60,
     )
     received = around(list(quarters[1:]), "x")
     (replicas,) = call(norm_grad_kernel, [chunks], at, parts, normed, inv, *partial, scalars=1)
     packed = exchange(replicas)
     packed_other = other_core(packed)
-    quarters = call(split_kernel, [shape(32, 768)] * 4, at, quarters[0], *received, scalars=1)
-    received = around(list(quarters[1:]), "h")
+    halves = call(halves_kernel, [shape(64, 768)] * 2, quarters[0], *received)
+    received = partners(*halves, (1, 3))
     entries = call(
         entry_grad_kernel, [shape(4, PACKED, 128)] * 4,
         at, packed, packed_other, tokens_keep, tokens_other, scalars=1,
@@ -471,15 +442,15 @@
         flops=2 * 512 * 512 * 640,
     )
     arrived = around(list(entries[1:]), "x")
-    up = (quarters[0] + received[0]) + (received[1] + received[2])
-    (up_all,) = call(stack_kernel, [shape(4, 32, 768)], up, *around(up, "h"))
-    entries = call(
-        entry_split_kernel, [shape(PACKED, 128)] * 4, at, entries[0], *arrived, scalars=1,
-    )
-    arrived = around(list(entries[1:]), "h")
-    received = [up_all] + around(up_all, "x")
-    (entry,) = call(entry_sum_kernel, [shape(PACKED, 128)], entries[0], *arrived)
-    entry = jnp.stack([entry] + around(entry, "h"))
+    halves = call(add_kernel, [shape(64, 768)] * 2, *halves, *received)
+    received = partners(*halves, (3, 1))
+    entry = call(halves_kernel, [shape(2, PACKED, 128)] * 2, entries[0], *arrived)
+    arrived = partners(*entry, (1, 3))
+    (up,) = call(add_stack_kernel, [shape(128, 768)], *halves, *received)
+    received = [up] + around(up, "x")
+    entry = call(add_kernel, [shape(2, PACKED, 128)] * 2, *entry, *arrived)
+    arrived = partners(*entry, (3, 1))
+    (entry,) = call(add_stack_kernel, [shape(4, PACKED, 128)], *entry, *arrived)
     entries = [entry] + around(entry, "x")
     others = [other_core(v) for v in received]
     grad_key, grad_value = call(

time: 194 us -> 182 us (0.938)
  starting transfers between devices: 73.7 us -> 51.4 us
  waiting for transfers between devices: 63.7 us -> 76.1 us
  Pallas kernels: 35.4 us -> 33.4 us
    ppermute x36 -> x31, starting transfers between devices: 57.9 us -> 35.7 us  [permute(): return lax.ppermute(value, AXES, pairs)]
    all_to_all x3, waiting for transfers between devices: 8.54 us -> 16.8 us  [exchange(): return lax.all_to_all(parts, 'tensor', 0, 0, tiled=True)]
    ppermute x36 -> x31, waiting for transfers between devices: 55.2 us -> 59.4 us  [permute(): return lax.ppermute(value, AXES, pairs)]
    pallas_call x14 -> x16, Pallas kernels: 35.4 us -> 33.4 us  [call(): pl.pallas_call(body, out_shape=outs, in_specs=specs, out_specs=[anywhere...]
  transfers between devices with their start and end apart: 39 -> 34, of which waited for: 15 -> 14; matrix products, arithmetic and copies ran while one was open for 2% -> 2% of each run, Pallas kernels for 9% -> 9%
where the time goes in v6:
time: 182 us; the launch traced here: 180 us
  waiting for transfers between devices  76.1 us (42%)
  starting transfers between devices  51.4 us (28%)
  Pallas kernels  33.4 us (18%)
  blocking collectives  11.7 us (6%)
  other arithmetic  3.32 us (2%)
  local copies, waits for them, and re-layouts  2.92 us (2%)
    ppermute x31, waiting for transfers between devices, permute(): return lax.ppermute(value, AXES, pairs)  59.4 us
    ppermute x31, starting transfers between devices, permute(): return lax.ppermute(value, AXES, pairs)  35.7 us
    pallas_call x16, Pallas kernels, call(): pl.pallas_call(body, out_shape=outs, in_specs=specs, out_specs=[anywhere...  33.4 us
    all_to_all x3, waiting for transfers between devices, exchange(): return lax.all_to_all(parts, 'tensor', 0, 0, tiled=True)  16.8 us
    all_to_all x3, starting transfers between devices, exchange(): return lax.all_to_all(parts, 'tensor', 0, 0, tiled=True)  15.6 us
    all_to_all x1, blocking collectives, exchange(): return lax.all_to_all(parts, 'tensor', 0, 0, tiled=True)  11.7 us
  transfers between devices with their start and end apart: 34, of which 14 were waited for; matrix products, arithmetic and copies ran while one was open for 2% of the time, Pallas kernels for 9%

profile of v6, /device:TPU:32, one launch (start us, length us, event | category | flops | bytes accessed | tf_op | source)
XLA Modules:
  0.0 179.9 jit_solution(10430939906797887180)
XLA Ops:
  0.6 2.8 %shard_map.120 = f32[8,144,128]{2,1,0:T(8,128)} custom-call(bf16[256,1024]{1,0:T(8,128)(2,1)} %bitcast.11, bf16[1024,512]{1,0:T(8,128)(2,1)} %down.1, bf16[64,1024]{1,0:T(8,128)(2,1)} %rope.1), custom_call_target="tpu_custom_call" | custom-call | flops 301989888 | bytes 2293760 | tf_op jit(solution)/shard_map/pallas_call | solution.py:49
  3.5 5.9 %all-to-all-start = ((f32[8,144,128]{2,1,0:T(8,128)}), f32[8,144,128]{2,1,0:T(8,128)S(1)}, u32[]{:S(2)}, u32[]{:S(2)}) async-start(f32[8,144,128]{2,1,0:T(8,128)} %shard_map.120), calls=%async_computation | async-start | bytes 1179648 | tf_op jit(solution)/shard_map/all_to_all | solution.py:367
  11.5 6.8 %shard_map.121 = (f32[256,1024]{1,0:T(8,128)}, bf16[512,256]{1,0:T(8,128)(2,1)}, f32[512,256]{1,0:T(8,128)}) custom-call(s32[4]{0:T(128)} %pad_add_fusion.at, bf16[256,1024]{1,0:T(8,128)(2,1)} %bitcast.9, bf16[256,128]{1,0:T(8,128)(2,1)} %bitcast.13, bf16[256,128]{1,0:T(8,128)(2,1)} %bitcast.14, f32[256,64]{1,0:T(8,128)} %get-tuple-element.73.cos_full, ...), custom_call_target="tpu_custom_call" | custom-call | flops 268435456 | bytes 3146768 | tf_op jit(solution)/shard_map/pallas_call | solution.py:49
  20.0 5.0 %all-to-all-start.1 = ((f32[8,144,128]{2,1,0:T(8,128)}), f32[8,144,128]{2,1,0:T(8,128)S(1)}, u32[]{:S(2)}, u32[]{:S(2)}) async-start(f32[8,144,128]{2,1,0:T(8,128)} %get-tuple-element.39), calls=%async_computation.1 | async-start | bytes 1179648 | tf_op jit(solution)/shard_map/all_to_all | solution.py:367
  26.2 7.8 %all-to-all-done.1.packed = f32[8,144,128]{2,1,0:T(8,128)S(1)} async-done(((f32[8,144,128]{2,1,0:T(8,128)}), f32[8,144,128]{2,1,0:T(8,128)S(1)}, u32[]{:S(2)}, u32[]{:S(2)}) %all-to-all-start.1) | async-done | bytes 589856 | tf_op jit(solution)/shard_map/all_to_all | solution.py:367
  34.9 11.1 %shard_map.123 = (bf16[256,1280]{1,0:T(8,128)(2,1)}, f32[256,1280]{1,0:T(8,128)}, f32[8,144,128]{2,1,0:T(8,128)}) custom-call(s32[4]{0:T(128)} %pad_add_fusion.at, f32[8,144,128]{2,1,0:T(8,128)} %copy-done.6, bf16[256,1024]{1,0:T(8,128)(2,1)} %bitcast.10, bf16[512,512]{1,0:T(8,128)(2,1)} %key_up_in.1, bf16[512,1024]{1,0:T(8,128)(2,1)} %value_up_in.1, ...), custom_call_target="tpu_custom_call" | custom-call | flops 671088640 | bytes 6358032 | tf_op jit(solution)/shard_map/pallas_call | solution.py:49
  46.0 4.7 %all-to-all-start.2 = ((f32[8,144,128]{2,1,0:T(8,128)}), f32[8,144,128]{2,1,0:T(8,128)S(1)}, u32[]{:S(2)}, u32[]{:S(2)}) async-start(f32[8,144,128]{2,1,0:T(8,128)} %get-tuple-element.41), calls=%async_computation.2 | async-start | bytes 1179648 | tf_op jit(solution)/shard_map/all_to_all | solution.py:367
  50.7 8.2 %all-to-all-done.2.parts = f32[8,144,128]{2,1,0:T(8,128)S(1)} async-done(((f32[8,144,128]{2,1,0:T(8,128)}), f32[8,144,128]{2,1,0:T(8,128)S(1)}, u32[]{:S(2)}, u32[]{:S(2)}) %all-to-all-start.2) | async-done | bytes 589856 | tf_op jit(solution)/shard_map/all_to_all | solution.py:367
  59.7 11.7 %all_to_all.20.packed = f32[8,144,128]{2,1,0:T(8,128)S(1)} all-to-all(f32[8,144,128]{2,1,0:T(8,128)S(1)} %shard_map.124), channel_id=1, replica_groups=mesh['dp'=32,'tensor'=8] {'tensor'}, dimensions={0} | all-to-all | bytes 1179648 | tf_op jit(solution)/shard_map/all_to_all | solution.py:367
  73.0 3.5 %shard_map.131 = (f32[128,768]{1,0:T(8,128)}, f32[128,768]{1,0:T(8,128)}, f32[128,768]{1,0:T(8,128)}, f32[128,768]{1,0:T(8,128)}) custom-call(s32[4]{0:T(128)} %pad_add_fusion.at, bf16[256,1280]{1,0:T(8,128)(2,1)} %get-tuple-element.58.own, f32[256,1280]{1,0:T(8,128)} %copy-done.7), custom_call_target="tpu_custom_call" | custom-call | flops 402653184 | bytes 3538960 | tf_op jit(solution)/shard_map/pallas_call | solution.py:49
  78.1 2.7 %collective-permute-start.18 = (f32[128,768]{1,0:T(8,128)}, f32[128,768]{1,0:T(8,128)S(1)}, u32[]{:S(2)}, u32[]{:S(2)}) collective-permute-start(f32[128,768]{1,0:T(8,128)} %get-tuple-element.62), channel_id=1, source_target_pairs={{0,128},{1,129},{2,130},{3,131},{4,132},{5,133},{6,134},{7,135},{8... | collective-permute-start | bytes 1179656 | tf_op jit(solution)/shard_map/ppermute | solution.py:349
  82.2 6.8 %collective-permute-done.17.first = f32[128,768]{1,0:T(8,128)S(1)} collective-permute-done((f32[128,768]{1,0:T(8,128)}, f32[128,768]{1,0:T(8,128)S(1)}, u32[]{:S(2)}, u32[]{:S(2)}) %collective-permute-start.17) | collective-permute-done | bytes 393248 | tf_op jit(solution)/shard_map/ppermute | solution.py:349
  89.0 9.4 %collective-permute-done.18.second = f32[128,768]{1,0:T(8,128)S(1)} collective-permute-done((f32[128,768]{1,0:T(8,128)}, f32[128,768]{1,0:T(8,128)S(1)}, u32[]{:S(2)}, u32[]{:S(2)}) %collective-permute-start.18) | collective-permute-done | bytes 393248 | tf_op jit(solution)/shard_map/ppermute | solution.py:349
  99.5 3.5 %collective-permute-start.20 = (f32[64,768]{1,0:T(8,128)S(1)}, f32[64,768]{1,0:T(8,128)S(1)}, u32[]{:S(2)}, u32[]{:S(2)}) collective-permute-start(f32[64,768]{1,0:T(8,128)S(1)} %get-tuple-element.64.a), channel_id=1, source_target_pairs={{0,16},{1,17},{2,18},{3,19},{4,20},{5,21},{6,22},{7,23},{8,24},{9,... | collective-permute-start | bytes 589832 | tf_op jit(solution)/shard_map/ppermute | solution.py:349
  103.0 3.6 %collective-permute-start.21 = (f32[64,768]{1,0:T(8,128)S(1)}, f32[64,768]{1,0:T(8,128)S(1)}, u32[]{:S(2)}, u32[]{:S(2)}) collective-permute-start(f32[64,768]{1,0:T(8,128)S(1)} %get-tuple-element.65.b), channel_id=1, source_target_pairs={{0,48},{1,49},{2,50},{3,51},{4,52},{5,53},{6,54},{7,55},{8,56},{9,... | collective-permute-start | bytes 589832 | tf_op jit(solution)/shard_map/ppermute | solution.py:349
  115.1 3.5 %collective-permute-start.22 = (f32[64,768]{1,0:T(8,128)S(1)}, f32[64,768]{1,0:T(8,128)S(1)}, u32[]{:S(2)}, u32[]{:S(2)}) collective-permute-start(f32[64,768]{1,0:T(8,128)S(1)} %get-tuple-element.66.a), channel_id=1, source_target_pairs={{0,48},{1,49},{2,50},{3,51},{4,52},{5,53},{6,54},{7,55},{8,56},{9,... | collective-permute-start | bytes 589832 | tf_op jit(solution)/shard_map/ppermute | solution.py:349
  118.6 7.9 %collective-permute-done.22.got_a = f32[64,768]{1,0:T(8,128)S(1)} collective-permute-done((f32[64,768]{1,0:T(8,128)S(1)}, f32[64,768]{1,0:T(8,128)S(1)}, u32[]{:S(2)}, u32[]{:S(2)}) %collective-permute-start.22) | collective-permute-done | bytes 196640 | tf_op jit(solution)/shard_map/ppermute | solution.py:349
  126.5 3.0 %collective-permute-done.23.got_b = f32[64,768]{1,0:T(8,128)S(1)} collective-permute-done((f32[64,768]{1,0:T(8,128)S(1)}, f32[64,768]{1,0:T(8,128)S(1)}, u32[]{:S(2)}, u32[]{:S(2)}) %collective-permute-start.23) | collective-permute-done | bytes 196640 | tf_op jit(solution)/shard_map/ppermute | solution.py:349
  131.1 3.1 %collective-permute-start.25 = (f32[128,768]{1,0:T(8,128)S(1)}, f32[128,768]{1,0:T(8,128)S(1)}, u32[]{:S(2)}, u32[]{:S(2)}) collective-permute-start(f32[128,768]{1,0:T(8,128)S(1)} %shard_map.134.refs_0_), channel_id=1, source_target_pairs={{0,128},{1,129},{2,130},{3,131},{4,132},{5,133},{6,134},{7,135},{8... | collective-permute-start | bytes 1179656 | tf_op jit(solution)/shard_map/ppermute | solution.py:349
  136.5 6.6 %collective-permute-done.5.got_a = f32[2,144,128]{2,1,0:T(8,128)S(1)} collective-permute-done((f32[2,144,128]{2,1,0:T(8,128)S(1)}, f32[2,144,128]{2,1,0:T(8,128)S(1)}, u32[]{:S(2)}, u32[]{:S(2)}) %collective-permute-start.5) | collective-permute-done | bytes 147488 | tf_op jit(solution)/shard_map/ppermute | solution.py:349
  145.0 5.6 %collective-permute-done.25.refs_2_ = f32[128,768]{1,0:T(8,128)S(1)} collective-permute-done((f32[128,768]{1,0:T(8,128)S(1)}, f32[128,768]{1,0:T(8,128)S(1)}, u32[]{:S(2)}, u32[]{:S(2)}) %collective-permute-start.25) | collective-permute-done | bytes 393248 | tf_op jit(solution)/shard_map/ppermute | solution.py:349
  150.6 4.2 %collective-permute-done.7.got_a = f32[2,144,128]{2,1,0:T(8,128)S(1)} collective-permute-done((f32[2,144,128]{2,1,0:T(8,128)S(1)}, f32[2,144,128]{2,1,0:T(8,128)S(1)}, u32[]{:S(2)}, u32[]{:S(2)}) %collective-permute-start.7) | collective-permute-done | bytes 147488 | tf_op jit(solution)/shard_map/ppermute | solution.py:349
  154.9 2.6 %collective-permute-done.8.got_b = f32[2,144,128]{2,1,0:T(8,128)S(1)} collective-permute-done((f32[2,144,128]{2,1,0:T(8,128)S(1)}, f32[2,144,128]{2,1,0:T(8,128)S(1)}, u32[]{:S(2)}, u32[]{:S(2)}) %collective-permute-start.8) | collective-permute-done | bytes 147488 | tf_op jit(solution)/shard_map/ppermute | solution.py:349
  161.9 11.3 %collective-permute-done.10.refs_1_ = f32[4,144,128]{2,1,0:T(8,128)S(1)} collective-permute-done((f32[4,144,128]{2,1,0:T(8,128)S(1)}, f32[4,144,128]{2,1,0:T(8,128)S(1)}, u32[]{:S(2)}, u32[]{:S(2)}) %collective-permute-start.10) | collective-permute-done | bytes 294944 | tf_op jit(solution)/shard_map/ppermute | solution.py:349
  (88 shorter events, 37.4 us)
Async XLA Ops:
  3.5 15.5 %all-to-all-start = ((f32[8,144,128]{2,1,0:T(8,128)}), f32[8,144,128]{2,1,0:T(8,128)S(1)}, u32[]{:S(2)}, u32[]{:S(2)}) async-start(f32[8,144,128]{2,1,0:T(8,128)} %shard_map.120), calls=%async_computation | async-start | bytes 1179648 | tf_op jit(solution)/shard_map/all_to_all | solution.py:367
  20.0 14.0 %all-to-all-start.1 = ((f32[8,144,128]{2,1,0:T(8,128)}), f32[8,144,128]{2,1,0:T(8,128)S(1)}, u32[]{:S(2)}, u32[]{:S(2)}) async-start(f32[8,144,128]{2,1,0:T(8,128)} %get-tuple-element.39), calls=%async_computation.1 | async-start | bytes 1179648 | tf_op jit(solution)/shard_map/all_to_all | solution.py:367
  46.0 13.0 %all-to-all-start.2 = ((f32[8,144,128]{2,1,0:T(8,128)}), f32[8,144,128]{2,1,0:T(8,128)S(1)}, u32[]{:S(2)}, u32[]{:S(2)}) async-start(f32[8,144,128]{2,1,0:T(8,128)} %get-tuple-element.41), calls=%async_computation.2 | async-start | bytes 1179648 | tf_op jit(solution)/shard_map/all_to_all | solution.py:367
  50.7 21.3 %collective-permute-start.16 = (f32[256,1280]{1,0:T(8,128)}, f32[256,1280]{1,0:T(8,128)S(1)}, u32[]{:S(2)}, u32[]{:S(2)}) collective-permute-start(f32[256,1280]{1,0:T(8,128)} %get-tuple-element.59), channel_id=1, source_target_pairs={{0,8},{1,9},{2,10},{3,11},{4,12},{5,13},{6,14},{7,15},{8,0},{9,1},... | collective-permute-start | bytes 3932168 | tf_op jit(solution)/shard_map/ppermute | solution.py:349
  71.5 35.2 %collective-permute-start = (f32[8,144,128]{2,1,0:T(8,128)S(1)}, f32[8,144,128]{2,1,0:T(8,128)S(1)}, u32[]{:S(2)}, u32[]{:S(2)}) collective-permute-start(f32[8,144,128]{2,1,0:T(8,128)S(1)} %all_to_all.20.packed), channel_id=1, source_target_pairs={{0,8},{1,9},{2,10},{3,11},{4,12},{5,13},{6,14},{7,15},{8,0},{9,1},... | collective-permute-start | bytes 1769480 | tf_op jit(solution)/shard_map/ppermute | solution.py:349
  71.5 35.2 %collective-permute-start.1 = (f32[512,256]{1,0:T(8,128)S(1)}, f32[512,256]{1,0:T(8,128)S(1)}, u32[]{:S(2)}, u32[]{:S(2)}) collective-permute-start(f32[512,256]{1,0:T(8,128)S(1)} %copy-done.9), channel_id=1, source_target_pairs={{0,8},{1,9},{2,10},{3,11},{4,12},{5,13},{6,14},{7,15},{8,0},{9,1},... | collective-permute-start | bytes 1572872 | tf_op jit(solution)/shard_map/ppermute | solution.py:349
  76.6 12.4 %collective-permute-start.17 = (f32[128,768]{1,0:T(8,128)}, f32[128,768]{1,0:T(8,128)S(1)}, u32[]{:S(2)}, u32[]{:S(2)}) collective-permute-start(f32[128,768]{1,0:T(8,128)} %get-tuple-element.61), channel_id=1, source_target_pairs={{0,64},{1,65},{2,66},{3,67},{4,68},{5,69},{6,70},{7,71},{8,72},{9,... | collective-permute-start | bytes 1179656 | tf_op jit(solution)/shard_map/ppermute | solution.py:349
  78.1 20.4 %collective-permute-start.18 = (f32[128,768]{1,0:T(8,128)}, f32[128,768]{1,0:T(8,128)S(1)}, u32[]{:S(2)}, u32[]{:S(2)}) collective-permute-start(f32[128,768]{1,0:T(8,128)} %get-tuple-element.62), channel_id=1, source_target_pairs={{0,128},{1,129},{2,130},{3,131},{4,132},{5,133},{6,134},{7,135},{8... | collective-permute-start | bytes 1179656 | tf_op jit(solution)/shard_map/ppermute | solution.py:349
  80.8 17.6 %collective-permute-start.19 = (f32[128,768]{1,0:T(8,128)}, f32[128,768]{1,0:T(8,128)S(1)}, u32[]{:S(2)}, u32[]{:S(2)}) collective-permute-start(f32[128,768]{1,0:T(8,128)} %get-tuple-element.63), channel_id=1, source_target_pairs={{0,192},{1,193},{2,194},{3,195},{4,196},{5,197},{6,198},{7,199},{8... | collective-permute-start | bytes 1179656 | tf_op jit(solution)/shard_map/ppermute | solution.py:349
  99.5 13.7 %collective-permute-start.20 = (f32[64,768]{1,0:T(8,128)S(1)}, f32[64,768]{1,0:T(8,128)S(1)}, u32[]{:S(2)}, u32[]{:S(2)}) collective-permute-start(f32[64,768]{1,0:T(8,128)S(1)} %get-tuple-element.64.a), channel_id=1, source_target_pairs={{0,16},{1,17},{2,18},{3,19},{4,20},{5,21},{6,22},{7,23},{8,24},{9,... | collective-permute-start | bytes 589832 | tf_op jit(solution)/shard_map/ppermute | solution.py:349
  103.0 12.0 %collective-permute-start.21 = (f32[64,768]{1,0:T(8,128)S(1)}, f32[64,768]{1,0:T(8,128)S(1)}, u32[]{:S(2)}, u32[]{:S(2)}) collective-permute-start(f32[64,768]{1,0:T(8,128)S(1)} %get-tuple-element.65.b), channel_id=1, source_target_pairs={{0,48},{1,49},{2,50},{3,51},{4,52},{5,53},{6,54},{7,55},{8,56},{9,... | collective-permute-start | bytes 589832 | tf_op jit(solution)/shard_map/ppermute | solution.py:349
  107.9 26.3 %collective-permute-start.2 = (f32[4,144,128]{2,1,0:T(8,128)S(1)}, f32[4,144,128]{2,1,0:T(8,128)S(1)}, u32[]{:S(2)}, u32[]{:S(2)}) collective-permute-start(f32[4,144,128]{2,1,0:T(8,128)S(1)} %get-tuple-element.47), channel_id=1, source_target_pairs={{0,64},{1,65},{2,66},{3,67},{4,68},{5,69},{6,70},{7,71},{8,72},{9,... | collective-permute-start | bytes 884744 | tf_op jit(solution)/shard_map/ppermute | solution.py:349
  109.3 24.9 %collective-permute-start.3 = (f32[4,144,128]{2,1,0:T(8,128)S(1)}, f32[4,144,128]{2,1,0:T(8,128)S(1)}, u32[]{:S(2)}, u32[]{:S(2)}) collective-permute-start(f32[4,144,128]{2,1,0:T(8,128)S(1)} %get-tuple-element.48), channel_id=1, source_target_pairs={{0,128},{1,129},{2,130},{3,131},{4,132},{5,133},{6,134},{7,135},{8... | collective-permute-start | bytes 884744 | tf_op jit(solution)/shard_map/ppermute | solution.py:349
  111.7 22.5 %collective-permute-start.4 = (f32[4,144,128]{2,1,0:T(8,128)S(1)}, f32[4,144,128]{2,1,0:T(8,128)S(1)}, u32[]{:S(2)}, u32[]{:S(2)}) collective-permute-start(f32[4,144,128]{2,1,0:T(8,128)S(1)} %get-tuple-element.49), channel_id=1, source_target_pairs={{0,192},{1,193},{2,194},{3,195},{4,196},{5,197},{6,198},{7,199},{8... | collective-permute-start | bytes 884744 | tf_op jit(solution)/shard_map/ppermute | solution.py:349
  129.5 15.4 %collective-permute-start.24 = (f32[128,768]{1,0:T(8,128)S(1)}, f32[128,768]{1,0:T(8,128)S(1)}, u32[]{:S(2)}, u32[]{:S(2)}) collective-permute-start(f32[128,768]{1,0:T(8,128)S(1)} %shard_map.134.refs_0_), channel_id=1, source_target_pairs={{0,64},{1,65},{2,66},{3,67},{4,68},{5,69},{6,70},{7,71},{8,72},{9,... | collective-permute-start | bytes 1179656 | tf_op jit(solution)/shard_map/ppermute | solution.py:349
  131.1 19.5 %collective-permute-start.25 = (f32[128,768]{1,0:T(8,128)S(1)}, f32[128,768]{1,0:T(8,128)S(1)}, u32[]{:S(2)}, u32[]{:S(2)}) collective-permute-start(f32[128,768]{1,0:T(8,128)S(1)} %shard_map.134.refs_0_), channel_id=1, source_target_pairs={{0,128},{1,129},{2,130},{3,131},{4,132},{5,133},{6,134},{7,135},{8... | collective-permute-start | bytes 1179656 | tf_op jit(solution)/shard_map/ppermute | solution.py:349
  136.1 21.5 %collective-permute-start.26 = (f32[128,768]{1,0:T(8,128)S(1)}, f32[128,768]{1,0:T(8,128)S(1)}, u32[]{:S(2)}, u32[]{:S(2)}) collective-permute-start(f32[128,768]{1,0:T(8,128)S(1)} %shard_map.134.refs_0_), channel_id=1, source_target_pairs={{0,192},{1,193},{2,194},{3,195},{4,196},{5,197},{6,198},{7,199},{8... | collective-permute-start | bytes 1179656 | tf_op jit(solution)/shard_map/ppermute | solution.py:349
  143.1 15.7 %collective-permute-start.27 = (f32[128,768]{1,0:T(8,128)S(1)}, f32[128,768]{1,0:T(8,128)S(1)}, u32[]{:S(2)}, u32[]{:S(2)}) collective-permute-start(f32[128,768]{1,0:T(8,128)S(1)} %shard_map.134.refs_0_), channel_id=1, source_target_pairs={{0,8},{1,9},{2,10},{3,11},{4,12},{5,13},{6,14},{7,15},{8,0},{9,1},... | collective-permute-start | bytes 1179656 | tf_op jit(solution)/shard_map/ppermute | solution.py:349
  145.0 16.4 %collective-permute-start.28 = (f32[128,768]{1,0:T(8,128)S(1)}, f32[128,768]{1,0:T(8,128)S(1)}, u32[]{:S(2)}, u32[]{:S(2)}) collective-permute-start(f32[128,768]{1,0:T(8,128)S(1)} %collective-permute-done.24.refs_1_), channel_id=1, source_target_pairs={{0,8},{1,9},{2,10},{3,11},{4,12},{5,13},{6,14},{7,15},{8,0},{9,1},... | collective-permute-start | bytes 1179656 | tf_op jit(solution)/shard_map/ppermute | solution.py:349
  157.5 15.6 %collective-permute-start.10 = (f32[4,144,128]{2,1,0:T(8,128)S(1)}, f32[4,144,128]{2,1,0:T(8,128)S(1)}, u32[]{:S(2)}, u32[]{:S(2)}) collective-permute-start(f32[4,144,128]{2,1,0:T(8,128)S(1)} %shard_map.128.refs_0_), channel_id=1, source_target_pairs={{0,64},{1,65},{2,66},{3,67},{4,68},{5,69},{6,70},{7,71},{8,72},{9,... | collective-permute-start | bytes 884744 | tf_op jit(solution)/shard_map/ppermute | solution.py:349
  157.6 15.5 %collective-permute-start.12 = (f32[4,144,128]{2,1,0:T(8,128)S(1)}, f32[4,144,128]{2,1,0:T(8,128)S(1)}, u32[]{:S(2)}, u32[]{:S(2)}) collective-permute-start(f32[4,144,128]{2,1,0:T(8,128)S(1)} %shard_map.128.refs_0_), channel_id=1, source_target_pairs={{0,128},{1,129},{2,130},{3,131},{4,132},{5,133},{6,134},{7,135},{8... | collective-permute-start | bytes 884744 | tf_op jit(solution)/shard_map/ppermute | solution.py:349
  158.8 14.9 %collective-permute-start.14 = (f32[4,144,128]{2,1,0:T(8,128)S(1)}, f32[4,144,128]{2,1,0:T(8,128)S(1)}, u32[]{:S(2)}, u32[]{:S(2)}) collective-permute-start(f32[4,144,128]{2,1,0:T(8,128)S(1)} %shard_map.128.refs_0_), channel_id=1, source_target_pairs={{0,192},{1,193},{2,194},{3,195},{4,196},{5,197},{6,198},{7,199},{8... | collective-permute-start | bytes 884744 | tf_op jit(solution)/shard_map/ppermute | solution.py:349
  161.4 12.4 %collective-permute-start.30 = (f32[128,768]{1,0:T(8,128)S(1)}, f32[128,768]{1,0:T(8,128)S(1)}, u32[]{:S(2)}, u32[]{:S(2)}) collective-permute-start(f32[128,768]{1,0:T(8,128)S(1)} %collective-permute-done.26.refs_3_), channel_id=1, source_target_pairs={{0,8},{1,9},{2,10},{3,11},{4,12},{5,13},{6,14},{7,15},{8,0},{9,1},... | collective-permute-start | bytes 1179656 | tf_op jit(solution)/shard_map/ppermute | solution.py:349
  161.4 16.5 %collective-permute-start.9 = (f32[4,144,128]{2,1,0:T(8,128)S(1)}, f32[4,144,128]{2,1,0:T(8,128)S(1)}, u32[]{:S(2)}, u32[]{:S(2)}) collective-permute-start(f32[4,144,128]{2,1,0:T(8,128)S(1)} %shard_map.128.refs_0_), channel_id=1, source_target_pairs={{0,8},{1,9},{2,10},{3,11},{4,12},{5,13},{6,14},{7,15},{8,0},{9,1},... | collective-permute-start | bytes 884744 | tf_op jit(solution)/shard_map/ppermute | solution.py:349
  (20 other events, 282.7 us)

commit v7 on v6

--- a/solution.py
+++ b/solution.py
@@ -238,7 +238,7 @@
         return dot_tn(score_grad, query)
 
     def heads(step, carry):
-        for p in (2 * step, 2 * step + 1):
+        for p in (4 * step, 4 * step + 1, 4 * step + 2, 4 * step + 3):
             both = nope[:, lanes(p)]
             first = head(2 * p, pltpu.roll(both, 64, 1))
             second = head(2 * p + 1, both)
@@ -246,13 +246,12 @@
             grads[:, lanes(p)] = jnp.where(low, pltpu.roll(first, 64, 1), second).astype(BF16)
         return carry
 
-    lax.fori_loop(0, 2, heads, 0)
+    lax.fori_loop(0, 1, heads, 0)
     for ref, c in ((send, 1 - at[0]), (keep, at[0])):
         keys = pl.ds(pl.multiple_of(c * 256, 256), 256)
         values = pl.ds(pl.multiple_of(512 + c * 512, 512), 512)
         ref[:, :256] = grads[:, keys].astype(ref.dtype)
-        ref[:, 256:768] = grads[:, values].astype(ref.dtype)
-        ref[:, 768:] = latent[...].astype(ref.dtype)
+        ref[:, 256:] = grads[:, values].astype(ref.dtype)
     puts = start((send, send_out, sems.at[4]), (keep, keep_out, sems.at[5]))
     wide = dot_nt(grads[:, :512], key_up[...]) + dot_nt(grads[:, 512:], value_up[...])
     rest_all = rest_sum[...]
@@ -261,9 +260,12 @@
     wait(puts + start((norm, norm_out, sems.at[6])))
 
 
-def up_kernel(at, own, other, *outs):
-    whole = dot_tn(own[:, 768:], own[:, :768])
-    whole = whole + dot_tn(other[:, 768:].astype(BF16), other[:, :768].astype(BF16))
+def up_kernel(at, packed, other_packed, grads, other_grads, *outs):
+    *outs, latent, rest = outs
+    unpack(packed, latent, rest)
+    whole = dot_tn(latent[...], grads[...])
+    unpack(other_packed, latent, rest)
+    whole = whole + dot_tn(latent[...], other_grads[...].astype(BF16))
     for quarter in range(4):
         for step in range(4):
             @pl.when((at[1] + step) % 4 == quarter)
@@ -401,9 +403,10 @@
     parts, teacher = lax.optimization_barrier((parts, teacher))
     replicas, normed, inv = call(norm_kernel, [chunks, shape(128, 128), shape(32, 128)], parts)
     packed = exchange(replicas)
+    packed_other = other_core(packed)
     grads_keep, grads_send, part = call(
         student_kernel,
-        [shape(SEQ, 1280, dtype=BF16), shape(SEQ, 1280), chunks],
+        [shape(SEQ, 768, dtype=BF16), shape(SEQ, 768), chunks],
         at, packed, queries, key_up, value_up, teacher, *partial, seg_row,
         scalars=1,
         scratch=unpacked + [
@@ -415,8 +418,8 @@
             pltpu.VMEM((LATENT, 512), BF16),
             pltpu.VMEM((LATENT, 1024), BF16),
             pltpu.VMEM((SEQ, 1024), F32),
-            pltpu.VMEM((SEQ, 1280), BF16),
-            pltpu.VMEM((SEQ, 1280), F32),
+            pltpu.VMEM((SEQ, 768), BF16),
+            pltpu.VMEM((SEQ, 768), F32),
             pltpu.VMEM((8, PACKED, 128), F32),
             pltpu.SemaphoreType.DMA((7,)),
         ],
@@ -426,8 +429,8 @@
     grads_other = other_core(grads_send)
     parts = exchange(part)
     quarters = call(
-        up_kernel, [shape(128, 768)] * 4, at, grads_keep, grads_other,
-        scalars=1, flops=2 * 512 * 512 * 768, mib=60,
+        up_kernel, [shape(128, 768)] * 4, at, packed, packed_other, grads_keep, grads_other,
+        scalars=1, scratch=unpacked, flops=2 * 512 * 512 * 768, mib=60,
     )
     received = around(list(quarters[1:]), "x")
     (replicas,) = call(norm_grad_kernel, [chunks], at, parts, normed, inv, *partial, scalars=1)

time: 182 us -> 183 us (level)
    ppermute x31 -> x32, waiting for transfers between devices: 59.4 us -> 59.9 us  [permute(): return lax.ppermute(value, AXES, pairs)]
    ppermute x31 -> x32, starting transfers between devices: 35.7 us -> 35.5 us  [permute(): return lax.ppermute(value, AXES, pairs)]
  transfers between devices with their start and end apart: 34 -> 35, of which waited for: 14 -> 14; matrix products, arithmetic and copies ran while one was open for 2% -> 2% of each run, Pallas kernels for 9% -> 9%
where the time goes in v7:
time: 183 us; the launch traced here: 181 us
  waiting for transfers between devices  75.8 us (41%)
  starting transfers between devices  51.2 us (28%)
  Pallas kernels  33.3 us (18%)
  blocking collectives  13 us (7%)
  other arithmetic  3.37 us (2%)
  local copies, waits for them, and re-layouts  2.9 us (2%)
    ppermute x32, waiting for transfers between devices, permute(): return lax.ppermute(value, AXES, pairs)  59.9 us
    ppermute x32, starting transfers between devices, permute(): return lax.ppermute(value, AXES, pairs)  35.5 us
    pallas_call x16, Pallas kernels, call(): pl.pallas_call(body, out_shape=outs, in_specs=specs, out_specs=[anywhere...  33.3 us
    all_to_all x3, waiting for transfers between devices, exchange(): return lax.all_to_all(parts, 'tensor', 0, 0, tiled=True)  15.8 us
    all_to_all x3, starting transfers between devices, exchange(): return lax.all_to_all(parts, 'tensor', 0, 0, tiled=True)  15.7 us
    all_to_all x1, blocking collectives, exchange(): return lax.all_to_all(parts, 'tensor', 0, 0, tiled=True)  13 us
  transfers between devices with their start and end apart: 35, of which 14 were waited for; matrix products, arithmetic and copies ran while one was open for 2% of the time, Pallas kernels for 9%

profile of v7, /device:TPU:32, one launch (start us, length us, event | category | flops | bytes accessed | tf_op | source)
XLA Modules:
  0.0 180.5 jit_solution(760978812247485253)
XLA Ops:
  0.6 2.8 %shard_map.120 = f32[8,144,128]{2,1,0:T(8,128)} custom-call(bf16[256,1024]{1,0:T(8,128)(2,1)} %bitcast.11, bf16[1024,512]{1,0:T(8,128)(2,1)} %down.1, bf16[64,1024]{1,0:T(8,128)(2,1)} %rope.1), custom_call_target="tpu_custom_call" | custom-call | flops 301989888 | bytes 2293760 | tf_op jit(solution)/shard_map/pallas_call | solution.py:49
  3.5 5.9 %all-to-all-start = ((f32[8,144,128]{2,1,0:T(8,128)}), f32[8,144,128]{2,1,0:T(8,128)S(1)}, u32[]{:S(2)}, u32[]{:S(2)}) async-start(f32[8,144,128]{2,1,0:T(8,128)} %shard_map.120), calls=%async_computation | async-start | bytes 1179648 | tf_op jit(solution)/shard_map/all_to_all | solution.py:369
  11.5 6.8 %shard_map.121 = (f32[256,1024]{1,0:T(8,128)}, bf16[512,256]{1,0:T(8,128)(2,1)}, f32[512,256]{1,0:T(8,128)}) custom-call(s32[4]{0:T(128)} %pad_add_fusion.at, bf16[256,1024]{1,0:T(8,128)(2,1)} %bitcast.9, bf16[256,128]{1,0:T(8,128)(2,1)} %bitcast.13, bf16[256,128]{1,0:T(8,128)(2,1)} %bitcast.14, f32[256,64]{1,0:T(8,128)} %get-tuple-element.73.cos_full, ...), custom_call_target="tpu_custom_call" | custom-call | flops 268435456 | bytes 3146768 | tf_op jit(solution)/shard_map/pallas_call | solution.py:49
  20.0 5.1 %all-to-all-start.1 = ((f32[8,144,128]{2,1,0:T(8,128)}), f32[8,144,128]{2,1,0:T(8,128)S(1)}, u32[]{:S(2)}, u32[]{:S(2)}) async-start(f32[8,144,128]{2,1,0:T(8,128)} %get-tuple-element.39), calls=%async_computation.1 | async-start | bytes 1179648 | tf_op jit(solution)/shard_map/all_to_all | solution.py:369
  26.3 7.8 %all-to-all-done.1.packed = f32[8,144,128]{2,1,0:T(8,128)S(1)} async-done(((f32[8,144,128]{2,1,0:T(8,128)}), f32[8,144,128]{2,1,0:T(8,128)S(1)}, u32[]{:S(2)}, u32[]{:S(2)}) %all-to-all-start.1) | async-done | bytes 589856 | tf_op jit(solution)/shard_map/all_to_all | solution.py:369
  34.9 9.8 %shard_map.123 = (bf16[256,768]{1,0:T(8,128)(2,1)}, f32[256,768]{1,0:T(8,128)}, f32[8,144,128]{2,1,0:T(8,128)}) custom-call(s32[4]{0:T(128)} %pad_add_fusion.at, f32[8,144,128]{2,1,0:T(8,128)} %copy-done.6, bf16[256,1024]{1,0:T(8,128)(2,1)} %bitcast.10, bf16[512,512]{1,0:T(8,128)(2,1)} %key_up_in.1, bf16[512,1024]{1,0:T(8,128)(2,1)} %value_up_in.1, ...), custom_call_target="tpu_custom_call" | custom-call | flops 671088640 | bytes 5571600 | tf_op jit(solution)/shard_map/pallas_call | solution.py:49
  44.8 13.0 %all_to_all.20.parts = f32[8,144,128]{2,1,0:T(8,128)S(1)} all-to-all(f32[8,144,128]{2,1,0:T(8,128)} %get-tuple-element.41), channel_id=1, replica_groups=mesh['dp'=32,'tensor'=8] {'tensor'}, dimensions={0} | all-to-all | bytes 1179648 | tf_op jit(solution)/shard_map/all_to_all | solution.py:369
  59.3 4.7 %all-to-all-start.3 = ((f32[8,144,128]{2,1,0:T(8,128)}), f32[8,144,128]{2,1,0:T(8,128)S(1)}, u32[]{:S(2)}, u32[]{:S(2)}) async-start(f32[8,144,128]{2,1,0:T(8,128)} %shard_map.124), calls=%async_computation.3 | async-start | bytes 1179648 | tf_op jit(solution)/shard_map/all_to_all | solution.py:369
  64.6 7.4 %all-to-all-done.3.packed = f32[8,144,128]{2,1,0:T(8,128)S(1)} async-done(((f32[8,144,128]{2,1,0:T(8,128)}), f32[8,144,128]{2,1,0:T(8,128)S(1)}, u32[]{:S(2)}, u32[]{:S(2)}) %all-to-all-start.3) | async-done | bytes 589856 | tf_op jit(solution)/shard_map/all_to_all | solution.py:369
  73.6 3.9 %shard_map.131 = (f32[128,768]{1,0:T(8,128)}, f32[128,768]{1,0:T(8,128)}, f32[128,768]{1,0:T(8,128)}, f32[128,768]{1,0:T(8,128)}) custom-call(s32[4]{0:T(128)} %pad_add_fusion.at, f32[8,144,128]{2,1,0:T(8,128)} %copy-done.6, f32[8,144,128]{2,1,0:T(8,128)} %copy-done.9, bf16[256,768]{1,0:T(8,128)(2,1)} %get-tuple-element.58.grads, f32[256,768]{1,0:T(8,128)} %copy-done.8), custom_call_target="tpu_custom_call" | custom-call | flops 402653184 | bytes 3932176 | tf_op jit(solution)/shard_map/pallas_call | solution.py:49
  78.9 2.7 %collective-permute-start.19 = (f32[128,768]{1,0:T(8,128)}, f32[128,768]{1,0:T(8,128)S(1)}, u32[]{:S(2)}, u32[]{:S(2)}) collective-permute-start(f32[128,768]{1,0:T(8,128)} %get-tuple-element.62), channel_id=1, source_target_pairs={{0,128},{1,129},{2,130},{3,131},{4,132},{5,133},{6,134},{7,135},{8... | collective-permute-start | bytes 1179656 | tf_op jit(solution)/shard_map/ppermute | solution.py:351
  83.1 6.8 %collective-permute-done.18.first = f32[128,768]{1,0:T(8,128)S(1)} collective-permute-done((f32[128,768]{1,0:T(8,128)}, f32[128,768]{1,0:T(8,128)S(1)}, u32[]{:S(2)}, u32[]{:S(2)}) %collective-permute-start.18) | collective-permute-done | bytes 393248 | tf_op jit(solution)/shard_map/ppermute | solution.py:351
  89.9 9.4 %collective-permute-done.19.second = f32[128,768]{1,0:T(8,128)S(1)} collective-permute-done((f32[128,768]{1,0:T(8,128)}, f32[128,768]{1,0:T(8,128)S(1)}, u32[]{:S(2)}, u32[]{:S(2)}) %collective-permute-start.19) | collective-permute-done | bytes 393248 | tf_op jit(solution)/shard_map/ppermute | solution.py:351
  100.4 3.4 %collective-permute-start.21 = (f32[64,768]{1,0:T(8,128)S(1)}, f32[64,768]{1,0:T(8,128)S(1)}, u32[]{:S(2)}, u32[]{:S(2)}) collective-permute-start(f32[64,768]{1,0:T(8,128)S(1)} %get-tuple-element.64.a), channel_id=1, source_target_pairs={{0,16},{1,17},{2,18},{3,19},{4,20},{5,21},{6,22},{7,23},{8,24},{9,... | collective-permute-start | bytes 589832 | tf_op jit(solution)/shard_map/ppermute | solution.py:351
  103.7 3.6 %collective-permute-start.22 = (f32[64,768]{1,0:T(8,128)S(1)}, f32[64,768]{1,0:T(8,128)S(1)}, u32[]{:S(2)}, u32[]{:S(2)}) collective-permute-start(f32[64,768]{1,0:T(8,128)S(1)} %get-tuple-element.65.b), channel_id=1, source_target_pairs={{0,48},{1,49},{2,50},{3,51},{4,52},{5,53},{6,54},{7,55},{8,56},{9,... | collective-permute-start | bytes 589832 | tf_op jit(solution)/shard_map/ppermute | solution.py:351
  115.7 3.4 %collective-permute-start.23 = (f32[64,768]{1,0:T(8,128)S(1)}, f32[64,768]{1,0:T(8,128)S(1)}, u32[]{:S(2)}, u32[]{:S(2)}) collective-permute-start(f32[64,768]{1,0:T(8,128)S(1)} %get-tuple-element.66.a), channel_id=1, source_target_pairs={{0,48},{1,49},{2,50},{3,51},{4,52},{5,53},{6,54},{7,55},{8,56},{9,... | collective-permute-start | bytes 589832 | tf_op jit(solution)/shard_map/ppermute | solution.py:351
  119.1 7.9 %collective-permute-done.23.got_a = f32[64,768]{1,0:T(8,128)S(1)} collective-permute-done((f32[64,768]{1,0:T(8,128)S(1)}, f32[64,768]{1,0:T(8,128)S(1)}, u32[]{:S(2)}, u32[]{:S(2)}) %collective-permute-start.23) | collective-permute-done | bytes 196640 | tf_op jit(solution)/shard_map/ppermute | solution.py:351
  127.0 3.0 %collective-permute-done.24.got_b = f32[64,768]{1,0:T(8,128)S(1)} collective-permute-done((f32[64,768]{1,0:T(8,128)S(1)}, f32[64,768]{1,0:T(8,128)S(1)}, u32[]{:S(2)}, u32[]{:S(2)}) %collective-permute-start.24) | collective-permute-done | bytes 196640 | tf_op jit(solution)/shard_map/ppermute | solution.py:351
  131.6 3.1 %collective-permute-start.26 = (f32[128,768]{1,0:T(8,128)S(1)}, f32[128,768]{1,0:T(8,128)S(1)}, u32[]{:S(2)}, u32[]{:S(2)}) collective-permute-start(f32[128,768]{1,0:T(8,128)S(1)} %shard_map.134.refs_0_), channel_id=1, source_target_pairs={{0,128},{1,129},{2,130},{3,131},{4,132},{5,133},{6,134},{7,135},{8... | collective-permute-start | bytes 1179656 | tf_op jit(solution)/shard_map/ppermute | solution.py:351
  137.0 7.0 %collective-permute-done.5.got_a = f32[2,144,128]{2,1,0:T(8,128)S(1)} collective-permute-done((f32[2,144,128]{2,1,0:T(8,128)S(1)}, f32[2,144,128]{2,1,0:T(8,128)S(1)}, u32[]{:S(2)}, u32[]{:S(2)}) %collective-permute-start.5) | collective-permute-done | bytes 147488 | tf_op jit(solution)/shard_map/ppermute | solution.py:351
  145.9 5.1 %collective-permute-done.26.refs_2_ = f32[128,768]{1,0:T(8,128)S(1)} collective-permute-done((f32[128,768]{1,0:T(8,128)S(1)}, f32[128,768]{1,0:T(8,128)S(1)}, u32[]{:S(2)}, u32[]{:S(2)}) %collective-permute-start.26) | collective-permute-done | bytes 393248 | tf_op jit(solution)/shard_map/ppermute | solution.py:351
  151.1 4.8 %collective-permute-done.7.got_a = f32[2,144,128]{2,1,0:T(8,128)S(1)} collective-permute-done((f32[2,144,128]{2,1,0:T(8,128)S(1)}, f32[2,144,128]{2,1,0:T(8,128)S(1)}, u32[]{:S(2)}, u32[]{:S(2)}) %collective-permute-start.7) | collective-permute-done | bytes 147488 | tf_op jit(solution)/shard_map/ppermute | solution.py:351
  158.8 2.9 %collective-permute-start.14 = (f32[4,144,128]{2,1,0:T(8,128)S(1)}, f32[4,144,128]{2,1,0:T(8,128)S(1)}, u32[]{:S(2)}, u32[]{:S(2)}) collective-permute-start(f32[4,144,128]{2,1,0:T(8,128)S(1)} %shard_map.128.refs_0_), channel_id=1, source_target_pairs={{0,192},{1,193},{2,194},{3,195},{4,196},{5,197},{6,198},{7,199},{8... | collective-permute-start | bytes 884744 | tf_op jit(solution)/shard_map/ppermute | solution.py:351
  162.2 11.6 %collective-permute-done.10.refs_1_ = f32[4,144,128]{2,1,0:T(8,128)S(1)} collective-permute-done((f32[4,144,128]{2,1,0:T(8,128)S(1)}, f32[4,144,128]{2,1,0:T(8,128)S(1)}, u32[]{:S(2)}, u32[]{:S(2)}) %collective-permute-start.10) | collective-permute-done | bytes 294944 | tf_op jit(solution)/shard_map/ppermute | solution.py:351
  (92 shorter events, 37.6 us)
Async XLA Ops:
  3.5 15.5 %all-to-all-start = ((f32[8,144,128]{2,1,0:T(8,128)}), f32[8,144,128]{2,1,0:T(8,128)S(1)}, u32[]{:S(2)}, u32[]{:S(2)}) async-start(f32[8,144,128]{2,1,0:T(8,128)} %shard_map.120), calls=%async_computation | async-start | bytes 1179648 | tf_op jit(solution)/shard_map/all_to_all | solution.py:369
  20.0 14.1 %all-to-all-start.1 = ((f32[8,144,128]{2,1,0:T(8,128)}), f32[8,144,128]{2,1,0:T(8,128)S(1)}, u32[]{:S(2)}, u32[]{:S(2)}) async-start(f32[8,144,128]{2,1,0:T(8,128)} %get-tuple-element.39), calls=%async_computation.1 | async-start | bytes 1179648 | tf_op jit(solution)/shard_map/all_to_all | solution.py:369
  59.3 12.6 %all-to-all-start.3 = ((f32[8,144,128]{2,1,0:T(8,128)}), f32[8,144,128]{2,1,0:T(8,128)S(1)}, u32[]{:S(2)}, u32[]{:S(2)}) async-start(f32[8,144,128]{2,1,0:T(8,128)} %shard_map.124), calls=%async_computation.3 | async-start | bytes 1179648 | tf_op jit(solution)/shard_map/all_to_all | solution.py:369
  72.0 35.3 %collective-permute-start = (f32[8,144,128]{2,1,0:T(8,128)S(1)}, f32[8,144,128]{2,1,0:T(8,128)S(1)}, u32[]{:S(2)}, u32[]{:S(2)}) collective-permute-start(f32[8,144,128]{2,1,0:T(8,128)S(1)} %all-to-all-done.3.packed), channel_id=1, source_target_pairs={{0,8},{1,9},{2,10},{3,11},{4,12},{5,13},{6,14},{7,15},{8,0},{9,1},... | collective-permute-start | bytes 1769480 | tf_op jit(solution)/shard_map/ppermute | solution.py:351
  72.0 35.3 %collective-permute-start.1 = (f32[512,256]{1,0:T(8,128)}, f32[512,256]{1,0:T(8,128)S(1)}, u32[]{:S(2)}, u32[]{:S(2)}) collective-permute-start(f32[512,256]{1,0:T(8,128)} %get-tuple-element.45), channel_id=1, source_target_pairs={{0,8},{1,9},{2,10},{3,11},{4,12},{5,13},{6,14},{7,15},{8,0},{9,1},... | collective-permute-start | bytes 1572872 | tf_op jit(solution)/shard_map/ppermute | solution.py:351
  77.4 12.4 %collective-permute-start.18 = (f32[128,768]{1,0:T(8,128)}, f32[128,768]{1,0:T(8,128)S(1)}, u32[]{:S(2)}, u32[]{:S(2)}) collective-permute-start(f32[128,768]{1,0:T(8,128)} %get-tuple-element.61), channel_id=1, source_target_pairs={{0,64},{1,65},{2,66},{3,67},{4,68},{5,69},{6,70},{7,71},{8,72},{9,... | collective-permute-start | bytes 1179656 | tf_op jit(solution)/shard_map/ppermute | solution.py:351
  78.9 20.4 %collective-permute-start.19 = (f32[128,768]{1,0:T(8,128)}, f32[128,768]{1,0:T(8,128)S(1)}, u32[]{:S(2)}, u32[]{:S(2)}) collective-permute-start(f32[128,768]{1,0:T(8,128)} %get-tuple-element.62), channel_id=1, source_target_pairs={{0,128},{1,129},{2,130},{3,131},{4,132},{5,133},{6,134},{7,135},{8... | collective-permute-start | bytes 1179656 | tf_op jit(solution)/shard_map/ppermute | solution.py:351
  81.6 17.6 %collective-permute-start.20 = (f32[128,768]{1,0:T(8,128)}, f32[128,768]{1,0:T(8,128)S(1)}, u32[]{:S(2)}, u32[]{:S(2)}) collective-permute-start(f32[128,768]{1,0:T(8,128)} %get-tuple-element.63), channel_id=1, source_target_pairs={{0,192},{1,193},{2,194},{3,195},{4,196},{5,197},{6,198},{7,199},{8... | collective-permute-start | bytes 1179656 | tf_op jit(solution)/shard_map/ppermute | solution.py:351
  100.4 13.6 %collective-permute-start.21 = (f32[64,768]{1,0:T(8,128)S(1)}, f32[64,768]{1,0:T(8,128)S(1)}, u32[]{:S(2)}, u32[]{:S(2)}) collective-permute-start(f32[64,768]{1,0:T(8,128)S(1)} %get-tuple-element.64.a), channel_id=1, source_target_pairs={{0,16},{1,17},{2,18},{3,19},{4,20},{5,21},{6,22},{7,23},{8,24},{9,... | collective-permute-start | bytes 589832 | tf_op jit(solution)/shard_map/ppermute | solution.py:351
  103.7 12.0 %collective-permute-start.22 = (f32[64,768]{1,0:T(8,128)S(1)}, f32[64,768]{1,0:T(8,128)S(1)}, u32[]{:S(2)}, u32[]{:S(2)}) collective-permute-start(f32[64,768]{1,0:T(8,128)S(1)} %get-tuple-element.65.b), channel_id=1, source_target_pairs={{0,48},{1,49},{2,50},{3,51},{4,52},{5,53},{6,54},{7,55},{8,56},{9,... | collective-permute-start | bytes 589832 | tf_op jit(solution)/shard_map/ppermute | solution.py:351
  108.6 26.2 %collective-permute-start.2 = (f32[4,144,128]{2,1,0:T(8,128)S(1)}, f32[4,144,128]{2,1,0:T(8,128)S(1)}, u32[]{:S(2)}, u32[]{:S(2)}) collective-permute-start(f32[4,144,128]{2,1,0:T(8,128)S(1)} %get-tuple-element.47), channel_id=1, source_target_pairs={{0,64},{1,65},{2,66},{3,67},{4,68},{5,69},{6,70},{7,71},{8,72},{9,... | collective-permute-start | bytes 884744 | tf_op jit(solution)/shard_map/ppermute | solution.py:351
  110.0 24.8 %collective-permute-start.3 = (f32[4,144,128]{2,1,0:T(8,128)S(1)}, f32[4,144,128]{2,1,0:T(8,128)S(1)}, u32[]{:S(2)}, u32[]{:S(2)}) collective-permute-start(f32[4,144,128]{2,1,0:T(8,128)S(1)} %get-tuple-element.48), channel_id=1, source_target_pairs={{0,128},{1,129},{2,130},{3,131},{4,132},{5,133},{6,134},{7,135},{8... | collective-permute-start | bytes 884744 | tf_op jit(solution)/shard_map/ppermute | solution.py:351
  112.4 22.4 %collective-permute-start.4 = (f32[4,144,128]{2,1,0:T(8,128)S(1)}, f32[4,144,128]{2,1,0:T(8,128)S(1)}, u32[]{:S(2)}, u32[]{:S(2)}) collective-permute-start(f32[4,144,128]{2,1,0:T(8,128)S(1)} %get-tuple-element.49), channel_id=1, source_target_pairs={{0,192},{1,193},{2,194},{3,195},{4,196},{5,197},{6,198},{7,199},{8... | collective-permute-start | bytes 884744 | tf_op jit(solution)/shard_map/ppermute | solution.py:351
  130.1 15.9 %collective-permute-start.25 = (f32[128,768]{1,0:T(8,128)S(1)}, f32[128,768]{1,0:T(8,128)S(1)}, u32[]{:S(2)}, u32[]{:S(2)}) collective-permute-start(f32[128,768]{1,0:T(8,128)S(1)} %shard_map.134.refs_0_), channel_id=1, source_target_pairs={{0,64},{1,65},{2,66},{3,67},{4,68},{5,69},{6,70},{7,71},{8,72},{9,... | collective-permute-start | bytes 1179656 | tf_op jit(solution)/shard_map/ppermute | solution.py:351
  131.6 19.4 %collective-permute-start.26 = (f32[128,768]{1,0:T(8,128)S(1)}, f32[128,768]{1,0:T(8,128)S(1)}, u32[]{:S(2)}, u32[]{:S(2)}) collective-permute-start(f32[128,768]{1,0:T(8,128)S(1)} %shard_map.134.refs_0_), channel_id=1, source_target_pairs={{0,128},{1,129},{2,130},{3,131},{4,132},{5,133},{6,134},{7,135},{8... | collective-permute-start | bytes 1179656 | tf_op jit(solution)/shard_map/ppermute | solution.py:351
  136.6 21.8 %collective-permute-start.27 = (f32[128,768]{1,0:T(8,128)S(1)}, f32[128,768]{1,0:T(8,128)S(1)}, u32[]{:S(2)}, u32[]{:S(2)}) collective-permute-start(f32[128,768]{1,0:T(8,128)S(1)} %shard_map.134.refs_0_), channel_id=1, source_target_pairs={{0,192},{1,193},{2,194},{3,195},{4,196},{5,197},{6,198},{7,199},{8... | collective-permute-start | bytes 1179656 | tf_op jit(solution)/shard_map/ppermute | solution.py:351
  144.1 14.7 %collective-permute-start.28 = (f32[128,768]{1,0:T(8,128)S(1)}, f32[128,768]{1,0:T(8,128)S(1)}, u32[]{:S(2)}, u32[]{:S(2)}) collective-permute-start(f32[128,768]{1,0:T(8,128)S(1)} %shard_map.134.refs_0_), channel_id=1, source_target_pairs={{0,8},{1,9},{2,10},{3,11},{4,12},{5,13},{6,14},{7,15},{8,0},{9,1},... | collective-permute-start | bytes 1179656 | tf_op jit(solution)/shard_map/ppermute | solution.py:351
  144.1 11.7 %collective-permute-start.7 = (f32[2,144,128]{2,1,0:T(8,128)S(1)}, f32[2,144,128]{2,1,0:T(8,128)S(1)}, u32[]{:S(2)}, u32[]{:S(2)}) collective-permute-start(f32[2,144,128]{2,1,0:T(8,128)S(1)} %get-tuple-element.52.a), channel_id=1, source_target_pairs={{0,48},{1,49},{2,50},{3,51},{4,52},{5,53},{6,54},{7,55},{8,56},{9,... | collective-permute-start | bytes 442376 | tf_op jit(solution)/shard_map/ppermute | solution.py:351
  145.9 15.8 %collective-permute-start.29 = (f32[128,768]{1,0:T(8,128)S(1)}, f32[128,768]{1,0:T(8,128)S(1)}, u32[]{:S(2)}, u32[]{:S(2)}) collective-permute-start(f32[128,768]{1,0:T(8,128)S(1)} %collective-permute-done.25.refs_1_), channel_id=1, source_target_pairs={{0,8},{1,9},{2,10},{3,11},{4,12},{5,13},{6,14},{7,15},{8,0},{9,1},... | collective-permute-start | bytes 1179656 | tf_op jit(solution)/shard_map/ppermute | solution.py:351
  158.3 15.5 %collective-permute-start.10 = (f32[4,144,128]{2,1,0:T(8,128)S(1)}, f32[4,144,128]{2,1,0:T(8,128)S(1)}, u32[]{:S(2)}, u32[]{:S(2)}) collective-permute-start(f32[4,144,128]{2,1,0:T(8,128)S(1)} %shard_map.128.refs_0_), channel_id=1, source_target_pairs={{0,64},{1,65},{2,66},{3,67},{4,68},{5,69},{6,70},{7,71},{8,72},{9,... | collective-permute-start | bytes 884744 | tf_op jit(solution)/shard_map/ppermute | solution.py:351
  158.4 15.4 %collective-permute-start.12 = (f32[4,144,128]{2,1,0:T(8,128)S(1)}, f32[4,144,128]{2,1,0:T(8,128)S(1)}, u32[]{:S(2)}, u32[]{:S(2)}) collective-permute-start(f32[4,144,128]{2,1,0:T(8,128)S(1)} %shard_map.128.refs_0_), channel_id=1, source_target_pairs={{0,128},{1,129},{2,130},{3,131},{4,132},{5,133},{6,134},{7,135},{8... | collective-permute-start | bytes 884744 | tf_op jit(solution)/shard_map/ppermute | solution.py:351
  158.8 15.6 %collective-permute-start.14 = (f32[4,144,128]{2,1,0:T(8,128)S(1)}, f32[4,144,128]{2,1,0:T(8,128)S(1)}, u32[]{:S(2)}, u32[]{:S(2)}) collective-permute-start(f32[4,144,128]{2,1,0:T(8,128)S(1)} %shard_map.128.refs_0_), channel_id=1, source_target_pairs={{0,192},{1,193},{2,194},{3,195},{4,196},{5,197},{6,198},{7,199},{8... | collective-permute-start | bytes 884744 | tf_op jit(solution)/shard_map/ppermute | solution.py:351
  161.7 12.7 %collective-permute-start.31 = (f32[128,768]{1,0:T(8,128)S(1)}, f32[128,768]{1,0:T(8,128)S(1)}, u32[]{:S(2)}, u32[]{:S(2)}) collective-permute-start(f32[128,768]{1,0:T(8,128)S(1)} %collective-permute-done.27.refs_3_), channel_id=1, source_target_pairs={{0,8},{1,9},{2,10},{3,11},{4,12},{5,13},{6,14},{7,15},{8,0},{9,1},... | collective-permute-start | bytes 1179656 | tf_op jit(solution)/shard_map/ppermute | solution.py:351
  161.7 16.9 %collective-permute-start.9 = (f32[4,144,128]{2,1,0:T(8,128)S(1)}, f32[4,144,128]{2,1,0:T(8,128)S(1)}, u32[]{:S(2)}, u32[]{:S(2)}) collective-permute-start(f32[4,144,128]{2,1,0:T(8,128)S(1)} %shard_map.128.refs_0_), channel_id=1, source_target_pairs={{0,8},{1,9},{2,10},{3,11},{4,12},{5,13},{6,14},{7,15},{8,0},{9,1},... | collective-permute-start | bytes 884744 | tf_op jit(solution)/shard_map/ppermute | solution.py:351
  (22 other events, 271.6 us)
